TPU v7x, 32 devices: a whole 2x2x4 slice. The times are simulated.
32 devices in a mesh: fsdp: 8 (over y, x, core), mode: 4 (over z).
Axes of the slice: x: 2, y: 2, z: 4, core: 2. Of those that a mesh axis runs over, the one named last changes fastest.
Arguments:
- gradient: float32 [32, 16, 2, 256, 512], P('mode', None, None, 'fsdp'), may hold values from -1000 to 1000, as said below
- start_in: float32 [512, 128], replicated, may hold values from -6 to 6
- start_out: float32 [256, 128], replicated, may hold values from -6 to 6
- start_x: float32 [32, 16], replicated, may hold values from -6 to 6
- start_y: float32 [16, 8], replicated, may hold values from -6 to 6
Outputs:
- factor_in: float32 [512, 128], P(('fsdp', 'mode'))
- factor_out: float32 [256, 128], P('fsdp')
- factor_x: float32 [32, 16], replicated
- factor_y: float32 [16, 8], replicated
- core: float32 [16, 128, 8, 2, 128], P('mode', 'fsdp')
Inputs may be any that keep to these rules, and one draw needn't show every extreme that they name: A weight gradient of one spectral layer, finite and bounded in magnitude.
All inputs are finite; a program needn't handle non-finite values.
Results may differ from a plain program's by a relative error of at most 0.0003.
Values sent between devices are 32-bit elements; how exact they have to be, the bound alone decides.
No kernel may reach another device: no remote copies, remote signals or barrier semaphores. Data moves between devices by JAX's collectives and lax.ppermute only.
A program may use at most 320 MiB of HBM per device.

v0:
```python
import jax
import jax.numpy as jnp
from jax import lax
from jax.experimental import pallas as pl
from jax.experimental.pallas import tpu as pltpu
from jax.sharding import PartitionSpec as P

SWEEPS = 2
ROWS = 8

precise = lax.Precision.HIGHEST
F32 = jnp.float32
BF16 = jnp.bfloat16


def split(a):
    high = a.astype(BF16)
    low = (a - high.astype(F32)).astype(BF16)
    return high, low


def dot_nt(a, b):
    return lax.dot_general(a, b, (((1,), (1,)), ((), ())), preferred_element_type=F32)


def dot_nn(a, b):
    return jnp.dot(a, b, preferred_element_type=F32)


def exact_nn(a, b):
    return lax.dot_general(
        a, b, (((1,), (0,)), ((), ())), precision=precise, preferred_element_type=F32
    )


def exact_nt(a, b):
    return lax.dot_general(
        a, b, (((1,), (1,)), ((), ())), precision=precise, preferred_element_type=F32
    )


def exact_tn(a, b):
    return lax.dot_general(
        a, b, (((0,), (0,)), ((), ())), precision=precise, preferred_element_type=F32
    )


def symmetric(acc, n):
    cross = acc[:, n:]
    return acc[:, :n] + cross + cross.T


def rows_gram(a):
    high, low = split(a)
    return dot_nt(high, jnp.concatenate([high, low], axis=0))


def same_row(n):
    r = lax.broadcasted_iota(jnp.int32, (n, n), 0)
    c = lax.broadcasted_iota(jnp.int32, (n, n), 1)
    return (r & (ROWS - 1)) == (c & (ROWS - 1))


def group_select(n, group, place=lambda k: k):
    r = lax.broadcasted_iota(jnp.int32, (n // group, n), 0)
    c = lax.broadcasted_iota(jnp.int32, (n // group, n), 1)
    return jnp.where(r == place(c // group), 1.0, 0.0).astype(F32)


def gram_y_kernel(g_ref, o_ref, acc_ref):
    _, ny, nc, no, ni = g_ref.shape
    n = ny * ROWS

    @pl.when(pl.program_id(0) == 0)
    def _():
        acc_ref[...] = jnp.zeros_like(acc_ref)

    acc_ref[...] += rows_gram(
        jnp.concatenate(
            [
                g_ref[0, :, c, t * ROWS : (t + 1) * ROWS, :].reshape(n, ni)
                for c in range(nc)
                for t in range(no // ROWS)
            ],
            axis=1,
        )
    )

    @pl.when(pl.program_id(0) == pl.num_programs(0) - 1)
    def _():
        full = jnp.where(same_row(n), symmetric(acc_ref[...], n), 0.0)
        select = group_select(n, ROWS)
        o_ref[...] = exact_nt(exact_nn(select, full), select)


def gram_y_part(gradient):
    nx, ny, nc, no, ni = gradient.shape
    return pl.pallas_call(
        gram_y_kernel,
        grid=(nx,),
        in_specs=[pl.BlockSpec((1, ny, nc, no, ni), lambda x: (x, 0, 0, 0, 0))],
        out_specs=pl.BlockSpec((ny, ny), lambda x: (0, 0)),
        out_shape=jax.ShapeDtypeStruct((ny, ny), F32),
        scratch_shapes=[pltpu.VMEM((ny * ROWS, 2 * ny * ROWS), F32)],
        name="gram_y",
    )(gradient)


def gram_x_part(own, base, received, place, prev):
    nx, count, no, ni = received[0].shape
    sources = len(received) + 1
    total = sources * nx
    n = total * ROWS

    def kernel(s_ref, own_ref, *refs):
        parts = (own_ref,) + refs[: sources - 1]
        prev_ref, o_ref, acc_ref = refs[sources - 1 :]

        @pl.when(pl.program_id(0) == 0)
        def _():
            acc_ref[...] = jnp.zeros_like(acc_ref)

        def rows(t):
            own_rows = [r[:, 0, t * ROWS : (t + 1) * ROWS, :] for r in parts]
            return jnp.concatenate([r.reshape(nx * ROWS, ni) for r in own_rows], axis=0)

        acc_ref[...] += rows_gram(
            jnp.concatenate([rows(t) for t in range(no // ROWS)], axis=1)
        )

        @pl.when(pl.program_id(0) == pl.num_programs(0) - 1)
        def _():
            full = jnp.where(same_row(n), symmetric(acc_ref[...], n), 0.0)
            mine = s_ref[1]
            select = group_select(n, ROWS, lambda k: ((k // nx) ^ mine) * nx + k % nx)
            o_ref[...] = prev_ref[...] + exact_nt(exact_nn(select, full), select)

    grid_spec = pltpu.PrefetchScalarGridSpec(
        num_scalar_prefetch=1,
        grid=(count,),
        in_specs=[pl.BlockSpec((nx, 1, no, ni), lambda u, s: (0, s[0] + u, 0, 0))]
        + [pl.BlockSpec((nx, 1, no, ni), lambda u, s: (0, u, 0, 0))] * (sources - 1)
        + [pl.BlockSpec((total, total), lambda u, s: (0, 0))],
        out_specs=pl.BlockSpec((total, total), lambda u, s: (0, 0)),
        scratch_shapes=[pltpu.VMEM((n, 2 * n), F32)],
    )
    scalars = jnp.stack([base, place]).astype(jnp.int32)
    return pl.pallas_call(
        kernel,
        grid_spec=grid_spec,
        out_shape=jax.ShapeDtypeStruct((total, total), F32),
        name="gram_x",
    )(scalars, own, *received, prev)


def gram_out_part(own, base, received, place, prev):
    nx, count, no, ni = received[0].shape
    sources = len(received) + 1
    n = sources * no

    def kernel(s_ref, own_ref, *refs):
        parts = (own_ref,) + refs[: sources - 1]
        prev_ref, o_ref, acc_ref = refs[sources - 1 :]

        @pl.when(pl.program_id(0) == 0)
        def _():
            acc_ref[...] = jnp.zeros_like(acc_ref)

        acc_ref[...] += rows_gram(
            jnp.concatenate(
                [jnp.concatenate([r[x, 0] for r in parts], axis=0) for x in range(nx)], axis=1
            )
        )

        @pl.when(pl.program_id(0) == pl.num_programs(0) - 1)
        def _():
            mine = s_ref[1]
            r = lax.broadcasted_iota(jnp.int32, (n, n), 0)
            c = lax.broadcasted_iota(jnp.int32, (n, n), 1)
            select = jnp.where(r == ((c // no) ^ mine) * no + c % no, 1.0, 0.0).astype(F32)
            full = symmetric(acc_ref[...], n)
            o_ref[...] = prev_ref[...] + exact_nt(exact_nn(select, full), select)

    grid_spec = pltpu.PrefetchScalarGridSpec(
        num_scalar_prefetch=1,
        grid=(count,),
        in_specs=[pl.BlockSpec((nx, 1, no, ni), lambda u, s: (0, s[0] + u, 0, 0))]
        + [pl.BlockSpec((nx, 1, no, ni), lambda u, s: (0, u, 0, 0))] * (sources - 1)
        + [pl.BlockSpec((n, n), lambda u, s: (0, 0))],
        out_specs=pl.BlockSpec((n, n), lambda u, s: (0, 0)),
        scratch_shapes=[pltpu.VMEM((n, 2 * n), F32)],
    )
    scalars = jnp.stack([base, place]).astype(jnp.int32)
    return pl.pallas_call(
        kernel,
        grid_spec=grid_spec,
        out_shape=jax.ShapeDtypeStruct((n, n), F32),
        name="gram_out",
    )(scalars, own, *received, prev)


def project(own, base, received, factor_in, factor_out):
    nx, count, no, ni = received[0].shape
    sources = len(received) + 1
    n = sources * no
    ra = factor_in.shape[1]
    rb = factor_out.shape[1]

    def kernel(s_ref, own_ref, *refs):
        parts = (own_ref,) + refs[: sources - 1]
        in_ref, out_ref, v_ref = refs[sources - 1 :]
        in_high, in_low = split(in_ref[...])
        in_both = jnp.concatenate([in_high, in_low], axis=1)
        out_high, out_low = split(out_ref[...].T)
        for x in range(nx):
            high, low = split(jnp.concatenate([r[x, 0] for r in parts], axis=0))
            u = dot_nn(high, in_both)
            u = u[:, :ra] + (u[:, ra:] + dot_nn(low, in_high))
            u_high, u_low = split(u)
            v = dot_nn(out_high, jnp.concatenate([u_high, u_low], axis=1))
            v_ref[x, 0] = v[:, :ra] + (v[:, ra:] + dot_nn(out_low, u_high))

    grid_spec = pltpu.PrefetchScalarGridSpec(
        num_scalar_prefetch=1,
        grid=(count,),
        in_specs=[pl.BlockSpec((nx, 1, no, ni), lambda u, s: (0, s[0] + u, 0, 0))]
        + [pl.BlockSpec((nx, 1, no, ni), lambda u, s: (0, u, 0, 0))] * (sources - 1)
        + [
            pl.BlockSpec((ni, ra), lambda u, s: (0, 0)),
            pl.BlockSpec((n, rb), lambda u, s: (0, 0)),
        ],
        out_specs=pl.BlockSpec((nx, 1, rb, ra), lambda u, s: (0, u, 0, 0)),
    )
    return pl.pallas_call(
        kernel,
        grid_spec=grid_spec,
        out_shape=jax.ShapeDtypeStruct((nx, count, rb, ra), F32),
        name="project",
    )(jnp.stack([base]).astype(jnp.int32), own, *received, factor_in, factor_out)


def contract_y(parts, place, factor_y, nc):
    nx, count, nb, na = parts[0].shape
    _, nq = factor_y.shape
    sources = len(parts)

    def kernel(s_ref, f_ref, *refs):
        o_ref = refs[sources]
        mine = s_ref[0]
        terms = [[[] for _ in range(nc)] for _ in range(nq)]
        for r in range(sources):
            for u in range(count):
                slot = (mine ^ r) * count + u
                y = slot // nc
                value = refs[r][0, u]
                for q in range(nq):
                    scaled = f_ref[y, q] * value
                    for c in range(nc):
                        if count % nc == 0:
                            if u % nc == c:
                                terms[q][c].append(scaled)
                        else:
                            terms[q][c].append(jnp.where(slot % nc == c, scaled, 0.0))
        for q in range(nq):
            for c in range(nc):
                total = terms[q][c][0]
                for term in terms[q][c][1:]:
                    total = total + term
                o_ref[0, :, q * nc + c, :] = total

    return pl.pallas_call(
        kernel,
        grid=(nx,),
        in_specs=[
            pl.BlockSpec(memory_space=pltpu.SMEM),
            pl.BlockSpec(memory_space=pltpu.SMEM),
        ]
        + [pl.BlockSpec((1, count, nb, na), lambda x: (x, 0, 0, 0))] * sources,
        out_specs=pl.BlockSpec((1, nb, nq * nc, na), lambda x: (x, 0, 0, 0)),
        out_shape=jax.ShapeDtypeStruct((nx, nb, nq * nc, na), F32),
        name="contract_y",
    )(jnp.stack([place]).astype(jnp.int32), factor_y, *parts)


def contract_x(parts, place, factor_x):
    nx, rows, na = parts[0].shape
    sources = len(parts)
    ranks = factor_x.shape[1]
    step = rows if rows % ROWS else ROWS

    def kernel(s_ref, f_ref, *refs):
        o_ref = refs[sources]
        mine = s_ref[0]
        for t in range(rows // step):
            here = slice(t * step, (t + 1) * step)
            totals = [None] * ranks
            for r in range(sources):
                for x in range(nx):
                    value = refs[r][x, here]
                    for p in range(ranks):
                        term = f_ref[(mine ^ r) * nx + x, p] * value
                        totals[p] = term if totals[p] is None else totals[p] + term
            for p in range(ranks):
                o_ref[p, here] = totals[p]

    return pl.pallas_call(
        kernel,
        in_specs=[
            pl.BlockSpec(memory_space=pltpu.SMEM),
            pl.BlockSpec(memory_space=pltpu.SMEM),
        ]
        + [pl.BlockSpec(memory_space=pltpu.VMEM)] * sources,
        out_specs=pl.BlockSpec(memory_space=pltpu.VMEM),
        out_shape=jax.ShapeDtypeStruct((ranks, rows, na), F32),
        name="contract_x",
    )(jnp.stack([place]).astype(jnp.int32), factor_x, *parts)


def assemble(parts, place):
    sources = len(parts)
    np_, rows, na = parts[0].shape

    def kernel(s_ref, *refs):
        for r in range(sources):
            refs[sources][:, s_ref[0] ^ r] = refs[r][...]

    return pl.pallas_call(
        kernel,
        in_specs=[pl.BlockSpec(memory_space=pltpu.SMEM)]
        + [pl.BlockSpec(memory_space=pltpu.VMEM)] * sources,
        out_specs=pl.BlockSpec(memory_space=pltpu.VMEM),
        out_shape=jax.ShapeDtypeStruct((np_, sources, rows, na), F32),
        name="assemble",
    )(jnp.stack([place]).astype(jnp.int32), *parts)


def splat(value, i, k):
    column = jnp.broadcast_to(value[:, k : k + 1], value.shape)
    return jnp.broadcast_to(column[i : i + 1, :], value.shape)


def inverse_factor(d):
    scale = [None] * ROWS
    lower = [[None] * ROWS for _ in range(ROWS)]
    for k in range(ROWS):
        y = lax.rsqrt(d[k][k])
        scale[k] = y * (1.5 - 0.5 * d[k][k] * y * y)
        for i in range(k + 1, ROWS):
            lower[i][k] = d[i][k] * scale[k]
        for j in range(k + 1, ROWS):
            for i in range(j, ROWS):
                d[i][j] = d[i][j] - lower[i][k] * lower[j][k]
    inverse = [[None] * ROWS for _ in range(ROWS)]
    for k in range(ROWS):
        inverse[k][k] = scale[k]
        for i in range(k + 1, ROWS):
            total = lower[i][k] * inverse[k][k]
            for j in range(k + 1, i):
                total = total + lower[i][j] * inverse[j][k]
            inverse[i][k] = -scale[i] * total
    return inverse


def panel(r, rolled, e):
    row = lax.broadcasted_iota(jnp.int32, r.shape, 0)
    d = [[splat(rolled, i, k) if i >= k else None for k in range(ROWS)] for i in range(ROWS)]
    inverse = inverse_factor(d)
    upper = jnp.zeros_like(r)
    out = jnp.zeros_like(e)
    for k in range(ROWS):
        column = jnp.zeros_like(r)
        for i in range(k, ROWS):
            column = jnp.where(row == i, inverse[i][k], column)
        upper = upper + column * jnp.broadcast_to(r[k : k + 1, :], r.shape)
        out = out + column * jnp.broadcast_to(e[k : k + 1, :], e.shape)
    return upper, out


def trailing(a_ref, e_ref, upper, out, turned, first, stop):
    shape = upper.shape
    upper_rows = [jnp.broadcast_to(upper[k : k + 1, :], shape) for k in range(ROWS)]
    out_rows = [jnp.broadcast_to(out[k : k + 1, :], shape) for k in range(ROWS)]
    for q in range(first, stop):
        here = slice(q * ROWS, (q + 1) * ROWS)
        a_part = jnp.zeros_like(upper)
        e_part = jnp.zeros_like(out)
        for k in range(ROWS):
            column = jnp.broadcast_to(turned[here, k : k + 1], shape)
            a_part = a_part + column * upper_rows[k]
            e_part = e_part + column * out_rows[k]
        a_ref[here, :] = a_ref[here, :] - a_part
        e_ref[here, :] = e_ref[here, :] - e_part


def invert_lower(a_ref, e_ref):
    n = a_ref.shape[0]
    i = lax.broadcasted_iota(jnp.int32, (n, n), 0)
    k = lax.broadcasted_iota(jnp.int32, (n, n), 1)
    e_ref[...] = jnp.where(i == k, 1.0, 0.0).astype(F32)
    groups = n // ROWS
    if n % 128:
        for p in range(groups):
            here = slice(p * ROWS, (p + 1) * ROWS)
            r = a_ref[here, :]
            rolled = r
            if p:
                rolled = jnp.concatenate([r[:, p * ROWS :], r[:, : p * ROWS]], axis=1)
            upper, out = panel(r, rolled, e_ref[here, :])
            e_ref[here, :] = out
            if p + 1 < groups:
                trailing(a_ref, e_ref, upper, out, upper.T, p + 1, groups)
        return

    def step(p, carry):
        start = pl.multiple_of(p * ROWS, ROWS)
        r = a_ref[pl.ds(start, ROWS), :]
        rolled = pltpu.roll(r, (n - start) % n, 1)
        upper, out = panel(r, rolled, e_ref[pl.ds(start, ROWS), :])
        e_ref[pl.ds(start, ROWS), :] = out
        turned = upper.T
        row = lax.broadcasted_iota(jnp.int32, turned.shape, 0)
        turned = jnp.where(row >= start + ROWS, turned, 0.0)
        trailing(a_ref, e_ref, upper, out, turned, 0, groups)
        return carry

    lax.fori_loop(0, groups, step, 0)


def sweeps(parts, start, turned=(False,) * SWEEPS):
    n, ranks = start.shape
    count = len(parts)

    def kernel(*refs):
        s_ref, o_ref, a_ref, e_ref = refs[count:]
        gram = jnp.concatenate([r[...] for r in refs[:count]], axis=0)
        subspace = s_ref[...]
        for turn in turned:
            product = exact_tn(gram, subspace) if turn else exact_nn(gram, subspace)
            a_ref[...] = exact_tn(product, product)
            invert_lower(a_ref, e_ref)
            subspace = exact_nt(product, e_ref[...])
        o_ref[...] = subspace

    return pl.pallas_call(
        kernel,
        in_specs=[pl.BlockSpec(memory_space=pltpu.VMEM)] * (count + 1),
        out_specs=pl.BlockSpec(memory_space=pltpu.VMEM),
        out_shape=jax.ShapeDtypeStruct((n, ranks), F32),
        scratch_shapes=[pltpu.VMEM((ranks, ranks), F32)] * 2,
        name="sweeps",
    )(*parts, start)


def swap(value, axis, s):
    n = lax.axis_size(axis)
    return lax.ppermute(value, axis, [(i, i ^ s) for i in range(n)])


def block(value, index, size, dim):
    return lax.dynamic_slice_in_dim(value, index * size, size, dim)


def pieces(count, shares):
    runs = []
    start = 0
    total = sum(shares)
    seen = 0
    for share in shares:
        seen += share
        stop = (count * seen) // total
        if stop > start:
            runs.append((start, stop - start))
            start = stop
    return runs


def fold(value, width):
    while 2 * value.shape[1] <= width and value.shape[0] % (2 * ROWS) == 0:
        half = value.shape[0] // 2
        value = jnp.concatenate([value[:half], value[half:]], axis=1)
    return jnp.pad(value, ((0, (-value.shape[0]) % ROWS), (0, width - value.shape[1])))


def unfold(value, rows, columns):
    width = value.shape[1]
    count = 1
    while 2 * count * columns <= width and (rows // count) % (2 * ROWS) == 0:
        count *= 2
    size = rows // count
    parts = [None] * count
    for place in range(count):
        bits = place
        index = 0
        span = count
        step = 1
        while span > 1:
            index += (bits & 1) * (count // (2 * step))
            bits >>= 1
            span //= 2
            step *= 2
        parts[index] = value[:size, place * columns : (place + 1) * columns]
    return jnp.concatenate(parts, axis=0)


def relative_rows(value, place, count):
    size = value.shape[0] // count
    return jnp.concatenate([block(value, place ^ s, size, 0) for s in range(count)], axis=0)


def shards(gradient, start_in, start_out, start_x, start_y):
    f = lax.axis_index("fsdp")
    m = lax.axis_index("mode")
    joint = lax.axis_index(("fsdp", "mode"))
    nf = lax.axis_size("fsdp")
    nm = lax.axis_size("mode")
    nx, ny, nc, no, ni = gradient.shape
    slots = ny * nc
    flat = gradient.reshape(nx, slots, no, ni)
    per_mode = slots // nm
    per_fsdp = slots // nf

    def cut(place, count, per, run, after=None):
        source = flat if after is None else lax.optimization_barrier((flat, after))[0]
        return [
            lax.dynamic_slice(source, (0, (place ^ s) * per + run[0], 0, 0), (nx, run[1], no, ni))
            for s in range(1, count)
        ]

    def exchange(axis, parts):
        return [swap(part, axis, s + 1) for s, part in enumerate(parts)]

    mode_runs = pieces(per_mode, (1, 4, 1, 1, 1))
    fsdp_runs = pieces(per_fsdp, (3, 1))

    def cut_mode(k, after=None):
        return cut(m, nm, per_mode, mode_runs[k], after)

    def cut_fsdp(k, after=None):
        return cut(f, nf, per_fsdp, fsdp_runs[k], after)

    mode_cuts = [cut_mode(0)]
    fsdp_cuts = [cut_fsdp(0, mode_cuts[0][0])]
    for k in range(1, len(fsdp_runs)):
        fsdp_cuts.append(cut_fsdp(k, fsdp_cuts[0][0]))
    for k in range(1, len(mode_runs)):
        mode_cuts.append(cut_mode(k, fsdp_cuts[-1][0]))
    mode_parts = []
    for parts in mode_cuts:
        mode_parts.append(exchange("mode", parts))
    fsdp_parts = []
    for parts in fsdp_cuts:
        fsdp_parts.append(exchange("fsdp", parts))

    source = lax.optimization_barrier((gradient, mode_cuts[1][0]))[0]
    gram_y = gram_y_part(source)
    rows = source.reshape(nx * slots * no, ni)
    gram_in = lax.dot_general(
        rows, rows, (((0,), (0,)), ((), ())), precision=lax.Precision.HIGH
    )
    gram_out = jnp.zeros((nf * no, nf * no), F32)
    for run, parts in zip(fsdp_runs, fsdp_parts):
        gram_out = gram_out_part(flat, f * per_fsdp + run[0], parts, f, gram_out)

    rows_in = ni // nf
    folded_y = fold(gram_y, ni)

    def message(s):
        return jnp.concatenate(
            [block(gram_in, f ^ s, rows_in, 0), fold(block(gram_out, f ^ s, no, 0), ni), folded_y],
            axis=0,
        )

    messages = [message(s) for s in range(nf)]
    summed = messages[0]
    for value in [swap(messages[s], "fsdp", s) for s in range(1, nf)]:
        summed = summed + value
    values = [swap(summed, "mode", s) for s in range(1, nm)]
    for value in values:
        summed = summed + value
    gram_y = unfold(summed[summed.shape[0] - folded_y.shape[0] :], ny, ny)
    summed = summed[: summed.shape[0] - folded_y.shape[0]]
    gathered = [summed] + [swap(summed, "fsdp", s) for s in range(1, nf)]
    full_in = sweeps([g[:rows_in] for g in gathered], start_in, (False, True))
    factor_y = sweeps([gram_y], start_y)
    full_out = sweeps(
        [unfold(g[rows_in:], no, nf * no) for g in gathered],
        relative_rows(start_out, f, nf),
        (True, False),
    )

    projected = jnp.concatenate(
        [
            project(flat, f * per_fsdp + run[0], parts, full_in, full_out)
            for run, parts in zip(fsdp_runs, fsdp_parts)
        ],
        axis=1,
    )
    nb = projected.shape[2] // nf
    by_b = [block(projected, f ^ s, nb, 2) for s in range(nf)]
    by_b = by_b[:1] + [swap(by_b[s], "fsdp", s) for s in range(1, nf)]
    reduced = contract_y(by_b, f, factor_y, nc)
    na = reduced.shape[3]
    reduced = reduced.reshape(nx, -1, na)
    nr = reduced.shape[1] // nm

    gram_x = jnp.zeros((nx * nm, nx * nm), F32)
    for run, parts in zip(mode_runs, mode_parts):
        gram_x = gram_x_part(flat, m * per_mode + run[0], parts, m, gram_x)
    s = 1
    while s < nm:
        gram_x = gram_x + swap(gram_x, "mode", s)
        s *= 2
    s = 1
    while s < nf:
        gram_x = gram_x + swap(gram_x, "fsdp", s)
        s *= 2
    by_x = [block(reduced, m ^ s, nr, 1) for s in range(nm)]
    by_x = by_x[:1] + [swap(by_x[s], "mode", s) for s in range(1, nm)]
    factor_x = sweeps([gram_x], start_x)
    by_p = contract_x(by_x, m, factor_x)
    np_ = by_p.shape[0] // nm
    by_p = [block(by_p, m ^ s, np_, 0) for s in range(nm)]
    by_p = by_p[:1] + [swap(by_p[s], "mode", s) for s in range(1, nm)]
    core = assemble(by_p, m).reshape(np_, nb, -1, nc, na)

    rows_in = ni // (nf * nm)
    factor_in = block(full_in, joint, rows_in, 0)
    return (factor_in, full_out[:no], factor_x, factor_y, core)


def solution(mesh):
    in_specs = (P("mode", None, None, "fsdp", None), P(), P(), P(), P())
    out_specs = (
        P(("fsdp", "mode"), None),
        P("fsdp", None),
        P(),
        P(),
        P("mode", "fsdp", None, None, None),
    )
    return jax.shard_map(shards, mesh=mesh, in_specs=in_specs, out_specs=out_specs, check_vma=False)
```

profile of v0, /device:TPU:0, one launch (start us, length us, event | category | flops | bytes accessed | tf_op | source)
XLA Modules:
  0.0 710.1 jit_solution(1225500997470354254)
XLA Ops:
  3.3 8.7 %constant_dynamic-slice_fusion.53 = (f32[8,3,32,512]{3,2,1,0:T(8,128)}, f32[8,3,32,512]{3,2,1,0:T(8,128)}, f32[8,3,32,512]{3,2,1,0:T(8,128)}, f32[8,3,32,512]{3,...) fusion(f32[8,32,32,512]{3,2,1,0:T(8,128)} %bitcast.19, ...), kind=kLoop, calls=%fused_computation.102 | loop fusion | bytes 22020124 | tf_op jit(solution)/shard_map/dynamic_slice | solution.py:525
  15.0 3.9 constant_dynamic-slice_fusion.59
  20.7 5.9 constant_dynamic-slice_fusion.18
  28.0 6.2 collective-permute-done.1.refs_1_
  35.8 82.1 %collective-permute-done.10.refs_3_ = f32[8,3,32,512]{3,2,1,0:T(8,128)S(1)} collective-permute-done((f32[8,3,32,512]{3,2,1,0:T(8,128)}, f32[8,3,32,512]{3,2,1,0:T(8,128)S(1)}, u32[]{:S(2)}, u32[]{:S(2)}) %collective-permute-start.10) | collective-permute-done | bytes 1572896 | tf_op jit(solution)/shard_map/ppermute | solution.py:456
  118.8 20.7 %convolution_bitcast_fusion = f32[512,512]{1,0:T(8,128)} fusion(f32[8,16,2,32,512]{4,3,2,1,0:T(8,128)} %g_ref), kind=kOutput, calls=%fused_computation.16 | convolution fusion | flops 12884901888 | bytes 17825792 | tf_op jit(solution)/shard_map/dot_general | solution.py:557
  139.6 11.7 %collective-permute-done.11.refs_4_ = f32[8,3,32,512]{3,2,1,0:T(8,128)} collective-permute-done((f32[8,3,32,512]{3,2,1,0:T(8,128)}, f32[8,3,32,512]{3,2,1,0:T(8,128)}, u32[]{:S(2)}, u32[]{:S(2)}) %collective-permute-start.11) | collective-permute-done | bytes 1572896 | tf_op jit(solution)/shard_map/ppermute | solution.py:456
  155.7 12.4 %collective-permute-done.9.refs_2_ = f32[8,3,32,512]{3,2,1,0:T(8,128)} collective-permute-done((f32[8,3,32,512]{3,2,1,0:T(8,128)}, f32[8,3,32,512]{3,2,1,0:T(8,128)}, u32[]{:S(2)}, u32[]{:S(2)}) %collective-permute-start.9) | collective-permute-done | bytes 1572896 | tf_op jit(solution)/shard_map/ppermute | solution.py:456
  170.7 12.0 %gram_y.1 = f32[16,16]{1,0:T(8,128)} custom-call(f32[8,16,2,32,512]{4,3,2,1,0:T(8,128)} %g_ref), custom_call_target="tpu_custom_call" | custom-call | tf_op jit(solution)/shard_map/gram_y/pallas_call | solution.py:98
  186.3 9.7 %gram_out.2.refs_7_ = f32[256,256]{1,0:T(8,128)} custom-call(s32[2]{0:T(128)} %get-tuple-element.115.s_ref, f32[8,32,32,512]{3,2,1,0:T(8,128)} %bitcast.22, f32[8,3,32,512]{3,2,1,0:T(8,128)} %copy-done.1, f32[8,3,32,512]{3,2,1,0:T(8,128)} %collective-permute-done.8.refs_1_, f32[8,3,32,512]{3,2,1,0:T(8,128)} %collective-permute-done.9.refs_2_, ...), custom_call_target="tpu_custom_call" | custom-call | tf_op jit(solution)/shard_map/gram_out/pallas_call | solution.py:194
  196.0 5.1 collective-permute-done.6.refs_6_
  201.9 6.0 gram_out.3
  225.1 6.1 collective-permute-done.18
  236.1 4.1 constant_dynamic-slice_fusion.20
  240.2 11.7 %collective-permute-done.21 = f32[88,512]{1,0:T(8,128)S(1)} collective-permute-done((f32[88,512]{1,0:T(8,128)S(1)}, f32[88,512]{1,0:T(8,128)S(1)}, u32[]{:S(2)}, u32[]{:S(2)}) %collective-permute-start.21) | collective-permute-done | bytes 180256 | tf_op jit(solution)/shard_map/ppermute | solution.py:456
  251.9 3.6 collective-permute-start.45
  255.5 4.1 collective-permute-done.23
  259.6 14.6 %collective-permute-start.30 = (f32[80,512]{1,0:T(8,128)S(1)}, f32[80,512]{1,0:T(8,128)S(1)}, u32[]{:S(2)}, u32[]{:S(2)}) collective-permute-start(f32[80,512]{1,0:T(8,128)S(1)} %slice.216), channel_id=1, source_target_pairs={{0,28},{4,24},{8,20},{12,16},{16,12},{20,8},{24,4},{28,0},{1,29},{... | collective-permute-start | bytes 491528 | tf_op jit(solution)/shard_map/ppermute | solution.py:456
  279.4 3.3 collective-permute-done.29
  292.6 4.4 collective-permute-start.37
  303.3 16.9 %collective-permute-done.37.refs_0_ = f32[8,1,32,512]{3,2,1,0:T(8,128)S(1)} collective-permute-done((f32[8,1,32,512]{3,2,1,0:T(8,128)S(1)}, f32[8,1,32,512]{3,2,1,0:T(8,128)S(1)}, u32[]{:S(2)}, u32[]{:S(2)}) %collective-permute-start.37) | collective-permute-done | bytes 524320 | tf_op jit(solution)/shard_map/ppermute | solution.py:456
  320.2 15.0 %collective-permute-done.38.refs_1_ = f32[8,1,32,512]{3,2,1,0:T(8,128)S(1)} collective-permute-done((f32[8,1,32,512]{3,2,1,0:T(8,128)S(1)}, f32[8,1,32,512]{3,2,1,0:T(8,128)S(1)}, u32[]{:S(2)}, u32[]{:S(2)}) %collective-permute-start.38) | collective-permute-done | bytes 524320 | tf_op jit(solution)/shard_map/ppermute | solution.py:456
  337.8 5.7 collective-permute-done.34.refs_0_
  347.4 21.7 %collective-permute-done.35.refs_1_ = f32[8,1,32,512]{3,2,1,0:T(8,128)S(1)} collective-permute-done((f32[8,1,32,512]{3,2,1,0:T(8,128)S(1)}, f32[8,1,32,512]{3,2,1,0:T(8,128)S(1)}, u32[]{:S(2)}, u32[]{:S(2)}) %collective-permute-start.35) | collective-permute-done | bytes 524320 | tf_op jit(solution)/shard_map/ppermute | solution.py:456
  370.5 24.0 %sweeps.5.refs_8_ = f32[256,128]{1,0:T(8,128)} custom-call(f32[32,256]{1,0:T(8,128)} %pad_maximum_fusion.8.refs_0_, f32[32,256]{1,0:T(8,128)} %pad_maximum_fusion.9.refs_1_, f32[32,256]{1,0:T(8,128)} %pad_maximum_fusion.10.refs_2_, f32[32,256]{1,0:T(8,128)} %pad_maximum_fusion.11.refs_3_, f32[32,256]{1,0:T(8,128)} %pad_maximum_fusion.12.refs_4_, ...), custom_call_target="tpu_custom_call" | custom-call | tf_op jit(solution)/shard_map/sweeps/pallas_call | solution.py:444
  402.7 27.6 %sweeps.4.refs_7_ = f32[512,128]{1,0:T(8,128)} custom-call(f32[64,512]{1,0:T(8,128)} %slice.215.refs_0_, f32[64,512]{1,0:T(8,128)} %slice.217.refs_1_, f32[64,512]{1,0:T(8,128)} %slice.218.refs_2_, f32[64,512]{1,0:T(8,128)} %slice.219.refs_3_, f32[64,512]{1,0:T(8,128)} %slice.220.refs_4_, f32[64,512]{1,0:T(8,128)} %slice.221.refs_5_, ...), custom_call_target="tpu_custom_call" | custom-call | tf_op jit(solution)/shard_map/sweeps/pallas_call | solution.py:444
  430.3 5.7 project.3
  436.1 11.3 %project.2 = f32[8,3,128,128]{3,2,1,0:T(8,128)} custom-call(s32[1]{0:T(128)} %bitcast.5.s_ref, f32[8,32,32,512]{3,2,1,0:T(8,128)} %bitcast.26, f32[8,3,32,512]{3,2,1,0:T(8,128)} %copy-done.1, f32[8,3,32,512]{3,2,1,0:T(8,128)} %collective-permute-done.8.refs_1_, f32[8,3,32,512]{3,2,1,0:T(8,128)} %collective-permute-done.9.refs_2_, ...), custom_call_target="tpu_custom_call" | custom-call | tf_op jit(solution)/shard_map/project/pallas_call | solution.py:234
  449.3 54.2 %collective-permute-done.36.refs_2_ = f32[8,1,32,512]{3,2,1,0:T(8,128)} collective-permute-done((f32[8,1,32,512]{3,2,1,0:T(8,128)}, f32[8,1,32,512]{3,2,1,0:T(8,128)}, u32[]{:S(2)}, u32[]{:S(2)}) %collective-permute-start.36) | collective-permute-done | bytes 524320 | tf_op jit(solution)/shard_map/ppermute | solution.py:456
  504.7 5.9 collective-permute-done.31.refs_0_
  512.6 6.0 collective-permute-done.56.refs_6_
  519.6 8.2 %collective-permute-done.52.refs_2_ = f32[8,4,16,128]{3,2,1,0:T(8,128)S(1)} collective-permute-done((f32[8,4,16,128]{3,2,1,0:T(8,128)}, f32[8,4,16,128]{3,2,1,0:T(8,128)S(1)}, u32[]{:S(2)}, u32[]{:S(2)}) %collective-permute-start.52) | collective-permute-done | bytes 262176 | tf_op jit(solution)/shard_map/ppermute | solution.py:456
  528.8 3.9 collective-permute-start.57
  534.1 5.9 collective-permute-done.54.refs_4_
  540.7 62.5 %collective-permute-start.32 = (f32[8,1,32,512]{3,2,1,0:T(8,128)S(1)}, f32[8,1,32,512]{3,2,1,0:T(8,128)S(1)}, u32[]{:S(2)}, u32[]{:S(2)}) collective-permute-start(f32[8,1,32,512]{3,2,1,0:T(8,128)S(1)} %get-tuple-element.31), channel_id=1, source_target_pairs={{0,2},{1,3},{2,0},{3,1},{4,6},{5,7},{6,4},{7,5},{8,10},{9,11},{10,... | collective-permute-start | bytes 1572872 | tf_op jit(solution)/shard_map/ppermute | solution.py:456
  606.1 2.7 sweeps.7.f_ref
  608.8 6.9 contract_y.1
  617.7 3.4 collective-permute-start.58
  626.0 4.2 gram_x.5.refs_3_
  630.1 7.6 %gram_x.6.refs_3_ = f32[32,32]{1,0:T(8,128)} custom-call(s32[2]{0:T(128)} %pad_add_fusion.5.s_ref, f32[8,32,32,512]{3,2,1,0:T(8,128)} %bitcast.28, f32[8,4,32,512]{3,2,1,0:T(8,128)} %collective-permute-done.40.refs_0_, f32[8,4,32,512]{3,2,1,0:T(8,128)} %collective-permute-done.41.refs_1_, f32[8,4,32,512]{3,2,1,0:T(8,128)} %collective-permute-done.42.refs_2_, ...), custom_call_target="tpu_custom_call" | custom-call | tf_op jit(solution)/shard_map/gram_x/pallas_call | solution.py:148
  637.8 4.2 gram_x.7.refs_3_
  641.9 4.2 gram_x.8.refs_3_
  646.1 3.6 collective-permute-done.32.refs_1_
  651.3 4.2 gram_x.9
  655.4 11.0 %collective-permute-start.46 = (f32[32,32]{1,0:T(8,128)}, f32[32,32]{1,0:T(8,128)S(1)}, u32[]{:S(2)}, u32[]{:S(2)}) collective-permute-start(f32[32,32]{1,0:T(8,128)} %gram_x.9), channel_id=1, source_target_pairs={{0,1},{1,0},{2,3},{3,2},{4,5},{5,4},{6,7},{7,6},{8,9},{9,8},{10,11... | collective-permute-start | bytes 12296 | tf_op jit(solution)/shard_map/ppermute | solution.py:456
  683.0 3.7 sweeps.6.f_ref
  687.5 5.3 contract_x.1
  703.0 4.2 collective-permute-done.62.refs_2_
  (259 shorter events, 132.9 us)
Async XLA Ops:
  12.0 22.2 %collective-permute-start.7 = (f32[8,3,32,512]{3,2,1,0:T(8,128)}, f32[8,3,32,512]{3,2,1,0:T(8,128)S(1)}, u32[]{:S(2)}, u32[]{:S(2)}) collective-permute-start(f32[8,3,32,512]{3,2,1,0:T(8,128)} %get-tuple-element.39), channel_id=1, source_target_pairs={{0,4},{4,0},{8,12},{12,8},{16,20},{20,16},{24,28},{28,24},{1,5},{5... | collective-permute-start | bytes 4718600 | tf_op jit(solution)/shard_map/ppermute | solution.py:456
  12.5 105.4 %collective-permute-start.10 = (f32[8,3,32,512]{3,2,1,0:T(8,128)}, f32[8,3,32,512]{3,2,1,0:T(8,128)S(1)}, u32[]{:S(2)}, u32[]{:S(2)}) collective-permute-start(f32[8,3,32,512]{3,2,1,0:T(8,128)} %get-tuple-element.36), channel_id=1, source_target_pairs={{0,16},{4,20},{8,24},{12,28},{16,0},{20,4},{24,8},{28,12},{1,17},{... | collective-permute-start | bytes 4718600 | tf_op jit(solution)/shard_map/ppermute | solution.py:456
  19.1 15.1 %collective-permute-start.1 = (f32[8,1,32,512]{3,2,1,0:T(8,128)}, f32[8,1,32,512]{3,2,1,0:T(8,128)}, u32[]{:S(2)}, u32[]{:S(2)}) collective-permute-start(f32[8,1,32,512]{3,2,1,0:T(8,128)} %get-tuple-element.45), channel_id=1, source_target_pairs={{0,8},{4,12},{8,0},{12,4},{16,24},{20,28},{24,16},{28,20},{1,9},{5... | collective-permute-start | bytes 1572872 | tf_op jit(solution)/shard_map/ppermute | solution.py:456
  20.6 130.7 %collective-permute-start.11 = (f32[8,3,32,512]{3,2,1,0:T(8,128)}, f32[8,3,32,512]{3,2,1,0:T(8,128)}, u32[]{:S(2)}, u32[]{:S(2)}) collective-permute-start(f32[8,3,32,512]{3,2,1,0:T(8,128)} %get-tuple-element.35), channel_id=1, source_target_pairs={{0,20},{4,16},{8,28},{12,24},{16,4},{20,0},{24,12},{28,8},{1,21},{... | collective-permute-start | bytes 4718600 | tf_op jit(solution)/shard_map/ppermute | solution.py:456
  26.5 126.4 %collective-permute-start.12 = (f32[8,3,32,512]{3,2,1,0:T(8,128)}, f32[8,3,32,512]{3,2,1,0:T(8,128)}, u32[]{:S(2)}, u32[]{:S(2)}) collective-permute-start(f32[8,3,32,512]{3,2,1,0:T(8,128)} %get-tuple-element.34), channel_id=1, source_target_pairs={{0,24},{4,28},{8,16},{12,20},{16,8},{20,12},{24,0},{28,4},{1,25},{... | collective-permute-start | bytes 4718600 | tf_op jit(solution)/shard_map/ppermute | solution.py:456
  34.2 120.3 %collective-permute-start.13 = (f32[8,3,32,512]{3,2,1,0:T(8,128)}, f32[8,3,32,512]{3,2,1,0:T(8,128)}, u32[]{:S(2)}, u32[]{:S(2)}) collective-permute-start(f32[8,3,32,512]{3,2,1,0:T(8,128)} %get-tuple-element.33), channel_id=1, source_target_pairs={{0,28},{4,24},{8,20},{12,16},{16,12},{20,8},{24,4},{28,0},{1,29},{... | collective-permute-start | bytes 4718600 | tf_op jit(solution)/shard_map/ppermute | solution.py:456
  34.2 120.3 %collective-permute-start.8 = (f32[8,3,32,512]{3,2,1,0:T(8,128)}, f32[8,3,32,512]{3,2,1,0:T(8,128)}, u32[]{:S(2)}, u32[]{:S(2)}) collective-permute-start(f32[8,3,32,512]{3,2,1,0:T(8,128)} %get-tuple-element.38), channel_id=1, source_target_pairs={{0,8},{4,12},{8,0},{12,4},{16,24},{20,28},{24,16},{28,20},{1,9},{5... | collective-permute-start | bytes 4718600 | tf_op jit(solution)/shard_map/ppermute | solution.py:456
  117.9 50.2 %collective-permute-start.9 = (f32[8,3,32,512]{3,2,1,0:T(8,128)}, f32[8,3,32,512]{3,2,1,0:T(8,128)}, u32[]{:S(2)}, u32[]{:S(2)}) collective-permute-start(f32[8,3,32,512]{3,2,1,0:T(8,128)} %get-tuple-element.37), channel_id=1, source_target_pairs={{0,12},{4,8},{8,4},{12,0},{16,28},{20,24},{24,20},{28,16},{1,13},{... | collective-permute-start | bytes 4718600 | tf_op jit(solution)/shard_map/ppermute | solution.py:456
  151.3 44.7 %collective-permute-start.2 = (f32[8,1,32,512]{3,2,1,0:T(8,128)}, f32[8,1,32,512]{3,2,1,0:T(8,128)S(1)}, u32[]{:S(2)}, u32[]{:S(2)}) collective-permute-start(f32[8,1,32,512]{3,2,1,0:T(8,128)} %get-tuple-element.44), channel_id=1, source_target_pairs={{0,12},{4,8},{8,4},{12,0},{16,28},{20,24},{24,20},{28,16},{1,13},{... | collective-permute-start | bytes 1572872 | tf_op jit(solution)/shard_map/ppermute | solution.py:456
  152.9 43.1 %collective-permute-start.3 = (f32[8,1,32,512]{3,2,1,0:T(8,128)}, f32[8,1,32,512]{3,2,1,0:T(8,128)S(1)}, u32[]{:S(2)}, u32[]{:S(2)}) collective-permute-start(f32[8,1,32,512]{3,2,1,0:T(8,128)} %get-tuple-element.43), channel_id=1, source_target_pairs={{0,16},{4,20},{8,24},{12,28},{16,0},{20,4},{24,8},{28,12},{1,17},{... | collective-permute-start | bytes 1572872 | tf_op jit(solution)/shard_map/ppermute | solution.py:456
  154.4 41.5 %collective-permute-start.4 = (f32[8,1,32,512]{3,2,1,0:T(8,128)}, f32[8,1,32,512]{3,2,1,0:T(8,128)S(1)}, u32[]{:S(2)}, u32[]{:S(2)}) collective-permute-start(f32[8,1,32,512]{3,2,1,0:T(8,128)} %get-tuple-element.42), channel_id=1, source_target_pairs={{0,20},{4,16},{8,28},{12,24},{16,4},{20,0},{24,12},{28,8},{1,21},{... | collective-permute-start | bytes 1572872 | tf_op jit(solution)/shard_map/ppermute | solution.py:456
  154.5 41.6 %collective-permute-start.5 = (f32[8,1,32,512]{3,2,1,0:T(8,128)}, f32[8,1,32,512]{3,2,1,0:T(8,128)S(1)}, u32[]{:S(2)}, u32[]{:S(2)}) collective-permute-start(f32[8,1,32,512]{3,2,1,0:T(8,128)} %get-tuple-element.41), channel_id=1, source_target_pairs={{0,24},{4,28},{8,16},{12,20},{16,8},{20,12},{24,0},{28,4},{1,25},{... | collective-permute-start | bytes 1572872 | tf_op jit(solution)/shard_map/ppermute | solution.py:456
  168.1 33.0 %collective-permute-start.6 = (f32[8,1,32,512]{3,2,1,0:T(8,128)}, f32[8,1,32,512]{3,2,1,0:T(8,128)S(1)}, u32[]{:S(2)}, u32[]{:S(2)}) collective-permute-start(f32[8,1,32,512]{3,2,1,0:T(8,128)} %get-tuple-element.40), channel_id=1, source_target_pairs={{0,28},{4,24},{8,20},{12,16},{16,12},{20,8},{24,4},{28,0},{1,29},{... | collective-permute-start | bytes 1572872 | tf_op jit(solution)/shard_map/ppermute | solution.py:456
  213.3 9.2 %collective-permute-start.17 = (f32[88,512]{1,0:T(8,128)S(1)}, f32[88,512]{1,0:T(8,128)S(1)}, u32[]{:S(2)}, u32[]{:S(2)}) collective-permute-start(f32[88,512]{1,0:T(8,128)S(1)} %get-tuple-element.108), channel_id=1, source_target_pairs={{0,16},{4,20},{8,24},{12,28},{16,0},{20,4},{24,8},{28,12},{1,17},{... | collective-permute-start | bytes 540680 | tf_op jit(solution)/shard_map/ppermute | solution.py:456
  214.9 16.4 %collective-permute-start.18 = (f32[88,512]{1,0:T(8,128)S(1)}, f32[88,512]{1,0:T(8,128)S(1)}, u32[]{:S(2)}, u32[]{:S(2)}) collective-permute-start(f32[88,512]{1,0:T(8,128)S(1)} %get-tuple-element.109), channel_id=1, source_target_pairs={{0,20},{4,16},{8,28},{12,24},{16,4},{20,0},{24,12},{28,8},{1,21},{... | collective-permute-start | bytes 540680 | tf_op jit(solution)/shard_map/ppermute | solution.py:456
  215.2 16.0 %collective-permute-start.19 = (f32[88,512]{1,0:T(8,128)S(1)}, f32[88,512]{1,0:T(8,128)S(1)}, u32[]{:S(2)}, u32[]{:S(2)}) collective-permute-start(f32[88,512]{1,0:T(8,128)S(1)} %get-tuple-element.110), channel_id=1, source_target_pairs={{0,24},{4,28},{8,16},{12,20},{16,8},{20,12},{24,0},{28,4},{1,25},{... | collective-permute-start | bytes 540680 | tf_op jit(solution)/shard_map/ppermute | solution.py:456
  217.9 13.4 %collective-permute-start.20 = (f32[88,512]{1,0:T(8,128)S(1)}, f32[88,512]{1,0:T(8,128)S(1)}, u32[]{:S(2)}, u32[]{:S(2)}) collective-permute-start(f32[88,512]{1,0:T(8,128)S(1)} %get-tuple-element.111), channel_id=1, source_target_pairs={{0,28},{4,24},{8,20},{12,16},{16,12},{20,8},{24,4},{28,0},{1,29},{... | collective-permute-start | bytes 540680 | tf_op jit(solution)/shard_map/ppermute | solution.py:456
  221.0 71.6 %collective-permute-start.43 = (f32[8,1,32,512]{3,2,1,0:T(8,128)S(1)}, f32[8,1,32,512]{3,2,1,0:T(8,128)S(1)}, u32[]{:S(2)}, u32[]{:S(2)}) collective-permute-start(f32[8,1,32,512]{3,2,1,0:T(8,128)S(1)} %copy-done.11), channel_id=1, source_target_pairs={{0,1},{1,0},{2,3},{3,2},{4,5},{5,4},{6,7},{7,6},{8,9},{9,8},{10,11... | collective-permute-start | bytes 1572872 | tf_op jit(solution)/shard_map/ppermute | solution.py:456
  222.5 74.5 %collective-permute-start.44 = (f32[8,1,32,512]{3,2,1,0:T(8,128)S(1)}, f32[8,1,32,512]{3,2,1,0:T(8,128)S(1)}, u32[]{:S(2)}, u32[]{:S(2)}) collective-permute-start(f32[8,1,32,512]{3,2,1,0:T(8,128)S(1)} %copy-done.10), channel_id=1, source_target_pairs={{0,2},{1,3},{2,0},{3,1},{4,6},{5,7},{6,4},{7,5},{8,10},{9,11},{10,... | collective-permute-start | bytes 1572872 | tf_op jit(solution)/shard_map/ppermute | solution.py:456
  231.4 20.5 %collective-permute-start.21 = (f32[88,512]{1,0:T(8,128)S(1)}, f32[88,512]{1,0:T(8,128)S(1)}, u32[]{:S(2)}, u32[]{:S(2)}) collective-permute-start(f32[88,512]{1,0:T(8,128)S(1)} %fusion.14), channel_id=1, source_target_pairs={{0,1},{1,0},{2,3},{3,2},{4,5},{5,4},{6,7},{7,6},{8,9},{9,8},{10,11... | collective-permute-start | bytes 540680 | tf_op jit(solution)/shard_map/ppermute | solution.py:456
  233.5 22.0 %collective-permute-start.22 = (f32[88,512]{1,0:T(8,128)S(1)}, f32[88,512]{1,0:T(8,128)S(1)}, u32[]{:S(2)}, u32[]{:S(2)}) collective-permute-start(f32[88,512]{1,0:T(8,128)S(1)} %fusion.14), channel_id=1, source_target_pairs={{0,2},{1,3},{2,0},{3,1},{4,6},{5,7},{6,4},{7,5},{8,10},{9,11},{10,... | collective-permute-start | bytes 540680 | tf_op jit(solution)/shard_map/ppermute | solution.py:456
  236.1 23.5 %collective-permute-start.23 = (f32[88,512]{1,0:T(8,128)S(1)}, f32[88,512]{1,0:T(8,128)S(1)}, u32[]{:S(2)}, u32[]{:S(2)}) collective-permute-start(f32[88,512]{1,0:T(8,128)S(1)} %fusion.14), channel_id=1, source_target_pairs={{0,3},{1,2},{2,1},{3,0},{4,7},{5,6},{6,5},{7,4},{8,11},{9,10},{10,... | collective-permute-start | bytes 540680 | tf_op jit(solution)/shard_map/ppermute | solution.py:456
  251.9 48.8 %collective-permute-start.45 = (f32[8,1,32,512]{3,2,1,0:T(8,128)S(1)}, f32[8,1,32,512]{3,2,1,0:T(8,128)S(1)}, u32[]{:S(2)}, u32[]{:S(2)}) collective-permute-start(f32[8,1,32,512]{3,2,1,0:T(8,128)S(1)} %copy-done.9), channel_id=1, source_target_pairs={{0,3},{1,2},{2,1},{3,0},{4,7},{5,6},{6,5},{7,4},{8,11},{9,10},{10,... | collective-permute-start | bytes 1572872 | tf_op jit(solution)/shard_map/ppermute | solution.py:456
  259.6 19.2 %collective-permute-start.30 = (f32[80,512]{1,0:T(8,128)S(1)}, f32[80,512]{1,0:T(8,128)S(1)}, u32[]{:S(2)}, u32[]{:S(2)}) collective-permute-start(f32[80,512]{1,0:T(8,128)S(1)} %slice.216), channel_id=1, source_target_pairs={{0,28},{4,24},{8,20},{12,16},{16,12},{20,8},{24,4},{28,0},{1,29},{... | collective-permute-start | bytes 491528 | tf_op jit(solution)/shard_map/ppermute | solution.py:456
  285.3 12.8 %collective-permute-start.26 = (f32[80,512]{1,0:T(8,128)S(1)}, f32[80,512]{1,0:T(8,128)S(1)}, u32[]{:S(2)}, u32[]{:S(2)}) collective-permute-start(f32[80,512]{1,0:T(8,128)S(1)} %slice.216), channel_id=1, source_target_pairs={{0,12},{4,8},{8,4},{12,0},{16,28},{20,24},{24,20},{28,16},{1,13},{... | collective-permute-start | bytes 491528 | tf_op jit(solution)/shard_map/ppermute | solution.py:456
  289.6 10.0 %collective-permute-start.25 = (f32[80,512]{1,0:T(8,128)S(1)}, f32[80,512]{1,0:T(8,128)S(1)}, u32[]{:S(2)}, u32[]{:S(2)}) collective-permute-start(f32[80,512]{1,0:T(8,128)S(1)} %slice.216), channel_id=1, source_target_pairs={{0,8},{4,12},{8,0},{12,4},{16,24},{20,28},{24,16},{28,20},{1,9},{5... | collective-permute-start | bytes 491528 | tf_op jit(solution)/shard_map/ppermute | solution.py:456
  292.6 27.6 %collective-permute-start.37 = (f32[8,1,32,512]{3,2,1,0:T(8,128)S(1)}, f32[8,1,32,512]{3,2,1,0:T(8,128)S(1)}, u32[]{:S(2)}, u32[]{:S(2)}) collective-permute-start(f32[8,1,32,512]{3,2,1,0:T(8,128)S(1)} %get-tuple-element.26), channel_id=1, source_target_pairs={{0,1},{1,0},{2,3},{3,2},{4,5},{5,4},{6,7},{7,6},{8,9},{9,8},{10,11... | collective-permute-start | bytes 1572872 | tf_op jit(solution)/shard_map/ppermute | solution.py:456
  297.0 38.2 %collective-permute-start.38 = (f32[8,1,32,512]{3,2,1,0:T(8,128)S(1)}, f32[8,1,32,512]{3,2,1,0:T(8,128)S(1)}, u32[]{:S(2)}, u32[]{:S(2)}) collective-permute-start(f32[8,1,32,512]{3,2,1,0:T(8,128)S(1)} %get-tuple-element.25), channel_id=1, source_target_pairs={{0,2},{1,3},{2,0},{3,1},{4,6},{5,7},{6,4},{7,5},{8,10},{9,11},{10,... | collective-permute-start | bytes 1572872 | tf_op jit(solution)/shard_map/ppermute | solution.py:456
  298.2 37.1 %collective-permute-start.39 = (f32[8,1,32,512]{3,2,1,0:T(8,128)S(1)}, f32[8,1,32,512]{3,2,1,0:T(8,128)S(1)}, u32[]{:S(2)}, u32[]{:S(2)}) collective-permute-start(f32[8,1,32,512]{3,2,1,0:T(8,128)S(1)} %get-tuple-element.24), channel_id=1, source_target_pairs={{0,3},{1,2},{2,1},{3,0},{4,7},{5,6},{6,5},{7,4},{8,11},{9,10},{10,... | collective-permute-start | bytes 1572872 | tf_op jit(solution)/shard_map/ppermute | solution.py:456
  299.6 43.9 %collective-permute-start.34 = (f32[8,1,32,512]{3,2,1,0:T(8,128)S(1)}, f32[8,1,32,512]{3,2,1,0:T(8,128)S(1)}, u32[]{:S(2)}, u32[]{:S(2)}) collective-permute-start(f32[8,1,32,512]{3,2,1,0:T(8,128)S(1)} %get-tuple-element.29), channel_id=1, source_target_pairs={{0,1},{1,0},{2,3},{3,2},{4,5},{5,4},{6,7},{7,6},{8,9},{9,8},{10,11... | collective-permute-start | bytes 1572872 | tf_op jit(solution)/shard_map/ppermute | solution.py:456
  300.7 68.4 %collective-permute-start.35 = (f32[8,1,32,512]{3,2,1,0:T(8,128)S(1)}, f32[8,1,32,512]{3,2,1,0:T(8,128)S(1)}, u32[]{:S(2)}, u32[]{:S(2)}) collective-permute-start(f32[8,1,32,512]{3,2,1,0:T(8,128)S(1)} %get-tuple-element.28), channel_id=1, source_target_pairs={{0,2},{1,3},{2,0},{3,1},{4,6},{5,7},{6,4},{7,5},{8,10},{9,11},{10,... | collective-permute-start | bytes 1572872 | tf_op jit(solution)/shard_map/ppermute | solution.py:456
  320.2 297.5 %collective-permute-start.40 = (f32[8,4,32,512]{3,2,1,0:T(8,128)}, f32[8,4,32,512]{3,2,1,0:T(8,128)}, u32[]{:S(2)}, u32[]{:S(2)}) collective-permute-start(f32[8,4,32,512]{3,2,1,0:T(8,128)} %get-tuple-element.23), channel_id=1, source_target_pairs={{0,1},{1,0},{2,3},{3,2},{4,5},{5,4},{6,7},{7,6},{8,9},{9,8},{10,11... | collective-permute-start | bytes 6291464 | tf_op jit(solution)/shard_map/ppermute | solution.py:456
  335.2 285.9 %collective-permute-start.41 = (f32[8,4,32,512]{3,2,1,0:T(8,128)}, f32[8,4,32,512]{3,2,1,0:T(8,128)}, u32[]{:S(2)}, u32[]{:S(2)}) collective-permute-start(f32[8,4,32,512]{3,2,1,0:T(8,128)} %get-tuple-element.22), channel_id=1, source_target_pairs={{0,2},{1,3},{2,0},{3,1},{4,6},{5,7},{6,4},{7,5},{8,10},{9,11},{10,... | collective-permute-start | bytes 6291464 | tf_op jit(solution)/shard_map/ppermute | solution.py:456
  335.3 286.9 %collective-permute-start.42 = (f32[8,4,32,512]{3,2,1,0:T(8,128)}, f32[8,4,32,512]{3,2,1,0:T(8,128)}, u32[]{:S(2)}, u32[]{:S(2)}) collective-permute-start(f32[8,4,32,512]{3,2,1,0:T(8,128)} %get-tuple-element.21), channel_id=1, source_target_pairs={{0,3},{1,2},{2,1},{3,0},{4,7},{5,6},{6,5},{7,4},{8,11},{9,10},{10,... | collective-permute-start | bytes 6291464 | tf_op jit(solution)/shard_map/ppermute | solution.py:456
  344.9 158.7 %collective-permute-start.36 = (f32[8,1,32,512]{3,2,1,0:T(8,128)}, f32[8,1,32,512]{3,2,1,0:T(8,128)}, u32[]{:S(2)}, u32[]{:S(2)}) collective-permute-start(f32[8,1,32,512]{3,2,1,0:T(8,128)} %get-tuple-element.27), channel_id=1, source_target_pairs={{0,3},{1,2},{2,1},{3,0},{4,7},{5,6},{6,5},{7,4},{8,11},{9,10},{10,... | collective-permute-start | bytes 1572872 | tf_op jit(solution)/shard_map/ppermute | solution.py:456
  369.1 141.5 %collective-permute-start.31 = (f32[8,1,32,512]{3,2,1,0:T(8,128)}, f32[8,1,32,512]{3,2,1,0:T(8,128)}, u32[]{:S(2)}, u32[]{:S(2)}) collective-permute-start(f32[8,1,32,512]{3,2,1,0:T(8,128)} %get-tuple-element.32), channel_id=1, source_target_pairs={{0,1},{1,0},{2,3},{3,2},{4,5},{5,4},{6,7},{7,6},{8,9},{9,8},{10,11... | collective-permute-start | bytes 1572872 | tf_op jit(solution)/shard_map/ppermute | solution.py:456
  518.6 9.2 %collective-permute-start.52 = (f32[8,4,16,128]{3,2,1,0:T(8,128)}, f32[8,4,16,128]{3,2,1,0:T(8,128)S(1)}, u32[]{:S(2)}, u32[]{:S(2)}) collective-permute-start(f32[8,4,16,128]{3,2,1,0:T(8,128)} %get-tuple-element.50), channel_id=1, source_target_pairs={{0,8},{4,12},{8,0},{12,4},{16,24},{20,28},{24,16},{28,20},{1,9},{5... | collective-permute-start | bytes 786440 | tf_op jit(solution)/shard_map/ppermute | solution.py:456
  519.0 9.8 %collective-permute-start.53 = (f32[8,4,16,128]{3,2,1,0:T(8,128)}, f32[8,4,16,128]{3,2,1,0:T(8,128)S(1)}, u32[]{:S(2)}, u32[]{:S(2)}) collective-permute-start(f32[8,4,16,128]{3,2,1,0:T(8,128)} %get-tuple-element.51), channel_id=1, source_target_pairs={{0,12},{4,8},{8,4},{12,0},{16,28},{20,24},{24,20},{28,16},{1,13},{... | collective-permute-start | bytes 786440 | tf_op jit(solution)/shard_map/ppermute | solution.py:456
  527.8 12.2 %collective-permute-start.54 = (f32[8,4,16,128]{3,2,1,0:T(8,128)}, f32[8,4,16,128]{3,2,1,0:T(8,128)S(1)}, u32[]{:S(2)}, u32[]{:S(2)}) collective-permute-start(f32[8,4,16,128]{3,2,1,0:T(8,128)} %get-tuple-element.52), channel_id=1, source_target_pairs={{0,16},{4,20},{8,24},{12,28},{16,0},{20,4},{24,8},{28,12},{1,17},{... | collective-permute-start | bytes 786440 | tf_op jit(solution)/shard_map/ppermute | solution.py:456
  528.8 74.4 %collective-permute-start.57 = (f32[8,4,16,128]{3,2,1,0:T(8,128)}, f32[8,4,16,128]{3,2,1,0:T(8,128)S(1)}, u32[]{:S(2)}, u32[]{:S(2)}) collective-permute-start(f32[8,4,16,128]{3,2,1,0:T(8,128)} %get-tuple-element.47), channel_id=1, source_target_pairs={{0,28},{4,24},{8,20},{12,16},{16,12},{20,8},{24,4},{28,0},{1,29},{... | collective-permute-start | bytes 786440 | tf_op jit(solution)/shard_map/ppermute | solution.py:456
  540.7 109.0 %collective-permute-start.32 = (f32[8,1,32,512]{3,2,1,0:T(8,128)S(1)}, f32[8,1,32,512]{3,2,1,0:T(8,128)S(1)}, u32[]{:S(2)}, u32[]{:S(2)}) collective-permute-start(f32[8,1,32,512]{3,2,1,0:T(8,128)S(1)} %get-tuple-element.31), channel_id=1, source_target_pairs={{0,2},{1,3},{2,0},{3,1},{4,6},{5,7},{6,4},{7,5},{8,10},{9,11},{10,... | collective-permute-start | bytes 1572872 | tf_op jit(solution)/shard_map/ppermute | solution.py:456
  603.9 45.8 %collective-permute-start.33 = (f32[8,1,32,512]{3,2,1,0:T(8,128)S(1)}, f32[8,1,32,512]{3,2,1,0:T(8,128)S(1)}, u32[]{:S(2)}, u32[]{:S(2)}) collective-permute-start(f32[8,1,32,512]{3,2,1,0:T(8,128)S(1)} %get-tuple-element.30), channel_id=1, source_target_pairs={{0,3},{1,2},{2,1},{3,0},{4,7},{5,6},{6,5},{7,4},{8,11},{9,10},{10,... | collective-permute-start | bytes 1572872 | tf_op jit(solution)/shard_map/ppermute | solution.py:456
  617.7 69.0 %collective-permute-start.58 = (f32[8,64,128]{2,1,0:T(8,128)S(1)}, f32[8,64,128]{2,1,0:T(8,128)S(1)}, u32[]{:S(2)}, u32[]{:S(2)}) collective-permute-start(f32[8,64,128]{2,1,0:T(8,128)S(1)} %get-tuple-element.57), channel_id=1, source_target_pairs={{0,1},{1,0},{2,3},{3,2},{4,5},{5,4},{6,7},{7,6},{8,9},{9,8},{10,11... | collective-permute-start | bytes 786440 | tf_op jit(solution)/shard_map/ppermute | solution.py:456
  621.2 65.6 %collective-permute-start.59 = (f32[8,64,128]{2,1,0:T(8,128)S(1)}, f32[8,64,128]{2,1,0:T(8,128)}, u32[]{:S(2)}, u32[]{:S(2)}) collective-permute-start(f32[8,64,128]{2,1,0:T(8,128)S(1)} %get-tuple-element.56), channel_id=1, source_target_pairs={{0,2},{1,3},{2,0},{3,1},{4,6},{5,7},{6,4},{7,5},{8,10},{9,11},{10,... | collective-permute-start | bytes 786440 | tf_op jit(solution)/shard_map/ppermute | solution.py:456
  622.1 64.7 %collective-permute-start.60 = (f32[8,64,128]{2,1,0:T(8,128)S(1)}, f32[8,64,128]{2,1,0:T(8,128)}, u32[]{:S(2)}, u32[]{:S(2)}) collective-permute-start(f32[8,64,128]{2,1,0:T(8,128)S(1)} %get-tuple-element.55), channel_id=1, source_target_pairs={{0,3},{1,2},{2,1},{3,0},{4,7},{5,6},{6,5},{7,4},{8,11},{9,10},{10,... | collective-permute-start | bytes 786440 | tf_op jit(solution)/shard_map/ppermute | solution.py:456
  655.4 12.9 %collective-permute-start.46 = (f32[32,32]{1,0:T(8,128)}, f32[32,32]{1,0:T(8,128)S(1)}, u32[]{:S(2)}, u32[]{:S(2)}) collective-permute-start(f32[32,32]{1,0:T(8,128)} %gram_x.9), channel_id=1, source_target_pairs={{0,1},{1,0},{2,3},{3,2},{4,5},{5,4},{6,7},{7,6},{8,9},{9,8},{10,11... | collective-permute-start | bytes 12296 | tf_op jit(solution)/shard_map/ppermute | solution.py:456
  696.7 10.6 %collective-permute-start.62 = (f32[4,64,128]{2,1,0:T(8,128)S(1)}, f32[4,64,128]{2,1,0:T(8,128)S(1)}, u32[]{:S(2)}, u32[]{:S(2)}) collective-permute-start(f32[4,64,128]{2,1,0:T(8,128)S(1)} %get-tuple-element.68), channel_id=1, source_target_pairs={{0,2},{1,3},{2,0},{3,1},{4,6},{5,7},{6,4},{7,5},{8,10},{9,11},{10,... | collective-permute-start | bytes 393224 | tf_op jit(solution)/shard_map/ppermute | solution.py:456
  696.8 10.4 %collective-permute-start.63 = (f32[4,64,128]{2,1,0:T(8,128)S(1)}, f32[4,64,128]{2,1,0:T(8,128)S(1)}, u32[]{:S(2)}, u32[]{:S(2)}) collective-permute-start(f32[4,64,128]{2,1,0:T(8,128)S(1)} %get-tuple-element.67), channel_id=1, source_target_pairs={{0,3},{1,2},{2,1},{3,0},{4,7},{5,6},{6,5},{7,4},{8,11},{9,10},{10,... | collective-permute-start | bytes 393224 | tf_op jit(solution)/shard_map/ppermute | solution.py:456
  (61 other events, 1525.7 us)
where the time goes:
time: 715 us; the launch traced here: 710 us
  waiting for transfers between devices  305 us (43%)
  starting transfers between devices  169 us (24%)
  Pallas kernels  141 us (20%)
  local copies, waits for them, and re-layouts  57.5 us (8%)
  matrix products  20.7 us (3%)
  other arithmetic  15 us (2%)
    ppermute x64, waiting for transfers between devices, swap(): return lax.ppermute(value, axis, [(i, i ^ s) for i in range(n)])  305 us
    ppermute x64, starting transfers between devices, swap(): return lax.ppermute(value, axis, [(i, i ^ s) for i in range(n)])  169 us
    pallas_call x4, Pallas kernels, sweeps(): pl.pallas_call(kernel, in_specs=[pl.BlockSpec(memory_space=pltpu.VMEM)] *...  58.1 us
    dynamic_slice x5, local copies, waits for them, and re-layouts, cut(): lax.dynamic_slice(source, (0, (place ^ s) * per + run[0], 0, 0), (nx, run...  25.1 us
    pallas_call x5, Pallas kernels, gram_x_part(): pl.pallas_call(kernel, grid_spec=grid_spec, out_shape=jax.ShapeDtypeStruc...  24.3 us
    dot_general x1, matrix products, shards(): lax.dot_general(rows, rows, (((0,), (0,)), ((), ())), precision=lax.Preci...  20.7 us
    pallas_call x2, Pallas kernels, project(): pl.pallas_call(kernel, grid_spec=grid_spec, out_shape=jax.ShapeDtypeStruc...  17 us
    pallas_call x2, Pallas kernels, gram_out_part(): pl.pallas_call(kernel, grid_spec=grid_spec, out_shape=jax.ShapeDtypeStruc...  15.6 us
  transfers between devices with their start and end apart: 64, of which 29 were waited for; matrix products, arithmetic and copies ran while one was open for 10% of the time, Pallas kernels for 18%

commit v1 on v0

v1 whole, which is shorter than its diff:
```python
import jax
import jax.numpy as jnp
from jax import lax
from jax.experimental import pallas as pl
from jax.experimental.pallas import tpu as pltpu
from jax.sharding import PartitionSpec as P

SWEEPS = 2
ROWS = 8

precise = lax.Precision.HIGHEST
F32 = jnp.float32
BF16 = jnp.bfloat16


def split(a):
    high = a.astype(BF16)
    low = (a - high.astype(F32)).astype(BF16)
    return high, low


def dot_nt(a, b):
    return lax.dot_general(a, b, (((1,), (1,)), ((), ())), preferred_element_type=F32)


def dot_nn(a, b):
    return jnp.dot(a, b, preferred_element_type=F32)


def exact_nn(a, b):
    return lax.dot_general(
        a, b, (((1,), (0,)), ((), ())), precision=precise, preferred_element_type=F32
    )


def exact_nt(a, b):
    return lax.dot_general(
        a, b, (((1,), (1,)), ((), ())), precision=precise, preferred_element_type=F32
    )


def exact_tn(a, b):
    return lax.dot_general(
        a, b, (((0,), (0,)), ((), ())), precision=precise, preferred_element_type=F32
    )


def symmetric(acc, n):
    cross = acc[:, n:]
    return acc[:, :n] + cross + cross.T


def rows_gram(a):
    high, low = split(a)
    return dot_nt(high, jnp.concatenate([high, low], axis=0))


def same_row(n):
    r = lax.broadcasted_iota(jnp.int32, (n, n), 0)
    c = lax.broadcasted_iota(jnp.int32, (n, n), 1)
    return (r & (ROWS - 1)) == (c & (ROWS - 1))


def group_select(n, group, place=lambda k: k):
    r = lax.broadcasted_iota(jnp.int32, (n // group, n), 0)
    c = lax.broadcasted_iota(jnp.int32, (n // group, n), 1)
    return jnp.where(r == place(c // group), 1.0, 0.0).astype(F32)


def gram_y_kernel(g_ref, o_ref, acc_ref):
    _, ny, nc, no, ni = g_ref.shape
    n = ny * ROWS

    @pl.when(pl.program_id(0) == 0)
    def _():
        acc_ref[...] = jnp.zeros_like(acc_ref)

    acc_ref[...] += rows_gram(
        jnp.concatenate(
            [
                g_ref[0, :, c, t * ROWS : (t + 1) * ROWS, :].reshape(n, ni)
                for c in range(nc)
                for t in range(no // ROWS)
            ],
            axis=1,
        )
    )

    @pl.when(pl.program_id(0) == pl.num_programs(0) - 1)
    def _():
        full = jnp.where(same_row(n), symmetric(acc_ref[...], n), 0.0)
        select = group_select(n, ROWS)
        o_ref[...] = exact_nt(exact_nn(select, full), select)


def gram_y_part(gradient):
    nx, ny, nc, no, ni = gradient.shape
    return pl.pallas_call(
        gram_y_kernel,
        grid=(nx,),
        in_specs=[pl.BlockSpec((1, ny, nc, no, ni), lambda x: (x, 0, 0, 0, 0))],
        out_specs=pl.BlockSpec((ny, ny), lambda x: (0, 0)),
        out_shape=jax.ShapeDtypeStruct((ny, ny), F32),
        scratch_shapes=[pltpu.VMEM((ny * ROWS, 2 * ny * ROWS), F32)],
        name="gram_y",
    )(gradient)


def gram_parts(kernel_rows, finish, own, base, received, place, prev, n, outs):
    nx, count, no, ni = received[0].shape
    sources = len(received) + 1
    n_prev = 0 if prev is None else 1
    n_out = len(outs)

    def kernel(s_ref, own_ref, *refs):
        parts = (own_ref, *refs[: sources - 1])
        o_refs = refs[sources - 1 + n_prev : sources - 1 + n_prev + n_out]
        acc_ref = refs[sources - 1 + n_prev + n_out]

        @pl.when(pl.program_id(0) == 0)
        def _():
            if n_prev:
                acc_ref[...] = refs[sources - 1][...]
            else:
                acc_ref[...] = jnp.zeros_like(acc_ref)

        kernel_rows(parts, acc_ref)

        @pl.when(pl.program_id(0) == pl.num_programs(0) - 1)
        def _():
            if finish is None:
                o_refs[0][...] = acc_ref[...]
            else:
                finish(acc_ref, s_ref[1], o_refs)

    grid_spec = pltpu.PrefetchScalarGridSpec(
        num_scalar_prefetch=1,
        grid=(count,),
        in_specs=[pl.BlockSpec((nx, 1, no, ni), lambda u, s: (0, s[0] + u, 0, 0))]
        + [pl.BlockSpec((nx, 1, no, ni), lambda u, s: (0, u, 0, 0))] * (sources - 1)
        + [pl.BlockSpec((n, 2 * n), lambda u, s: (0, 0))] * n_prev,
        out_specs=[pl.BlockSpec(o, lambda u, s: (0, 0)) for o in outs],
        scratch_shapes=[pltpu.VMEM((n, 2 * n), F32)],
    )
    scalars = jnp.stack([base, place]).astype(jnp.int32)
    return pl.pallas_call(
        kernel, grid_spec=grid_spec, out_shape=[jax.ShapeDtypeStruct(o, F32) for o in outs]
    )(scalars, own, *received, *(() if prev is None else (prev,)))


def gram_x_part(own, base, received, place, prev, last):
    nx, _, no, ni = received[0].shape
    total = (len(received) + 1) * nx
    n = total * ROWS

    def add(parts, acc_ref):
        pair = 2 if no % (2 * ROWS) == 0 else 1

        def rows(start):
            own_rows = [r[:, 0, pl.ds(start, ROWS), :] for r in parts]
            return jnp.concatenate([r.reshape(nx * ROWS, ni) for r in own_rows], axis=0)

        def step(t, carry):
            starts = [pl.multiple_of((pair * t + j) * ROWS, ROWS) for j in range(pair)]
            acc_ref[...] += rows_gram(jnp.concatenate([rows(k) for k in starts], axis=1))
            return carry

        lax.fori_loop(0, no // (pair * ROWS), step, 0)

    def finish(acc_ref, mine, o_refs):
        full = jnp.where(same_row(n), symmetric(acc_ref[...], n), 0.0)
        select = group_select(n, ROWS, lambda k: ((k // nx) ^ mine) * nx + k % nx)
        o_refs[0][...] = exact_nt(exact_nn(select, full), select)

    outs = [(total, total)] if last else [(n, 2 * n)]
    return gram_parts(add, finish if last else None, own, base, received, place, prev, n, outs)[0]


def gram_out_part(own, base, received, place, prev, last):
    nx, _, no, _ = received[0].shape
    sources = len(received) + 1
    n = sources * no

    def add(parts, acc_ref):
        def step(k, carry):
            pair = [jnp.concatenate([r[2 * k + j, 0] for r in parts], axis=0) for j in range(2)]
            acc_ref[...] += rows_gram(jnp.concatenate(pair, axis=1))
            return carry

        lax.fori_loop(0, nx // 2, step, 0)

    def finish(acc_ref, mine, o_refs):
        r = lax.broadcasted_iota(jnp.int32, (n, n), 0)
        c = lax.broadcasted_iota(jnp.int32, (n, n), 1)
        select = jnp.where(r == ((c // no) ^ mine) * no + c % no, 1.0, 0.0).astype(F32)
        full = exact_nt(symmetric(acc_ref[...], n), select)
        for d in range(sources):
            o_refs[d][...] = full[d * no : (d + 1) * no]

    outs = [(no, n)] * sources if last else [(n, 2 * n)]
    return gram_parts(add, finish if last else None, own, base, received, place, prev, n, outs)


def project(own, base, received, first, slots, factor_in, turned_out, prev):
    nx, count, no, ni = received[0].shape
    sources = len(received) + 1
    ra = factor_in.shape[1]
    nb = turned_out.shape[0] // sources
    n_prev = 0 if prev is None else sources

    def kernel(s_ref, own_ref, *refs):
        parts = (own_ref, *refs[: sources - 1])
        in_ref, out_ref = refs[sources - 1 : sources + 1]
        v_refs = refs[sources + 1 + n_prev :]
        in_high, in_low = split(in_ref[...])
        in_both = jnp.concatenate([in_high, in_low], axis=1)
        out_high, out_low = split(out_ref[...])

        def step(x, carry):
            high, low = split(jnp.concatenate([r[x, 0] for r in parts], axis=0))
            u = dot_nn(high, in_both)
            u = u[:, :ra] + (u[:, ra:] + dot_nn(low, in_high))
            u_high, u_low = split(u)
            v = dot_nn(out_high, jnp.concatenate([u_high, u_low], axis=1))
            v = v[:, :ra] + (v[:, ra:] + dot_nn(out_low, u_high))
            for d in range(sources):
                v_refs[d][x, 0] = v[d * nb : (d + 1) * nb]
            return carry

        lax.fori_loop(0, nx, step, 0)

    grid_spec = pltpu.PrefetchScalarGridSpec(
        num_scalar_prefetch=1,
        grid=(count,),
        in_specs=[pl.BlockSpec((nx, 1, no, ni), lambda u, s: (0, s[0] + u, 0, 0))]
        + [pl.BlockSpec((nx, 1, no, ni), lambda u, s: (0, u, 0, 0))] * (sources - 1)
        + [
            pl.BlockSpec(factor_in.shape, lambda u, s: (0, 0)),
            pl.BlockSpec(turned_out.shape, lambda u, s: (0, 0)),
        ]
        + [pl.BlockSpec(memory_space=pl.ANY)] * n_prev,
        out_specs=[pl.BlockSpec((nx, 1, nb, ra), lambda u, s: (0, first + u, 0, 0))] * sources,
    )
    return pl.pallas_call(
        kernel,
        grid_spec=grid_spec,
        out_shape=[jax.ShapeDtypeStruct((nx, slots, nb, ra), F32)] * sources,
        input_output_aliases={sources + 3 + d: d for d in range(n_prev)},
        name="project",
    )(jnp.stack([base]).astype(jnp.int32), own, *received, factor_in, turned_out, *(prev or ()))


def contract_y(parts, place, factor_y, nc):
    nx, count, nb, na = parts[0].shape
    _, nq = factor_y.shape
    sources = len(parts)
    x_step = 4 if nx % 4 == 0 else nx
    q_step = 2 if nq % 2 == 0 else 1

    def kernel(s_ref, f_ref, *refs):
        o_ref = refs[sources]
        mine = s_ref[0]
        for q0 in range(0, nq, q_step):
            totals = {}
            for r in range(sources):
                for u in range(count):
                    slot = (mine ^ r) * count + u
                    scales = [f_ref[slot // nc, q0 + j] for j in range(q_step)]
                    for x in range(x_step):
                        value = refs[r][x, u]
                        for j in range(q_step):
                            term = scales[j] * value
                            for c in range(nc):
                                if count % nc == 0:
                                    if u % nc != c:
                                        continue
                                    part = term
                                else:
                                    part = jnp.where(slot % nc == c, term, 0.0)
                                key = (j, x, c)
                                totals[key] = totals[key] + part if key in totals else part
            for (j, x, c), total in totals.items():
                o_ref[x, :, (q0 + j) * nc + c, :] = total

    return pl.pallas_call(
        kernel,
        grid=(nx // x_step,),
        in_specs=[
            pl.BlockSpec(memory_space=pltpu.SMEM),
            pl.BlockSpec(memory_space=pltpu.SMEM),
        ]
        + [pl.BlockSpec((x_step, count, nb, na), lambda x: (x, 0, 0, 0))] * sources,
        out_specs=pl.BlockSpec((x_step, nb, nq * nc, na), lambda x: (x, 0, 0, 0)),
        out_shape=jax.ShapeDtypeStruct((nx, nb, nq * nc, na), F32),
        name="contract_y",
    )(jnp.stack([place]).astype(jnp.int32), factor_y, *parts)


def contract_x(parts, place, factor_x):
    nx, rows, na = parts[0].shape
    sources = len(parts)
    np_ = factor_x.shape[1] // sources

    def kernel(s_ref, f_ref, *refs):
        mine = s_ref[0]
        for d in range(sources):
            totals = [None] * np_
            for r in range(sources):
                for x in range(nx):
                    value = refs[r][x]
                    for p in range(np_):
                        scale = f_ref[(mine ^ r) * nx + x, (mine ^ d) * np_ + p]
                        term = scale * value
                        totals[p] = term if totals[p] is None else totals[p] + term
            for p in range(np_):
                refs[sources + d][p] = totals[p]

    return pl.pallas_call(
        kernel,
        in_specs=[
            pl.BlockSpec(memory_space=pltpu.SMEM),
            pl.BlockSpec(memory_space=pltpu.SMEM),
        ]
        + [pl.BlockSpec(memory_space=pltpu.VMEM)] * sources,
        out_specs=[pl.BlockSpec(memory_space=pltpu.VMEM)] * sources,
        out_shape=[jax.ShapeDtypeStruct((np_, rows, na), F32)] * sources,
        name="contract_x",
    )(jnp.stack([place]).astype(jnp.int32), factor_x, *parts)


def assemble(parts, place):
    sources = len(parts)
    np_, rows, na = parts[0].shape

    def kernel(s_ref, *refs):
        for r in range(sources):
            refs[sources][:, s_ref[0] ^ r] = refs[r][...]

    return pl.pallas_call(
        kernel,
        in_specs=[pl.BlockSpec(memory_space=pltpu.SMEM)]
        + [pl.BlockSpec(memory_space=pltpu.VMEM)] * sources,
        out_specs=pl.BlockSpec(memory_space=pltpu.VMEM),
        out_shape=jax.ShapeDtypeStruct((np_, sources, rows, na), F32),
        name="assemble",
    )(jnp.stack([place]).astype(jnp.int32), *parts)


def splat(value, i, k):
    column = jnp.broadcast_to(value[:, k : k + 1], value.shape)
    return jnp.broadcast_to(column[i : i + 1, :], value.shape)


def inverse_factor(d):
    scale = [None] * ROWS
    lower = [[None] * ROWS for _ in range(ROWS)]
    for k in range(ROWS):
        y = lax.rsqrt(d[k][k])
        scale[k] = y * (1.5 - 0.5 * d[k][k] * y * y)
        for i in range(k + 1, ROWS):
            lower[i][k] = d[i][k] * scale[k]
        for j in range(k + 1, ROWS):
            for i in range(j, ROWS):
                d[i][j] = d[i][j] - lower[i][k] * lower[j][k]
    inverse = [[None] * ROWS for _ in range(ROWS)]
    for k in range(ROWS):
        inverse[k][k] = scale[k]
        for i in range(k + 1, ROWS):
            total = lower[i][k] * inverse[k][k]
            for j in range(k + 1, i):
                total = total + lower[i][j] * inverse[j][k]
            inverse[i][k] = -scale[i] * total
    return inverse


def panel(r, rolled, e):
    row = lax.broadcasted_iota(jnp.int32, r.shape, 0)
    d = [[splat(rolled, i, k) if i >= k else None for k in range(ROWS)] for i in range(ROWS)]
    inverse = inverse_factor(d)
    upper = jnp.zeros_like(r)
    out = jnp.zeros_like(e)
    for k in range(ROWS):
        column = jnp.zeros_like(r)
        for i in range(k, ROWS):
            column = jnp.where(row == i, inverse[i][k], column)
        upper = upper + column * jnp.broadcast_to(r[k : k + 1, :], r.shape)
        out = out + column * jnp.broadcast_to(e[k : k + 1, :], e.shape)
    return upper, out


def trailing(a_ref, e_ref, upper, out, turned, first, stop):
    shape = upper.shape
    upper_rows = [jnp.broadcast_to(upper[k : k + 1, :], shape) for k in range(ROWS)]
    out_rows = [jnp.broadcast_to(out[k : k + 1, :], shape) for k in range(ROWS)]
    for q in range(first, stop):
        here = slice(q * ROWS, (q + 1) * ROWS)
        a_part = jnp.zeros_like(upper)
        e_part = jnp.zeros_like(out)
        for k in range(ROWS):
            column = jnp.broadcast_to(turned[here, k : k + 1], shape)
            a_part = a_part + column * upper_rows[k]
            e_part = e_part + column * out_rows[k]
        a_ref[here, :] = a_ref[here, :] - a_part
        e_ref[here, :] = e_ref[here, :] - e_part


def invert_lower(a_ref, e_ref):
    n = a_ref.shape[0]
    i = lax.broadcasted_iota(jnp.int32, (n, n), 0)
    k = lax.broadcasted_iota(jnp.int32, (n, n), 1)
    e_ref[...] = jnp.where(i == k, 1.0, 0.0).astype(F32)
    groups = n // ROWS
    if n % 128:
        for p in range(groups):
            here = slice(p * ROWS, (p + 1) * ROWS)
            r = a_ref[here, :]
            rolled = r
            if p:
                rolled = jnp.concatenate([r[:, p * ROWS :], r[:, : p * ROWS]], axis=1)
            upper, out = panel(r, rolled, e_ref[here, :])
            e_ref[here, :] = out
            if p + 1 < groups:
                trailing(a_ref, e_ref, upper, out, upper.T, p + 1, groups)
        return

    def step(p, carry):
        start = pl.multiple_of(p * ROWS, ROWS)
        r = a_ref[pl.ds(start, ROWS), :]
        rolled = pltpu.roll(r, (n - start) % n, 1)
        upper, out = panel(r, rolled, e_ref[pl.ds(start, ROWS), :])
        e_ref[pl.ds(start, ROWS), :] = out
        turned = upper.T
        row = lax.broadcasted_iota(jnp.int32, turned.shape, 0)
        turned = jnp.where(row >= start + ROWS, turned, 0.0)
        trailing(a_ref, e_ref, upper, out, turned, 0, groups)
        return carry

    lax.fori_loop(0, groups, step, 0)


def sweeps(parts, start, turned=(False,) * SWEEPS, place=None, cuts=1, keep=None):
    n, ranks = start.shape
    count = len(parts)
    size = ranks // cuts
    n_out = 1 if place is None else 2

    def kernel(place_ref, *refs):
        s_ref = refs[count]
        outs = refs[count + 1 : count + 1 + n_out]
        a_ref, e_ref = refs[count + 1 + n_out :]
        gram = jnp.concatenate([r[:keep] for r in refs[:count]], axis=0)
        subspace = s_ref[...]
        for turn in turned:
            product = exact_tn(gram, subspace) if turn else exact_nn(gram, subspace)
            a_ref[...] = exact_tn(product, product)
            invert_lower(a_ref, e_ref)
            subspace = exact_nt(product, e_ref[...])
        outs[0][...] = subspace
        if place is not None:
            mine = place_ref[0]
            r = lax.broadcasted_iota(jnp.int32, (ranks, ranks), 0)
            c = lax.broadcasted_iota(jnp.int32, (ranks, ranks), 1)
            select = jnp.where(c == ((r // size) ^ mine) * size + r % size, 1.0, 0.0).astype(F32)
            outs[1][...] = exact_nt(exact_nn(select, e_ref[...]), product)

    return pl.pallas_call(
        kernel,
        in_specs=[pl.BlockSpec(memory_space=pltpu.SMEM)]
        + [pl.BlockSpec(memory_space=pltpu.VMEM)] * (count + 1),
        out_specs=[pl.BlockSpec(memory_space=pltpu.VMEM)] * n_out,
        out_shape=[jax.ShapeDtypeStruct((n, ranks), F32), jax.ShapeDtypeStruct((ranks, n), F32)][
            :n_out
        ],
        scratch_shapes=[pltpu.VMEM((ranks, ranks), F32)] * 2,
        name="sweeps",
    )(jnp.stack([0 if place is None else place]).astype(jnp.int32), *parts, start)


def swap(value, axis, s):
    n = lax.axis_size(axis)
    return lax.ppermute(value, axis, [(i, i ^ s) for i in range(n)])


def total_over(value, axis):
    n = lax.axis_size(axis)
    base = 1
    while base < n:
        group = min(4, n // base)
        arrived = [swap(value, axis, base * k) for k in range(1, group)]
        for other in arrived:
            value = value + other
        base *= group
    return value


def block(value, index, size, dim):
    return lax.dynamic_slice_in_dim(value, index * size, size, dim)


def pieces(count, shares):
    runs = []
    start = 0
    total = sum(shares)
    seen = 0
    for share in shares:
        seen += share
        stop = (count * seen) // total
        if stop > start:
            runs.append((start, stop - start))
            start = stop
    return runs


def all_but(value, axis):
    return [swap(value, axis, s) for s in range(1, lax.axis_size(axis))]


def added(values):
    total = values[0]
    for value in values[1:]:
        total = total + value
    return total


def relative_rows(value, place, count):
    size = value.shape[0] // count
    return jnp.concatenate([block(value, place ^ s, size, 0) for s in range(count)], axis=0)


def shards(gradient, start_in, start_out, start_x, start_y):
    f = lax.axis_index("fsdp")
    m = lax.axis_index("mode")
    joint = lax.axis_index(("fsdp", "mode"))
    nf = lax.axis_size("fsdp")
    nm = lax.axis_size("mode")
    nx, ny, nc, no, ni = gradient.shape
    slots = ny * nc
    flat = gradient.reshape(nx, slots, no, ni)
    per_mode = slots // nm
    per_fsdp = slots // nf

    def cut(place, count, per, run, after=None):
        source = flat if after is None else lax.optimization_barrier((flat, after))[0]
        return [
            lax.dynamic_slice(source, (0, (place ^ s) * per + run[0], 0, 0), (nx, run[1], no, ni))
            for s in range(1, count)
        ]

    def exchange(axis, parts):
        return [swap(part, axis, s + 1) for s, part in enumerate(parts)]

    mode_runs = pieces(per_mode, (2, 1, 1, 1, 1, 2))
    fsdp_runs = pieces(per_fsdp, (1, 3))

    def cut_mode(k, after=None):
        return cut(m, nm, per_mode, mode_runs[k], after)

    def cut_fsdp(k, after=None):
        return cut(f, nf, per_fsdp, fsdp_runs[k], after)

    mode_cuts = [cut_mode(0)]
    fsdp_cuts = [cut_fsdp(0, mode_cuts[0][0])]
    for k in range(1, len(fsdp_runs)):
        fsdp_cuts.append(cut_fsdp(k, fsdp_cuts[0][0]))
    for k in range(1, len(mode_runs)):
        mode_cuts.append(cut_mode(k, fsdp_cuts[-1][0]))
    mode_parts = []
    for parts in mode_cuts:
        mode_parts.append(exchange("mode", parts))
    fsdp_parts = []
    for parts in fsdp_cuts:
        fsdp_parts.append(exchange("fsdp", parts))

    source = lax.optimization_barrier((gradient, fsdp_cuts[0][0]))[0]
    gram_y = gram_y_part(source)
    groups_y = range(0, ny, ROWS)
    folded_y = jnp.concatenate([gram_y[k : k + ROWS] for k in groups_y], axis=1)
    folded_y = jnp.pad(folded_y, ((0, 0), (0, ni - folded_y.shape[1])))
    rows = source.reshape(nx * slots * no, ni)
    gram_in = lax.dot_general(rows, rows, (((0,), (0,)), ((), ())), precision=lax.Precision.HIGH)

    rows_in = ni // nf
    rows_one = rows_in // nm
    messages = [
        jnp.concatenate([block(gram_in, f ^ s, rows_in, 0), folded_y], axis=0)
        for s in range(nf)
    ]
    arrived = [swap(messages[s], "fsdp", s) for s in range(1, nf)]
    sum_in = added([messages[0]] + arrived)
    messages = [
        jnp.concatenate([block(sum_in, m ^ s, rows_one, 0), sum_in[rows_in:]], axis=0)
        for s in range(nm)
    ]
    arrived = [swap(messages[s], "mode", s) for s in range(1, nm)]
    sum_in = added([messages[0]] + arrived)
    folded_y = sum_in[rows_one:]
    gram_y = jnp.concatenate(
        [folded_y[:, k // ROWS * ny : (k // ROWS + 1) * ny] for k in groups_y], axis=0
    )
    sum_in = sum_in[:rows_one]
    sum_in = jnp.concatenate([sum_in] + all_but(sum_in, "mode"), axis=0)
    gathered = [sum_in] + all_but(sum_in, "fsdp")
    (full_in,) = sweeps(gathered, start_in, (False, True))
    (factor_y,) = sweeps([gram_y], start_y)

    gram_out = [None]
    for k, (run, parts) in enumerate(zip(fsdp_runs, fsdp_parts)):
        last = k == len(fsdp_runs) - 1
        base = f * per_fsdp + run[0]
        gram_out = gram_out_part(flat, base, parts, f, gram_out[0], last)
    sum_out = added([gram_out[0]] + [swap(gram_out[s], "fsdp", s) for s in range(1, nf)])
    sum_out = added([sum_out] + all_but(sum_out, "mode"))
    gathered = [sum_out] + all_but(sum_out, "fsdp")
    full_out, turned_out = sweeps(gathered, relative_rows(start_out, f, nf), (True, False), f, nf)

    by_b = None
    for run, parts in zip(fsdp_runs, fsdp_parts):
        base = f * per_fsdp + run[0]
        by_b = project(flat, base, parts, run[0], per_fsdp, full_in, turned_out, by_b)
    by_b = [by_b[0]] + [swap(by_b[s], "fsdp", s) for s in range(1, nf)]
    reduced = contract_y(by_b, f, factor_y, nc)
    nb, na = reduced.shape[1], reduced.shape[3]
    reduced = reduced.reshape(nx, -1, na)
    nr = reduced.shape[1] // nm

    gram_x = None
    for k, (run, parts) in enumerate(zip(mode_runs, mode_parts)):
        last = k == len(mode_runs) - 1
        gram_x = gram_x_part(flat, m * per_mode + run[0], parts, m, gram_x, last)
    gram_x = total_over(gram_x, "mode")
    gram_x = total_over(gram_x, "fsdp")
    by_x = [block(reduced, m ^ s, nr, 1) for s in range(nm)]
    by_x = by_x[:1] + [swap(by_x[s], "mode", s) for s in range(1, nm)]
    (factor_x,) = sweeps([gram_x], start_x)
    by_p = contract_x(by_x, m, factor_x)
    by_p = [by_p[0]] + [swap(by_p[s], "mode", s) for s in range(1, nm)]
    core = assemble(by_p, m)
    core = core.reshape(core.shape[0], nb, -1, nc, na)

    rows_in = ni // (nf * nm)
    factor_in = block(full_in, joint, rows_in, 0)
    return (factor_in, full_out[:no], factor_x, factor_y, core)


def solution(mesh):
    in_specs = (P("mode", None, None, "fsdp", None), P(), P(), P(), P())
    out_specs = (
        P(("fsdp", "mode"), None),
        P("fsdp", None),
        P(),
        P(),
        P("mode", "fsdp", None, None, None),
    )
    return jax.shard_map(shards, mesh=mesh, in_specs=in_specs, out_specs=out_specs, check_vma=False)
```

time: 715 us -> 715 us (level)
  local copies, waits for them, and re-layouts: 57.5 us -> 42.2 us
  starting transfers between devices: 169 us -> 180 us
  other arithmetic: 15 us -> 7.41 us
    ppermute x64 -> x89, starting transfers between devices: 169 us -> 180 us  [swap(): return lax.ppermute(value, axis, [(i, i ^ s) for i in range(n)])]
    slice x20 -> x4, local copies, waits for them, and re-layouts: 10.7 us -> 0.08 us  [the longest x1 0.07 us: shards(): folded_y[:, k // ROWS * ny:(k // ROWS + 1) * ny]]
    concatenate x14 -> x5, other arithmetic: 9.77 us -> 0.8 us  [the longest x1 0.6 us: shards(): jnp.concatenate([folded_y[:, k // ROWS * ny:(k // ROWS + 1) * ny] for k i...]
    ppermute x64 -> x89, waiting for transfers between devices: 305 us -> 311 us  [swap(): return lax.ppermute(value, axis, [(i, i ^ s) for i in range(n)])]
    pallas_call x14 -> x15, Pallas kernels: 122 us -> 127 us  [the longest x4 58.3 us: sweeps(): pl.pallas_call(kernel, in_specs=[pl.BlockSpec(memory_space=pltpu.SMEM)] +...]
  transfers between devices with their start and end apart: 64 -> 89, of which waited for: 29 -> 38; matrix products, arithmetic and copies ran while one was open for 10% -> 5% of each run, Pallas kernels for 18% -> 18%
where the time goes in v1:
time: 715 us; the launch traced here: 707 us
  waiting for transfers between devices  311 us (43%)
  starting transfers between devices  180 us (25%)
  Pallas kernels  144 us (20%)
  local copies, waits for them, and re-layouts  42.2 us (6%)
  matrix products  19.8 us (3%)
  other arithmetic  7.41 us (1%)
    ppermute x89, waiting for transfers between devices, swap(): return lax.ppermute(value, axis, [(i, i ^ s) for i in range(n)])  311 us
    ppermute x89, starting transfers between devices, swap(): return lax.ppermute(value, axis, [(i, i ^ s) for i in range(n)])  180 us
    pallas_call x4, Pallas kernels, sweeps(): pl.pallas_call(kernel, in_specs=[pl.BlockSpec(memory_space=pltpu.SMEM)] +...  58.3 us
    pallas_call x8, Pallas kernels, gram_parts(): pl.pallas_call(kernel, grid_spec=grid_spec, out_shape=[jax.ShapeDtypeStru...  43 us
    dynamic_slice x5, local copies, waits for them, and re-layouts, cut(): lax.dynamic_slice(source, (0, (place ^ s) * per + run[0], 0, 0), (nx, run...  25.2 us
    pallas_call x2, Pallas kernels, project(): pl.pallas_call(kernel, grid_spec=grid_spec, out_shape=[jax.ShapeDtypeStru...  21.9 us
    dot_general x1, matrix products, shards(): lax.dot_general(rows, rows, (((0,), (0,)), ((), ())), precision=lax.Preci...  19.8 us
  transfers between devices with their start and end apart: 89, of which 38 were waited for; matrix products, arithmetic and copies ran while one was open for 5% of the time, Pallas kernels for 18%

profile of v1, /device:TPU:0, one launch (start us, length us, event | category | flops | bytes accessed | tf_op | source)
XLA Modules:
  0.0 707.1 jit_solution(1459094716397446027)
XLA Ops:
  0.8 3.6 constant_dynamic-slice_fusion.4
  4.4 3.9 constant_dynamic-slice_fusion.21
  8.3 12.0 %gram_y.1 = f32[16,16]{1,0:T(8,128)} custom-call(f32[8,16,2,32,512]{4,3,2,1,0:T(8,128)} %g_ref), custom_call_target="tpu_custom_call" | custom-call | tf_op jit(solution)/shard_map/gram_y/pallas_call | solution.py:98
  20.3 19.8 %convolution_bitcast_fusion = f32[512,512]{1,0:T(8,128)S(1)} fusion(f32[8,16,2,32,512]{4,3,2,1,0:T(8,128)} %g_ref), kind=kOutput, calls=%fused_computation | convolution fusion | flops 12884901888 | bytes 17825792 | tf_op jit(solution)/shard_map/dot_general | solution.py:580
  50.9 7.5 %collective-permute-done.4 = f32[72,512]{1,0:T(8,128)S(1)} collective-permute-done((f32[72,512]{1,0:T(8,128)S(1)}, f32[72,512]{1,0:T(8,128)S(1)}, u32[]{:S(2)}, u32[]{:S(2)}) %collective-permute-start.4) | collective-permute-done | bytes 147488 | tf_op jit(solution)/shard_map/ppermute | solution.py:481
  73.6 8.5 %constant_dynamic-slice_fusion.27 = (f32[8,3,32,512]{3,2,1,0:T(8,128)S(1)}, f32[8,3,32,512]{3,2,1,0:T(8,128)S(1)}, f32[8,3,32,512]{3,2,1,0:T(8,128)}, f32[8,3,32...) fusion(f32[8,32,32,512]{3,2,1,0:T(8,128)} %bitcast.21, ...), kind=kLoop, calls=%fused_computation.65 | loop fusion | bytes 22020124 | tf_op jit(solution)/shard_map/dynamic_slice | solution.py:545
  87.3 35.2 %collective-permute-done.19.refs_7_ = f32[64,512]{1,0:T(8,128)S(1)} collective-permute-done((f32[64,512]{1,0:T(8,128)S(1)}, f32[64,512]{1,0:T(8,128)S(1)}, u32[]{:S(2)}, u32[]{:S(2)}) %collective-permute-start.19) | collective-permute-done | bytes 131104 | tf_op jit(solution)/shard_map/ppermute | solution.py:481
  128.4 36.2 %collective-permute-done.16.refs_4_ = f32[64,512]{1,0:T(8,128)S(1)} collective-permute-done((f32[64,512]{1,0:T(8,128)S(1)}, f32[64,512]{1,0:T(8,128)S(1)}, u32[]{:S(2)}, u32[]{:S(2)}) %collective-permute-start.16) | collective-permute-done | bytes 131104 | tf_op jit(solution)/shard_map/ppermute | solution.py:481
  167.4 3.5 collective-permute-done.14.refs_2_
  172.2 9.3 %collective-permute-done.32.refs_5_ = f32[8,1,32,512]{3,2,1,0:T(8,128)S(1)} collective-permute-done((f32[8,1,32,512]{3,2,1,0:T(8,128)S(1)}, f32[8,1,32,512]{3,2,1,0:T(8,128)S(1)}, u32[]{:S(2)}, u32[]{:S(2)}) %collective-permute-start.32) | collective-permute-done | bytes 524320 | tf_op jit(solution)/shard_map/ppermute | solution.py:481
  181.5 11.2 %collective-permute-done.31.refs_4_ = f32[8,1,32,512]{3,2,1,0:T(8,128)S(1)} collective-permute-done((f32[8,1,32,512]{3,2,1,0:T(8,128)S(1)}, f32[8,1,32,512]{3,2,1,0:T(8,128)S(1)}, u32[]{:S(2)}, u32[]{:S(2)}) %collective-permute-start.31) | collective-permute-done | bytes 524320 | tf_op jit(solution)/shard_map/ppermute | solution.py:481
  193.3 10.5 %collective-permute-done.30.refs_3_ = f32[8,1,32,512]{3,2,1,0:T(8,128)S(1)} collective-permute-done((f32[8,1,32,512]{3,2,1,0:T(8,128)S(1)}, f32[8,1,32,512]{3,2,1,0:T(8,128)S(1)}, u32[]{:S(2)}, u32[]{:S(2)}) %collective-permute-start.30) | collective-permute-done | bytes 524320 | tf_op jit(solution)/shard_map/ppermute | solution.py:481
  209.9 5.6 constant_dynamic-slice_fusion.6
  215.5 25.0 %collective-permute-done.24.refs_4_ = f32[8,3,32,512]{3,2,1,0:T(8,128)} collective-permute-done((f32[8,3,32,512]{3,2,1,0:T(8,128)}, f32[8,3,32,512]{3,2,1,0:T(8,128)}, u32[]{:S(2)}, u32[]{:S(2)}) %collective-permute-start.24) | collective-permute-done | bytes 1572896 | tf_op jit(solution)/shard_map/ppermute | solution.py:481
  241.9 32.9 %collective-permute-done.23.refs_3_ = f32[8,3,32,512]{3,2,1,0:T(8,128)} collective-permute-done((f32[8,3,32,512]{3,2,1,0:T(8,128)}, f32[8,3,32,512]{3,2,1,0:T(8,128)}, u32[]{:S(2)}, u32[]{:S(2)}) %collective-permute-start.23) | collective-permute-done | bytes 1572896 | tf_op jit(solution)/shard_map/ppermute | solution.py:481
  279.7 5.6 shard_map.92.refs_7_
  285.4 10.2 %shard_map.93 = (f32[32,256]{1,0:T(8,128)}, f32[32,256]{1,0:T(8,128)}, f32[32,256]{1,0:T(8,128)}, f32[32,256]{1,0:T(8,128)}, f32[32,256]{1,0:T(8,128)}, /*index=...) custom-call(s32[2]{0:T(128)} %get-tuple-element.140.s_ref, f32[8,32,32,512]{3,2,1,0:T(8,128)} %bitcast.24, ...), custom_call_target="tpu_custom_call" | custom-call | tf_op jit(solution)/shard_map/pallas_call | solution.py:146
  297.2 4.2 collective-permute-done.64.refs_1_
  301.9 10.8 %collective-permute-done.62.refs_2_ = f32[8,1,32,512]{3,2,1,0:T(8,128)S(1)} collective-permute-done((f32[8,1,32,512]{3,2,1,0:T(8,128)}, f32[8,1,32,512]{3,2,1,0:T(8,128)S(1)}, u32[]{:S(2)}, u32[]{:S(2)}) %collective-permute-start.62) | collective-permute-done | bytes 524320 | tf_op jit(solution)/shard_map/ppermute | solution.py:481
  312.7 21.6 %collective-permute-start.60 = (f32[8,1,32,512]{3,2,1,0:T(8,128)}, f32[8,1,32,512]{3,2,1,0:T(8,128)}, u32[]{:S(2)}, u32[]{:S(2)}) collective-permute-start(f32[8,1,32,512]{3,2,1,0:T(8,128)} %get-tuple-element.86), channel_id=1, source_target_pairs={{0,1},{1,0},{2,3},{3,2},{4,5},{5,4},{6,7},{7,6},{8,9},{9,8},{10,11... | collective-permute-start | bytes 1572872 | tf_op jit(solution)/shard_map/ppermute | solution.py:481
  338.5 3.7 collective-permute-done.38
  343.3 3.9 collective-permute-done.39
  347.2 4.4 collective-permute-done.40
  356.3 11.2 %collective-permute-done.60.refs_0_ = f32[8,1,32,512]{3,2,1,0:T(8,128)} collective-permute-done((f32[8,1,32,512]{3,2,1,0:T(8,128)}, f32[8,1,32,512]{3,2,1,0:T(8,128)}, u32[]{:S(2)}, u32[]{:S(2)}) %collective-permute-start.60) | collective-permute-done | bytes 524320 | tf_op jit(solution)/shard_map/ppermute | solution.py:481
  367.5 35.8 %collective-permute-start.57 = (f32[8,1,32,512]{3,2,1,0:T(8,128)}, f32[8,1,32,512]{3,2,1,0:T(8,128)}, u32[]{:S(2)}, u32[]{:S(2)}) collective-permute-start(f32[8,1,32,512]{3,2,1,0:T(8,128)} %get-tuple-element.89), channel_id=1, source_target_pairs={{0,1},{1,0},{2,3},{3,2},{4,5},{5,4},{6,7},{7,6},{8,9},{9,8},{10,11... | collective-permute-start | bytes 1572872 | tf_op jit(solution)/shard_map/ppermute | solution.py:481
  403.3 10.7 %collective-permute-done.58.refs_1_ = f32[8,1,32,512]{3,2,1,0:T(8,128)} collective-permute-done((f32[8,1,32,512]{3,2,1,0:T(8,128)}, f32[8,1,32,512]{3,2,1,0:T(8,128)}, u32[]{:S(2)}, u32[]{:S(2)}) %collective-permute-start.58) | collective-permute-done | bytes 524320 | tf_op jit(solution)/shard_map/ppermute | solution.py:481
  415.8 33.4 %collective-permute-start.55 = (f32[8,1,32,512]{3,2,1,0:T(8,128)}, f32[8,1,32,512]{3,2,1,0:T(8,128)}, u32[]{:S(2)}, u32[]{:S(2)}) collective-permute-start(f32[8,1,32,512]{3,2,1,0:T(8,128)} %get-tuple-element.91), channel_id=1, source_target_pairs={{0,2},{1,3},{2,0},{3,1},{4,6},{5,7},{6,4},{7,5},{8,10},{9,11},{10,... | collective-permute-start | bytes 1572872 | tf_op jit(solution)/shard_map/ppermute | solution.py:481
  450.0 11.5 %collective-permute-done.41 = f32[32,256]{1,0:T(8,128)} collective-permute-done((f32[32,256]{1,0:T(8,128)S(1)}, f32[32,256]{1,0:T(8,128)}, u32[]{:S(2)}, u32[]{:S(2)}) %collective-permute-start.41) | collective-permute-done | bytes 32800 | tf_op jit(solution)/shard_map/ppermute | solution.py:481
  464.0 3.6 constant_dynamic-slice_fusion.18
  468.6 3.9 collective-permute-start.67
  472.5 10.4 %collective-permute-done.55.refs_1_ = f32[8,1,32,512]{3,2,1,0:T(8,128)} collective-permute-done((f32[8,1,32,512]{3,2,1,0:T(8,128)}, f32[8,1,32,512]{3,2,1,0:T(8,128)}, u32[]{:S(2)}, u32[]{:S(2)}) %collective-permute-start.55) | collective-permute-done | bytes 524320 | tf_op jit(solution)/shard_map/ppermute | solution.py:481
  484.4 21.0 %collective-permute-done.54.refs_0_ = f32[8,1,32,512]{3,2,1,0:T(8,128)} collective-permute-done((f32[8,1,32,512]{3,2,1,0:T(8,128)}, f32[8,1,32,512]{3,2,1,0:T(8,128)}, u32[]{:S(2)}, u32[]{:S(2)}) %collective-permute-start.54) | collective-permute-done | bytes 524320 | tf_op jit(solution)/shard_map/ppermute | solution.py:481
  523.1 27.6 %sweeps.4.refs_7_ = f32[512,128]{1,0:T(8,128)} custom-call(s32[1]{0:T(128)} %constant.45.clone.1.place_ref, f32[64,512]{1,0:T(8,128)} %copy-done.21, f32[64,512]{1,0:T(8,128)} %copy-done.37, f32[64,512]{1,0:T(8,128)} %copy-done.36, f32[64,512]{1,0:T(8,128)} %copy-done.35, f32[64,512]{1,0:T(8,128)} %copy-done.34, f32[64,512]{1,0:T(8,128)} %copy-done.33, ...), custom_call_target="tpu_custom_call" | custom-call | tf_op jit(solution)/shard_map/sweeps/pallas_call | solution.py:466
  550.7 24.2 %sweeps.5 = (f32[256,128]{1,0:T(8,128)}, f32[128,256]{1,0:T(8,128)}) custom-call(s32[1]{0:T(128)} %bitcast.4.place_ref.s_ref, f32[32,256]{1,0:T(8,128)} %copy-done.38, f32[32,256]{1,0:T(8,128)} %collective-permute-done.44.refs_1_, f32[32,256]{1,0:T(8,128)} %copy-done.50, f32[32,256]{1,0:T(8,128)} %copy-done.49, f32[32,256]{1,0:T(8,128)} %copy-done.48, ...), custom_call_target="tpu_custom_call" | custom-call | tf_op jit(solution)/shard_map/sweeps/pallas_call | solution.py:466
  574.9 7.0 project.2
  581.9 15.0 %project.3 = (f32[8,4,16,128]{3,2,1,0:T(8,128)}, f32[8,4,16,128]{3,2,1,0:T(8,128)}, f32[8,4,16,128]{3,2,1,0:T(8,128)}, f32[8,4,16,128]{3,2,1,0:T(8,128)}, f32[8,...) custom-call(s32[1]{0:T(128)} %bitcast.5.s_ref, ...), custom_call_target="tpu_custom_call", output_to_operand_aliasing={{0}: (11, {}), {1}: (12, {}), {2}: (13, {}), {3}: (14, {}),... | custom-call | tf_op jit(solution)/shard_map/project/pallas_call | solution.py:244
  601.3 16.4 %collective-permute-done.52.refs_1_ = f32[8,2,32,512]{3,2,1,0:T(8,128)} collective-permute-done((f32[8,2,32,512]{3,2,1,0:T(8,128)}, f32[8,2,32,512]{3,2,1,0:T(8,128)}, u32[]{:S(2)}, u32[]{:S(2)}) %collective-permute-start.52) | collective-permute-done | bytes 1048608 | tf_op jit(solution)/shard_map/ppermute | solution.py:481
  625.5 5.0 shard_map.94.refs_3_
  630.5 4.2 shard_map.95.refs_3_
  634.7 4.2 shard_map.96.refs_3_
  638.9 4.2 shard_map.97.refs_3_
  643.1 4.2 shard_map.98.refs_3_
  647.2 5.5 shard_map.99
  657.2 4.2 contract_y.1
  676.6 3.7 sweeps.6.f_ref
  680.4 7.7 %collective-permute-done.84.refs_2_ = f32[8,64,128]{2,1,0:T(8,128)S(1)} collective-permute-done((f32[8,64,128]{2,1,0:T(8,128)S(1)}, f32[8,64,128]{2,1,0:T(8,128)S(1)}, u32[]{:S(2)}, u32[]{:S(2)}) %collective-permute-start.84) | collective-permute-done | bytes 262176 | tf_op jit(solution)/shard_map/ppermute | solution.py:481
  688.8 3.1 contract_x.1
  701.0 3.2 collective-permute-done.87.refs_2_
  (302 shorter events, 135.4 us)
Async XLA Ops:
  63.2 108.4 %collective-permute-start.33 = (f32[8,1,32,512]{3,2,1,0:T(8,128)}, f32[8,1,32,512]{3,2,1,0:T(8,128)}, u32[]{:S(2)}, u32[]{:S(2)}) collective-permute-start(f32[8,1,32,512]{3,2,1,0:T(8,128)} %get-tuple-element.96), channel_id=1, source_target_pairs={{0,28},{4,24},{8,20},{12,16},{16,12},{20,8},{24,4},{28,0},{1,29},{... | collective-permute-start | bytes 1572872 | tf_op jit(solution)/shard_map/ppermute | solution.py:481
  82.1 125.9 %collective-permute-start.26 = (f32[8,3,32,512]{3,2,1,0:T(8,128)S(1)}, f32[8,3,32,512]{3,2,1,0:T(8,128)S(1)}, u32[]{:S(2)}, u32[]{:S(2)}) collective-permute-start(f32[8,3,32,512]{3,2,1,0:T(8,128)S(1)} %get-tuple-element.103), channel_id=1, source_target_pairs={{0,28},{4,24},{8,20},{12,16},{16,12},{20,8},{24,4},{28,0},{1,29},{... | collective-permute-start | bytes 4718600 | tf_op jit(solution)/shard_map/ppermute | solution.py:481
  82.2 40.3 %collective-permute-start.19 = (f32[64,512]{1,0:T(8,128)S(1)}, f32[64,512]{1,0:T(8,128)S(1)}, u32[]{:S(2)}, u32[]{:S(2)}) collective-permute-start(f32[64,512]{1,0:T(8,128)S(1)} %pad_maximum_fusion.8.refs_0_), channel_id=1, source_target_pairs={{0,28},{4,24},{8,20},{12,16},{16,12},{20,8},{24,4},{28,0},{1,29},{... | collective-permute-start | bytes 393224 | tf_op jit(solution)/shard_map/ppermute | solution.py:481
  84.9 40.6 %collective-permute-start.18 = (f32[64,512]{1,0:T(8,128)S(1)}, f32[64,512]{1,0:T(8,128)S(1)}, u32[]{:S(2)}, u32[]{:S(2)}) collective-permute-start(f32[64,512]{1,0:T(8,128)S(1)} %pad_maximum_fusion.8.refs_0_), channel_id=1, source_target_pairs={{0,24},{4,28},{8,16},{12,20},{16,8},{20,12},{24,0},{28,4},{1,25},{... | collective-permute-start | bytes 393224 | tf_op jit(solution)/shard_map/ppermute | solution.py:481
  87.3 40.9 %collective-permute-start.17 = (f32[64,512]{1,0:T(8,128)S(1)}, f32[64,512]{1,0:T(8,128)S(1)}, u32[]{:S(2)}, u32[]{:S(2)}) collective-permute-start(f32[64,512]{1,0:T(8,128)S(1)} %pad_maximum_fusion.8.refs_0_), channel_id=1, source_target_pairs={{0,20},{4,16},{8,28},{12,24},{16,4},{20,0},{24,12},{28,8},{1,21},{... | collective-permute-start | bytes 393224 | tf_op jit(solution)/shard_map/ppermute | solution.py:481
  122.5 42.0 %collective-permute-start.16 = (f32[64,512]{1,0:T(8,128)S(1)}, f32[64,512]{1,0:T(8,128)S(1)}, u32[]{:S(2)}, u32[]{:S(2)}) collective-permute-start(f32[64,512]{1,0:T(8,128)S(1)} %pad_maximum_fusion.8.refs_0_), channel_id=1, source_target_pairs={{0,16},{4,20},{8,24},{12,28},{16,0},{20,4},{24,8},{28,12},{1,17},{... | collective-permute-start | bytes 393224 | tf_op jit(solution)/shard_map/ppermute | solution.py:481
  125.4 83.6 %collective-permute-start.25 = (f32[8,3,32,512]{3,2,1,0:T(8,128)S(1)}, f32[8,3,32,512]{3,2,1,0:T(8,128)S(1)}, u32[]{:S(2)}, u32[]{:S(2)}) collective-permute-start(f32[8,3,32,512]{3,2,1,0:T(8,128)S(1)} %get-tuple-element.104), channel_id=1, source_target_pairs={{0,24},{4,28},{8,16},{12,20},{16,8},{20,12},{24,0},{28,4},{1,25},{... | collective-permute-start | bytes 4718600 | tf_op jit(solution)/shard_map/ppermute | solution.py:481
  128.2 37.0 %collective-permute-start.15 = (f32[64,512]{1,0:T(8,128)S(1)}, f32[64,512]{1,0:T(8,128)S(1)}, u32[]{:S(2)}, u32[]{:S(2)}) collective-permute-start(f32[64,512]{1,0:T(8,128)S(1)} %pad_maximum_fusion.8.refs_0_), channel_id=1, source_target_pairs={{0,12},{4,8},{8,4},{12,0},{16,28},{20,24},{24,20},{28,16},{1,13},{... | collective-permute-start | bytes 393224 | tf_op jit(solution)/shard_map/ppermute | solution.py:481
  171.6 32.2 %collective-permute-start.30 = (f32[8,1,32,512]{3,2,1,0:T(8,128)S(1)}, f32[8,1,32,512]{3,2,1,0:T(8,128)S(1)}, u32[]{:S(2)}, u32[]{:S(2)}) collective-permute-start(f32[8,1,32,512]{3,2,1,0:T(8,128)S(1)} %copy-done.18), channel_id=1, source_target_pairs={{0,16},{4,20},{8,24},{12,28},{16,0},{20,4},{24,8},{28,12},{1,17},{... | collective-permute-start | bytes 1572872 | tf_op jit(solution)/shard_map/ppermute | solution.py:481
  181.5 22.5 %collective-permute-start.29 = (f32[8,1,32,512]{3,2,1,0:T(8,128)S(1)}, f32[8,1,32,512]{3,2,1,0:T(8,128)S(1)}, u32[]{:S(2)}, u32[]{:S(2)}) collective-permute-start(f32[8,1,32,512]{3,2,1,0:T(8,128)S(1)} %copy-done.17), channel_id=1, source_target_pairs={{0,12},{4,8},{8,4},{12,0},{16,28},{20,24},{24,20},{28,16},{1,13},{... | collective-permute-start | bytes 1572872 | tf_op jit(solution)/shard_map/ppermute | solution.py:481
  204.0 36.5 %collective-permute-start.24 = (f32[8,3,32,512]{3,2,1,0:T(8,128)}, f32[8,3,32,512]{3,2,1,0:T(8,128)}, u32[]{:S(2)}, u32[]{:S(2)}) collective-permute-start(f32[8,3,32,512]{3,2,1,0:T(8,128)} %get-tuple-element.105), channel_id=1, source_target_pairs={{0,20},{4,16},{8,28},{12,24},{16,4},{20,0},{24,12},{28,8},{1,21},{... | collective-permute-start | bytes 4718600 | tf_op jit(solution)/shard_map/ppermute | solution.py:481
  206.5 68.2 %collective-permute-start.23 = (f32[8,3,32,512]{3,2,1,0:T(8,128)}, f32[8,3,32,512]{3,2,1,0:T(8,128)}, u32[]{:S(2)}, u32[]{:S(2)}) collective-permute-start(f32[8,3,32,512]{3,2,1,0:T(8,128)} %get-tuple-element.106), channel_id=1, source_target_pairs={{0,16},{4,20},{8,24},{12,28},{16,0},{20,4},{24,8},{28,12},{1,17},{... | collective-permute-start | bytes 4718600 | tf_op jit(solution)/shard_map/ppermute | solution.py:481
  207.9 66.9 %collective-permute-start.22 = (f32[8,3,32,512]{3,2,1,0:T(8,128)}, f32[8,3,32,512]{3,2,1,0:T(8,128)}, u32[]{:S(2)}, u32[]{:S(2)}) collective-permute-start(f32[8,3,32,512]{3,2,1,0:T(8,128)} %get-tuple-element.107), channel_id=1, source_target_pairs={{0,12},{4,8},{8,4},{12,0},{16,28},{20,24},{24,20},{28,16},{1,13},{... | collective-permute-start | bytes 4718600 | tf_op jit(solution)/shard_map/ppermute | solution.py:481
  208.0 69.7 %collective-permute-start.21 = (f32[8,3,32,512]{3,2,1,0:T(8,128)}, f32[8,3,32,512]{3,2,1,0:T(8,128)}, u32[]{:S(2)}, u32[]{:S(2)}) collective-permute-start(f32[8,3,32,512]{3,2,1,0:T(8,128)} %get-tuple-element.108), channel_id=1, source_target_pairs={{0,8},{4,12},{8,0},{12,4},{16,24},{20,28},{24,16},{28,20},{1,9},{5... | collective-permute-start | bytes 4718600 | tf_op jit(solution)/shard_map/ppermute | solution.py:481
  209.1 70.1 %collective-permute-start.20 = (f32[8,3,32,512]{3,2,1,0:T(8,128)}, f32[8,3,32,512]{3,2,1,0:T(8,128)}, u32[]{:S(2)}, u32[]{:S(2)}) collective-permute-start(f32[8,3,32,512]{3,2,1,0:T(8,128)} %get-tuple-element.109), channel_id=1, source_target_pairs={{0,4},{4,0},{8,12},{12,8},{16,20},{20,16},{24,28},{28,24},{1,5},{5... | collective-permute-start | bytes 4718600 | tf_op jit(solution)/shard_map/ppermute | solution.py:481
  240.5 55.6 %collective-permute-start.65 = (f32[8,1,32,512]{3,2,1,0:T(8,128)}, f32[8,1,32,512]{3,2,1,0:T(8,128)S(1)}, u32[]{:S(2)}, u32[]{:S(2)}) collective-permute-start(f32[8,1,32,512]{3,2,1,0:T(8,128)} %get-tuple-element.81), channel_id=1, source_target_pairs={{0,3},{1,2},{2,1},{3,0},{4,7},{5,6},{6,5},{7,4},{8,11},{9,10},{10,... | collective-permute-start | bytes 1572872 | tf_op jit(solution)/shard_map/ppermute | solution.py:481
  274.7 26.7 %collective-permute-start.64 = (f32[8,1,32,512]{3,2,1,0:T(8,128)}, f32[8,1,32,512]{3,2,1,0:T(8,128)S(1)}, u32[]{:S(2)}, u32[]{:S(2)}) collective-permute-start(f32[8,1,32,512]{3,2,1,0:T(8,128)} %get-tuple-element.82), channel_id=1, source_target_pairs={{0,2},{1,3},{2,0},{3,1},{4,6},{5,7},{6,4},{7,5},{8,10},{9,11},{10,... | collective-permute-start | bytes 1572872 | tf_op jit(solution)/shard_map/ppermute | solution.py:481
  274.8 26.8 %collective-permute-start.63 = (f32[8,1,32,512]{3,2,1,0:T(8,128)}, f32[8,1,32,512]{3,2,1,0:T(8,128)S(1)}, u32[]{:S(2)}, u32[]{:S(2)}) collective-permute-start(f32[8,1,32,512]{3,2,1,0:T(8,128)} %get-tuple-element.83), channel_id=1, source_target_pairs={{0,1},{1,0},{2,3},{3,2},{4,5},{5,4},{6,7},{7,6},{8,9},{9,8},{10,11... | collective-permute-start | bytes 1572872 | tf_op jit(solution)/shard_map/ppermute | solution.py:481
  277.7 35.0 %collective-permute-start.62 = (f32[8,1,32,512]{3,2,1,0:T(8,128)}, f32[8,1,32,512]{3,2,1,0:T(8,128)S(1)}, u32[]{:S(2)}, u32[]{:S(2)}) collective-permute-start(f32[8,1,32,512]{3,2,1,0:T(8,128)} %get-tuple-element.84), channel_id=1, source_target_pairs={{0,3},{1,2},{2,1},{3,0},{4,7},{5,6},{6,5},{7,4},{8,11},{9,10},{10,... | collective-permute-start | bytes 1572872 | tf_op jit(solution)/shard_map/ppermute | solution.py:481
  295.6 38.7 %collective-permute-start.34 = (f32[32,256]{1,0:T(8,128)}, f32[32,256]{1,0:T(8,128)S(1)}, u32[]{:S(2)}, u32[]{:S(2)}) collective-permute-start(f32[32,256]{1,0:T(8,128)} %get-tuple-element.43), channel_id=1, source_target_pairs={{0,4},{4,0},{8,12},{12,8},{16,20},{20,16},{24,28},{28,24},{1,5},{5... | collective-permute-start | bytes 98312 | tf_op jit(solution)/shard_map/ppermute | solution.py:481
  296.2 39.4 %collective-permute-start.35 = (f32[32,256]{1,0:T(8,128)}, f32[32,256]{1,0:T(8,128)S(1)}, u32[]{:S(2)}, u32[]{:S(2)}) collective-permute-start(f32[32,256]{1,0:T(8,128)} %get-tuple-element.44), channel_id=1, source_target_pairs={{0,8},{4,12},{8,0},{12,4},{16,24},{20,28},{24,16},{28,20},{1,9},{5... | collective-permute-start | bytes 98312 | tf_op jit(solution)/shard_map/ppermute | solution.py:481
  301.4 36.0 %collective-permute-start.36 = (f32[32,256]{1,0:T(8,128)}, f32[32,256]{1,0:T(8,128)S(1)}, u32[]{:S(2)}, u32[]{:S(2)}) collective-permute-start(f32[32,256]{1,0:T(8,128)} %get-tuple-element.45), channel_id=1, source_target_pairs={{0,12},{4,8},{8,4},{12,0},{16,28},{20,24},{24,20},{28,16},{1,13},{... | collective-permute-start | bytes 98312 | tf_op jit(solution)/shard_map/ppermute | solution.py:481
  301.6 52.7 %collective-permute-start.61 = (f32[8,1,32,512]{3,2,1,0:T(8,128)}, f32[8,1,32,512]{3,2,1,0:T(8,128)}, u32[]{:S(2)}, u32[]{:S(2)}) collective-permute-start(f32[8,1,32,512]{3,2,1,0:T(8,128)} %get-tuple-element.85), channel_id=1, source_target_pairs={{0,2},{1,3},{2,0},{3,1},{4,6},{5,7},{6,4},{7,5},{8,10},{9,11},{10,... | collective-permute-start | bytes 1572872 | tf_op jit(solution)/shard_map/ppermute | solution.py:481
  312.7 54.8 %collective-permute-start.60 = (f32[8,1,32,512]{3,2,1,0:T(8,128)}, f32[8,1,32,512]{3,2,1,0:T(8,128)}, u32[]{:S(2)}, u32[]{:S(2)}) collective-permute-start(f32[8,1,32,512]{3,2,1,0:T(8,128)} %get-tuple-element.86), channel_id=1, source_target_pairs={{0,1},{1,0},{2,3},{3,2},{4,5},{5,4},{6,7},{7,6},{8,9},{9,8},{10,11... | collective-permute-start | bytes 1572872 | tf_op jit(solution)/shard_map/ppermute | solution.py:481
  335.6 31.9 %collective-permute-start.59 = (f32[8,1,32,512]{3,2,1,0:T(8,128)}, f32[8,1,32,512]{3,2,1,0:T(8,128)}, u32[]{:S(2)}, u32[]{:S(2)}) collective-permute-start(f32[8,1,32,512]{3,2,1,0:T(8,128)} %get-tuple-element.87), channel_id=1, source_target_pairs={{0,3},{1,2},{2,1},{3,0},{4,7},{5,6},{6,5},{7,4},{8,11},{9,10},{10,... | collective-permute-start | bytes 1572872 | tf_op jit(solution)/shard_map/ppermute | solution.py:481
  337.4 76.6 %collective-permute-start.58 = (f32[8,1,32,512]{3,2,1,0:T(8,128)}, f32[8,1,32,512]{3,2,1,0:T(8,128)}, u32[]{:S(2)}, u32[]{:S(2)}) collective-permute-start(f32[8,1,32,512]{3,2,1,0:T(8,128)} %get-tuple-element.88), channel_id=1, source_target_pairs={{0,2},{1,3},{2,0},{3,1},{4,6},{5,7},{6,4},{7,5},{8,10},{9,11},{10,... | collective-permute-start | bytes 1572872 | tf_op jit(solution)/shard_map/ppermute | solution.py:481
  351.7 155.0 %collective-permute-start.68 = (f32[8,2,32,512]{3,2,1,0:T(8,128)}, f32[8,2,32,512]{3,2,1,0:T(8,128)S(1)}, u32[]{:S(2)}, u32[]{:S(2)}) collective-permute-start(f32[8,2,32,512]{3,2,1,0:T(8,128)} %get-tuple-element.78), channel_id=1, source_target_pairs={{0,3},{1,2},{2,1},{3,0},{4,7},{5,6},{6,5},{7,4},{8,11},{9,10},{10,... | collective-permute-start | bytes 3145736 | tf_op jit(solution)/shard_map/ppermute | solution.py:481
  354.2 61.6 %collective-permute-start.43 = (f32[32,256]{1,0:T(8,128)S(1)}, f32[32,256]{1,0:T(8,128)S(1)}, u32[]{:S(2)}, u32[]{:S(2)}) collective-permute-start(f32[32,256]{1,0:T(8,128)S(1)} %add_add_fusion.1), channel_id=1, source_target_pairs={{0,3},{1,2},{2,1},{3,0},{4,7},{5,6},{6,5},{7,4},{8,11},{9,10},{10,... | collective-permute-start | bytes 98312 | tf_op jit(solution)/shard_map/ppermute | solution.py:481
  367.5 81.7 %collective-permute-start.42 = (f32[32,256]{1,0:T(8,128)S(1)}, f32[32,256]{1,0:T(8,128)S(1)}, u32[]{:S(2)}, u32[]{:S(2)}) collective-permute-start(f32[32,256]{1,0:T(8,128)S(1)} %add_add_fusion.1), channel_id=1, source_target_pairs={{0,2},{1,3},{2,0},{3,1},{4,6},{5,7},{6,4},{7,5},{8,10},{9,11},{10,... | collective-permute-start | bytes 98312 | tf_op jit(solution)/shard_map/ppermute | solution.py:481
  367.5 101.0 %collective-permute-start.57 = (f32[8,1,32,512]{3,2,1,0:T(8,128)}, f32[8,1,32,512]{3,2,1,0:T(8,128)}, u32[]{:S(2)}, u32[]{:S(2)}) collective-permute-start(f32[8,1,32,512]{3,2,1,0:T(8,128)} %get-tuple-element.89), channel_id=1, source_target_pairs={{0,1},{1,0},{2,3},{3,2},{4,5},{5,4},{6,7},{7,6},{8,9},{9,8},{10,11... | collective-permute-start | bytes 1572872 | tf_op jit(solution)/shard_map/ppermute | solution.py:481
  414.0 54.6 %collective-permute-start.56 = (f32[8,1,32,512]{3,2,1,0:T(8,128)}, f32[8,1,32,512]{3,2,1,0:T(8,128)}, u32[]{:S(2)}, u32[]{:S(2)}) collective-permute-start(f32[8,1,32,512]{3,2,1,0:T(8,128)} %get-tuple-element.90), channel_id=1, source_target_pairs={{0,3},{1,2},{2,1},{3,0},{4,7},{5,6},{6,5},{7,4},{8,11},{9,10},{10,... | collective-permute-start | bytes 1572872 | tf_op jit(solution)/shard_map/ppermute | solution.py:481
  415.8 67.1 %collective-permute-start.55 = (f32[8,1,32,512]{3,2,1,0:T(8,128)}, f32[8,1,32,512]{3,2,1,0:T(8,128)}, u32[]{:S(2)}, u32[]{:S(2)}) collective-permute-start(f32[8,1,32,512]{3,2,1,0:T(8,128)} %get-tuple-element.91), channel_id=1, source_target_pairs={{0,2},{1,3},{2,0},{3,1},{4,6},{5,7},{6,4},{7,5},{8,10},{9,11},{10,... | collective-permute-start | bytes 1572872 | tf_op jit(solution)/shard_map/ppermute | solution.py:481
  461.4 44.0 %collective-permute-start.54 = (f32[8,1,32,512]{3,2,1,0:T(8,128)}, f32[8,1,32,512]{3,2,1,0:T(8,128)}, u32[]{:S(2)}, u32[]{:S(2)}) collective-permute-start(f32[8,1,32,512]{3,2,1,0:T(8,128)} %get-tuple-element.92), channel_id=1, source_target_pairs={{0,1},{1,0},{2,3},{3,2},{4,5},{5,4},{6,7},{7,6},{8,9},{9,8},{10,11... | collective-permute-start | bytes 1572872 | tf_op jit(solution)/shard_map/ppermute | solution.py:481
  468.5 128.4 %collective-permute-start.66 = (f32[8,2,32,512]{3,2,1,0:T(8,128)}, f32[8,2,32,512]{3,2,1,0:T(8,128)S(1)}, u32[]{:S(2)}, u32[]{:S(2)}) collective-permute-start(f32[8,2,32,512]{3,2,1,0:T(8,128)} %get-tuple-element.80), channel_id=1, source_target_pairs={{0,1},{1,0},{2,3},{3,2},{4,5},{5,4},{6,7},{7,6},{8,9},{9,8},{10,11... | collective-permute-start | bytes 3145736 | tf_op jit(solution)/shard_map/ppermute | solution.py:481
  468.6 128.3 %collective-permute-start.67 = (f32[8,2,32,512]{3,2,1,0:T(8,128)}, f32[8,2,32,512]{3,2,1,0:T(8,128)S(1)}, u32[]{:S(2)}, u32[]{:S(2)}) collective-permute-start(f32[8,2,32,512]{3,2,1,0:T(8,128)} %get-tuple-element.79), channel_id=1, source_target_pairs={{0,2},{1,3},{2,0},{3,1},{4,6},{5,7},{6,4},{7,5},{8,10},{9,11},{10,... | collective-permute-start | bytes 3145736 | tf_op jit(solution)/shard_map/ppermute | solution.py:481
  482.9 23.8 %collective-permute-start.50 = (f32[32,256]{1,0:T(8,128)S(1)}, f32[32,256]{1,0:T(8,128)S(1)}, u32[]{:S(2)}, u32[]{:S(2)}) collective-permute-start(f32[32,256]{1,0:T(8,128)S(1)} %add_add_fusion.refs_0_), channel_id=1, source_target_pairs={{0,28},{4,24},{8,20},{12,16},{16,12},{20,8},{24,4},{28,0},{1,29},{... | collective-permute-start | bytes 98312 | tf_op jit(solution)/shard_map/ppermute | solution.py:481
  513.7 86.4 %collective-permute-start.53 = (f32[8,2,32,512]{3,2,1,0:T(8,128)}, f32[8,2,32,512]{3,2,1,0:T(8,128)}, u32[]{:S(2)}, u32[]{:S(2)}) collective-permute-start(f32[8,2,32,512]{3,2,1,0:T(8,128)} %get-tuple-element.93), channel_id=1, source_target_pairs={{0,3},{1,2},{2,1},{3,0},{4,7},{5,6},{6,5},{7,4},{8,11},{9,10},{10,... | collective-permute-start | bytes 3145736 | tf_op jit(solution)/shard_map/ppermute | solution.py:481
  515.7 102.0 %collective-permute-start.52 = (f32[8,2,32,512]{3,2,1,0:T(8,128)}, f32[8,2,32,512]{3,2,1,0:T(8,128)}, u32[]{:S(2)}, u32[]{:S(2)}) collective-permute-start(f32[8,2,32,512]{3,2,1,0:T(8,128)} %get-tuple-element.94), channel_id=1, source_target_pairs={{0,2},{1,3},{2,0},{3,1},{4,6},{5,7},{6,4},{7,5},{8,10},{9,11},{10,... | collective-permute-start | bytes 3145736 | tf_op jit(solution)/shard_map/ppermute | solution.py:481
  515.8 103.2 %collective-permute-start.51 = (f32[8,2,32,512]{3,2,1,0:T(8,128)}, f32[8,2,32,512]{3,2,1,0:T(8,128)}, u32[]{:S(2)}, u32[]{:S(2)}) collective-permute-start(f32[8,2,32,512]{3,2,1,0:T(8,128)} %get-tuple-element.95), channel_id=1, source_target_pairs={{0,1},{1,0},{2,3},{3,2},{4,5},{5,4},{6,7},{7,6},{8,9},{9,8},{10,11... | collective-permute-start | bytes 3145736 | tf_op jit(solution)/shard_map/ppermute | solution.py:481
  596.9 22.2 %collective-permute-start.76 = (f32[8,4,16,128]{3,2,1,0:T(8,128)}, f32[8,4,16,128]{3,2,1,0:T(8,128)S(1)}, u32[]{:S(2)}, u32[]{:S(2)}) collective-permute-start(f32[8,4,16,128]{3,2,1,0:T(8,128)} %get-tuple-element.62), channel_id=1, source_target_pairs={{0,4},{4,0},{8,12},{12,8},{16,20},{20,16},{24,28},{28,24},{1,5},{5... | collective-permute-start | bytes 786440 | tf_op jit(solution)/shard_map/ppermute | solution.py:481
  597.0 23.4 %collective-permute-start.77 = (f32[8,4,16,128]{3,2,1,0:T(8,128)}, f32[8,4,16,128]{3,2,1,0:T(8,128)S(1)}, u32[]{:S(2)}, u32[]{:S(2)}) collective-permute-start(f32[8,4,16,128]{3,2,1,0:T(8,128)} %get-tuple-element.63), channel_id=1, source_target_pairs={{0,8},{4,12},{8,0},{12,4},{16,24},{20,28},{24,16},{28,20},{1,9},{5... | collective-permute-start | bytes 786440 | tf_op jit(solution)/shard_map/ppermute | solution.py:481
  600.1 52.6 %collective-permute-start.78 = (f32[8,4,16,128]{3,2,1,0:T(8,128)}, f32[8,4,16,128]{3,2,1,0:T(8,128)S(1)}, u32[]{:S(2)}, u32[]{:S(2)}) collective-permute-start(f32[8,4,16,128]{3,2,1,0:T(8,128)} %get-tuple-element.64), channel_id=1, source_target_pairs={{0,12},{4,8},{8,4},{12,0},{16,28},{20,24},{24,20},{28,16},{1,13},{... | collective-permute-start | bytes 786440 | tf_op jit(solution)/shard_map/ppermute | solution.py:481
  617.7 36.9 %collective-permute-start.79 = (f32[8,4,16,128]{3,2,1,0:T(8,128)}, f32[8,4,16,128]{3,2,1,0:T(8,128)S(1)}, u32[]{:S(2)}, u32[]{:S(2)}) collective-permute-start(f32[8,4,16,128]{3,2,1,0:T(8,128)} %get-tuple-element.65), channel_id=1, source_target_pairs={{0,16},{4,20},{8,24},{12,28},{16,0},{20,4},{24,8},{28,12},{1,17},{... | collective-permute-start | bytes 786440 | tf_op jit(solution)/shard_map/ppermute | solution.py:481
  619.0 35.6 %collective-permute-start.80 = (f32[8,4,16,128]{3,2,1,0:T(8,128)}, f32[8,4,16,128]{3,2,1,0:T(8,128)S(1)}, u32[]{:S(2)}, u32[]{:S(2)}) collective-permute-start(f32[8,4,16,128]{3,2,1,0:T(8,128)} %get-tuple-element.66), channel_id=1, source_target_pairs={{0,20},{4,16},{8,28},{12,24},{16,4},{20,0},{24,12},{28,8},{1,21},{... | collective-permute-start | bytes 786440 | tf_op jit(solution)/shard_map/ppermute | solution.py:481
  619.1 38.1 %collective-permute-start.81 = (f32[8,4,16,128]{3,2,1,0:T(8,128)}, f32[8,4,16,128]{3,2,1,0:T(8,128)}, u32[]{:S(2)}, u32[]{:S(2)}) collective-permute-start(f32[8,4,16,128]{3,2,1,0:T(8,128)} %get-tuple-element.67), channel_id=1, source_target_pairs={{0,24},{4,28},{8,16},{12,20},{16,8},{20,12},{24,0},{28,4},{1,25},{... | collective-permute-start | bytes 786440 | tf_op jit(solution)/shard_map/ppermute | solution.py:481
  620.4 36.8 %collective-permute-start.82 = (f32[8,4,16,128]{3,2,1,0:T(8,128)}, f32[8,4,16,128]{3,2,1,0:T(8,128)}, u32[]{:S(2)}, u32[]{:S(2)}) collective-permute-start(f32[8,4,16,128]{3,2,1,0:T(8,128)} %get-tuple-element.68), channel_id=1, source_target_pairs={{0,28},{4,24},{8,20},{12,16},{16,12},{20,8},{24,4},{28,0},{1,29},{... | collective-permute-start | bytes 786440 | tf_op jit(solution)/shard_map/ppermute | solution.py:481
  665.2 22.8 %collective-permute-start.84 = (f32[8,64,128]{2,1,0:T(8,128)S(1)}, f32[8,64,128]{2,1,0:T(8,128)S(1)}, u32[]{:S(2)}, u32[]{:S(2)}) collective-permute-start(f32[8,64,128]{2,1,0:T(8,128)S(1)} %get-tuple-element.111), channel_id=1, source_target_pairs={{0,2},{1,3},{2,0},{3,1},{4,6},{5,7},{6,4},{7,5},{8,10},{9,11},{10,... | collective-permute-start | bytes 786440 | tf_op jit(solution)/shard_map/ppermute | solution.py:481
  665.5 22.5 %collective-permute-start.83 = (f32[8,64,128]{2,1,0:T(8,128)S(1)}, f32[8,64,128]{2,1,0:T(8,128)S(1)}, u32[]{:S(2)}, u32[]{:S(2)}) collective-permute-start(f32[8,64,128]{2,1,0:T(8,128)S(1)} %get-tuple-element.112), channel_id=1, source_target_pairs={{0,1},{1,0},{2,3},{3,2},{4,5},{5,4},{6,7},{7,6},{8,9},{9,8},{10,11... | collective-permute-start | bytes 786440 | tf_op jit(solution)/shard_map/ppermute | solution.py:481
  (95 other events, 2921.9 us)

commit v2 on v1

--- a/solution.py
+++ b/solution.py
@@ -13,6 +13,9 @@
 BF16 = jnp.bfloat16
 
 
+LIMITED = pltpu.CompilerParams(vmem_limit_bytes=50 * 2**20)
+
+
 def split(a):
     high = a.astype(BF16)
     low = (a - high.astype(F32)).astype(BF16)
@@ -75,16 +78,14 @@
     def _():
         acc_ref[...] = jnp.zeros_like(acc_ref)
 
-    acc_ref[...] += rows_gram(
-        jnp.concatenate(
-            [
-                g_ref[0, :, c, t * ROWS : (t + 1) * ROWS, :].reshape(n, ni)
-                for c in range(nc)
-                for t in range(no // ROWS)
-            ],
-            axis=1,
+    def step(t, carry):
+        here = pl.ds(pl.multiple_of(t * ROWS, ROWS), ROWS)
+        acc_ref[...] += rows_gram(
+            jnp.concatenate([g_ref[0, :, c, here, :].reshape(n, ni) for c in range(nc)], axis=1)
         )
-    )
+        return carry
+
+    lax.fori_loop(0, no // ROWS, step, 0)
 
     @pl.when(pl.program_id(0) == pl.num_programs(0) - 1)
     def _():
@@ -102,20 +103,32 @@
         out_specs=pl.BlockSpec((ny, ny), lambda x: (0, 0)),
         out_shape=jax.ShapeDtypeStruct((ny, ny), F32),
         scratch_shapes=[pltpu.VMEM((ny * ROWS, 2 * ny * ROWS), F32)],
+        compiler_params=LIMITED,
         name="gram_y",
     )(gradient)
 
 
-def gram_parts(kernel_rows, finish, own, base, received, place, prev, n, outs):
+def gram_parts(kernel_rows, finish, own, base, received, place, prev, n, outs, extra=(), resident=False):
     nx, count, no, ni = received[0].shape
     sources = len(received) + 1
+    if resident:
+        received = [pltpu.with_memory_space_constraint(part, pltpu.VMEM) for part in received]
+        arrived_spec = pl.BlockSpec(memory_space=pltpu.VMEM)
+    else:
+        arrived_spec = pl.BlockSpec((nx, 1, no, ni), lambda u, s: (0, u, 0, 0))
     n_prev = 0 if prev is None else 1
+    n_extra = len(extra)
+    first_out = sources - 1 + n_prev + n_extra
     n_out = len(outs)
 
     def kernel(s_ref, own_ref, *refs):
-        parts = (own_ref, *refs[: sources - 1])
-        o_refs = refs[sources - 1 + n_prev : sources - 1 + n_prev + n_out]
-        acc_ref = refs[sources - 1 + n_prev + n_out]
+        parts = refs[: sources - 1]
+        if resident:
+            parts = [part.at[:, pl.ds(pl.program_id(0), 1)] for part in parts]
+        parts = (own_ref, *parts)
+        e_refs = refs[first_out - n_extra : first_out]
+        o_refs = refs[first_out : first_out + n_out]
+        acc_ref = refs[first_out + n_out]
 
         @pl.when(pl.program_id(0) == 0)
         def _():
@@ -131,21 +144,25 @@
             if finish is None:
                 o_refs[0][...] = acc_ref[...]
             else:
-                finish(acc_ref, s_ref[1], o_refs)
+                finish(acc_ref, s_ref[1], o_refs, *e_refs)
 
     grid_spec = pltpu.PrefetchScalarGridSpec(
         num_scalar_prefetch=1,
         grid=(count,),
         in_specs=[pl.BlockSpec((nx, 1, no, ni), lambda u, s: (0, s[0] + u, 0, 0))]
-        + [pl.BlockSpec((nx, 1, no, ni), lambda u, s: (0, u, 0, 0))] * (sources - 1)
-        + [pl.BlockSpec((n, 2 * n), lambda u, s: (0, 0))] * n_prev,
+        + [arrived_spec] * (sources - 1)
+        + [pl.BlockSpec((n, 2 * n), lambda u, s: (0, 0))] * n_prev
+        + [pl.BlockSpec(e.shape, lambda u, s: (0, 0)) for e in extra],
         out_specs=[pl.BlockSpec(o, lambda u, s: (0, 0)) for o in outs],
         scratch_shapes=[pltpu.VMEM((n, 2 * n), F32)],
     )
     scalars = jnp.stack([base, place]).astype(jnp.int32)
     return pl.pallas_call(
-        kernel, grid_spec=grid_spec, out_shape=[jax.ShapeDtypeStruct(o, F32) for o in outs]
-    )(scalars, own, *received, *(() if prev is None else (prev,)))
+        kernel,
+        grid_spec=grid_spec,
+        out_shape=[jax.ShapeDtypeStruct(o, F32) for o in outs],
+        compiler_params=LIMITED,
+    )(scalars, own, *received, *(() if prev is None else (prev,)), *extra)
 
 
 def gram_x_part(own, base, received, place, prev, last):
@@ -173,10 +190,12 @@
         o_refs[0][...] = exact_nt(exact_nn(select, full), select)
 
     outs = [(total, total)] if last else [(n, 2 * n)]
-    return gram_parts(add, finish if last else None, own, base, received, place, prev, n, outs)[0]
-
-
-def gram_out_part(own, base, received, place, prev, last):
+    return gram_parts(
+        add, finish if last else None, own, base, received, place, prev, n, outs, resident=last
+    )[0]
+
+
+def gram_out_part(own, base, received, place, prev, last, extra):
     nx, _, no, _ = received[0].shape
     sources = len(received) + 1
     n = sources * no
@@ -189,16 +208,18 @@
 
         lax.fori_loop(0, nx // 2, step, 0)
 
-    def finish(acc_ref, mine, o_refs):
+    def finish(acc_ref, mine, o_refs, e_ref):
         r = lax.broadcasted_iota(jnp.int32, (n, n), 0)
         c = lax.broadcasted_iota(jnp.int32, (n, n), 1)
         select = jnp.where(r == ((c // no) ^ mine) * no + c % no, 1.0, 0.0).astype(F32)
         full = exact_nt(symmetric(acc_ref[...], n), select)
         for d in range(sources):
-            o_refs[d][...] = full[d * no : (d + 1) * no]
-
-    outs = [(no, n)] * sources if last else [(n, 2 * n)]
-    return gram_parts(add, finish if last else None, own, base, received, place, prev, n, outs)
+            o_refs[d][:no] = full[d * no : (d + 1) * no]
+            o_refs[d][no:] = e_ref[...]
+
+    outs = [(no + extra.shape[0], n)] * sources if last else [(n, 2 * n)]
+    finish, extra = (finish, (extra,)) if last else (None, ())
+    return gram_parts(add, finish, own, base, received, place, prev, n, outs, extra)
 
 
 def project(own, base, received, first, slots, factor_in, turned_out, prev):
@@ -246,6 +267,7 @@
         grid_spec=grid_spec,
         out_shape=[jax.ShapeDtypeStruct((nx, slots, nb, ra), F32)] * sources,
         input_output_aliases={sources + 3 + d: d for d in range(n_prev)},
+        compiler_params=LIMITED,
         name="project",
     )(jnp.stack([base]).astype(jnp.int32), own, *received, factor_in, turned_out, *(prev or ()))
 
@@ -292,6 +314,7 @@
         + [pl.BlockSpec((x_step, count, nb, na), lambda x: (x, 0, 0, 0))] * sources,
         out_specs=pl.BlockSpec((x_step, nb, nq * nc, na), lambda x: (x, 0, 0, 0)),
         out_shape=jax.ShapeDtypeStruct((nx, nb, nq * nc, na), F32),
+        compiler_params=LIMITED,
         name="contract_y",
     )(jnp.stack([place]).astype(jnp.int32), factor_y, *parts)
 
@@ -299,6 +322,7 @@
 def contract_x(parts, place, factor_x):
     nx, rows, na = parts[0].shape
     sources = len(parts)
+    parts = [pltpu.with_memory_space_constraint(part, pltpu.VMEM) for part in parts]
     np_ = factor_x.shape[1] // sources
 
     def kernel(s_ref, f_ref, *refs):
@@ -324,11 +348,13 @@
         + [pl.BlockSpec(memory_space=pltpu.VMEM)] * sources,
         out_specs=[pl.BlockSpec(memory_space=pltpu.VMEM)] * sources,
         out_shape=[jax.ShapeDtypeStruct((np_, rows, na), F32)] * sources,
+        compiler_params=LIMITED,
         name="contract_x",
     )(jnp.stack([place]).astype(jnp.int32), factor_x, *parts)
 
 
 def assemble(parts, place):
+    parts = [pltpu.with_memory_space_constraint(part, pltpu.VMEM) for part in parts]
     sources = len(parts)
     np_, rows, na = parts[0].shape
 
@@ -342,6 +368,7 @@
         + [pl.BlockSpec(memory_space=pltpu.VMEM)] * sources,
         out_specs=pl.BlockSpec(memory_space=pltpu.VMEM),
         out_shape=jax.ShapeDtypeStruct((np_, sources, rows, na), F32),
+        compiler_params=LIMITED,
         name="assemble",
     )(jnp.stack([place]).astype(jnp.int32), *parts)
 
@@ -472,6 +499,7 @@
             :n_out
         ],
         scratch_shapes=[pltpu.VMEM((ranks, ranks), F32)] * 2,
+        compiler_params=LIMITED,
         name="sweeps",
     )(jnp.stack([0 if place is None else place]).astype(jnp.int32), *parts, start)
 
@@ -575,41 +603,37 @@
     gram_y = gram_y_part(source)
     groups_y = range(0, ny, ROWS)
     folded_y = jnp.concatenate([gram_y[k : k + ROWS] for k in groups_y], axis=1)
-    folded_y = jnp.pad(folded_y, ((0, 0), (0, ni - folded_y.shape[1])))
+    folded_y = jnp.pad(folded_y, ((0, 0), (0, nf * no - folded_y.shape[1])))
     rows = source.reshape(nx * slots * no, ni)
     gram_in = lax.dot_general(rows, rows, (((0,), (0,)), ((), ())), precision=lax.Precision.HIGH)
 
     rows_in = ni // nf
-    rows_one = rows_in // nm
-    messages = [
-        jnp.concatenate([block(gram_in, f ^ s, rows_in, 0), folded_y], axis=0)
-        for s in range(nf)
-    ]
+    messages = [block(gram_in, f ^ s, rows_in, 0) for s in range(nf)]
     arrived = [swap(messages[s], "fsdp", s) for s in range(1, nf)]
     sum_in = added([messages[0]] + arrived)
-    messages = [
-        jnp.concatenate([block(sum_in, m ^ s, rows_one, 0), sum_in[rows_in:]], axis=0)
-        for s in range(nm)
-    ]
-    arrived = [swap(messages[s], "mode", s) for s in range(1, nm)]
-    sum_in = added([messages[0]] + arrived)
-    folded_y = sum_in[rows_one:]
-    gram_y = jnp.concatenate(
-        [folded_y[:, k // ROWS * ny : (k // ROWS + 1) * ny] for k in groups_y], axis=0
-    )
-    sum_in = sum_in[:rows_one]
-    sum_in = jnp.concatenate([sum_in] + all_but(sum_in, "mode"), axis=0)
+    kept, sent = (block(sum_in, (m & 1) ^ s, rows_in // 2, 0) for s in range(2))
+    sum_in = kept + swap(sent, "mode", 1)
+    s = 2
+    while s < nm:
+        sum_in = sum_in + swap(sum_in, "mode", s)
+        s *= 2
+    sum_in = jnp.concatenate([sum_in, swap(sum_in, "mode", 1)], axis=0)
     gathered = [sum_in] + all_but(sum_in, "fsdp")
     (full_in,) = sweeps(gathered, start_in, (False, True))
-    (factor_y,) = sweeps([gram_y], start_y)
 
     gram_out = [None]
     for k, (run, parts) in enumerate(zip(fsdp_runs, fsdp_parts)):
         last = k == len(fsdp_runs) - 1
         base = f * per_fsdp + run[0]
-        gram_out = gram_out_part(flat, base, parts, f, gram_out[0], last)
+        gram_out = gram_out_part(flat, base, parts, f, gram_out[0], last, folded_y)
     sum_out = added([gram_out[0]] + [swap(gram_out[s], "fsdp", s) for s in range(1, nf)])
     sum_out = added([sum_out] + all_but(sum_out, "mode"))
+    folded_y = sum_out[no:]
+    gram_y = jnp.concatenate(
+        [folded_y[:, k // ROWS * ny : (k // ROWS + 1) * ny] for k in groups_y], axis=0
+    )
+    (factor_y,) = sweeps([gram_y], start_y)
+    sum_out = sum_out[:no]
     gathered = [sum_out] + all_but(sum_out, "fsdp")
     full_out, turned_out = sweeps(gathered, relative_rows(start_out, f, nf), (True, False), f, nf)
 

time: 715 us -> 683 us (0.955)
  local copies, waits for them, and re-layouts: 42.2 us -> 63.5 us
  Pallas kernels: 144 us -> 125 us
  waiting for transfers between devices: 311 us -> 295 us
    unnamed x119 -> x169, local copies, waits for them, and re-layouts: 11.4 us -> 35.5 us
    ppermute x89 -> x86, waiting for transfers between devices: 311 us -> 295 us  [swap(): return lax.ppermute(value, axis, [(i, i ^ s) for i in range(n)])]
    pallas_call x8, Pallas kernels: 43 us -> 33.8 us  [gram_parts(): pl.pallas_call(kernel, grid_spec=grid_spec, out_shape=[jax.ShapeDtypeStru...]
    ppermute x89 -> x86, starting transfers between devices: 180 us -> 176 us  [swap(): return lax.ppermute(value, axis, [(i, i ^ s) for i in range(n)])]
  transfers between devices with their start and end apart: 89 -> 86, of which waited for: 38 -> 39; matrix products, arithmetic and copies ran while one was open for 5% -> 4% of each run, Pallas kernels for 18% -> 18%
where the time goes in v2:
time: 683 us; the launch traced here: 682 us
  waiting for transfers between devices  295 us (43%)
  starting transfers between devices  176 us (26%)
  Pallas kernels  125 us (18%)
  local copies, waits for them, and re-layouts  63.5 us (9%)
  matrix products  19.5 us (3%)
    ppermute x86, waiting for transfers between devices, swap(): return lax.ppermute(value, axis, [(i, i ^ s) for i in range(n)])  295 us
    ppermute x86, starting transfers between devices, swap(): return lax.ppermute(value, axis, [(i, i ^ s) for i in range(n)])  176 us
    pallas_call x4, Pallas kernels, sweeps(): pl.pallas_call(kernel, in_specs=[pl.BlockSpec(memory_space=pltpu.SMEM)] +...  51.6 us
    unnamed x169, local copies, waits for them, and re-layouts  35.5 us
    pallas_call x8, Pallas kernels, gram_parts(): pl.pallas_call(kernel, grid_spec=grid_spec, out_shape=[jax.ShapeDtypeStru...  33.8 us
    dynamic_slice x5, local copies, waits for them, and re-layouts, cut(): lax.dynamic_slice(source, (0, (place ^ s) * per + run[0], 0, 0), (nx, run...  25 us
    pallas_call x2, Pallas kernels, project(): pl.pallas_call(kernel, grid_spec=grid_spec, out_shape=[jax.ShapeDtypeStru...  20.7 us
    dot_general x1, matrix products, shards(): lax.dot_general(rows, rows, (((0,), (0,)), ((), ())), precision=lax.Preci...  19.5 us
  transfers between devices with their start and end apart: 86, of which 39 were waited for; matrix products, arithmetic and copies ran while one was open for 4% of the time, Pallas kernels for 18%

profile of v2, /device:TPU:0, one launch (start us, length us, event | category | flops | bytes accessed | tf_op | source)
XLA Modules:
  0.0 681.8 jit_solution(17410808024478579459)
XLA Ops:
  0.8 3.6 constant_dynamic-slice_fusion.4
  4.3 3.8 constant_dynamic-slice_fusion.21
  8.1 19.5 %convolution_bitcast_fusion = f32[512,512]{1,0:T(8,128)S(1)} fusion(f32[8,16,2,32,512]{4,3,2,1,0:T(8,128)} %g_ref), kind=kOutput, calls=%fused_computation | convolution fusion | flops 12884901888 | bytes 17825792 | tf_op jit(solution)/shard_map/dot_general | solution.py:608
  28.3 3.6 collective-permute-start.6
  41.5 2.9 collective-permute-done.3
  56.0 8.4 %constant_dynamic-slice_fusion.27 = (f32[8,3,32,512]{3,2,1,0:T(8,128)S(1)}, f32[8,3,32,512]{3,2,1,0:T(8,128)S(1)}, f32[8,3,32,512]{3,2,1,0:T(8,128)}, f32[8,3,32...) fusion(f32[8,32,32,512]{3,2,1,0:T(8,128)} %bitcast.22, ...), kind=kLoop, calls=%fused_computation.43 | loop fusion | bytes 22020124 | tf_op jit(solution)/shard_map/dynamic_slice | solution.py:573
  70.1 34.7 %collective-permute-done.16.refs_7_ = f32[64,512]{1,0:T(8,128)S(1)} collective-permute-done((f32[64,512]{1,0:T(8,128)S(1)}, f32[64,512]{1,0:T(8,128)S(1)}, u32[]{:S(2)}, u32[]{:S(2)}) %collective-permute-start.16) | collective-permute-done | bytes 131104 | tf_op jit(solution)/shard_map/ppermute | solution.py:509
  108.3 35.8 %collective-permute-done.14.refs_5_ = f32[64,512]{1,0:T(8,128)S(1)} collective-permute-done((f32[64,512]{1,0:T(8,128)S(1)}, f32[64,512]{1,0:T(8,128)S(1)}, u32[]{:S(2)}, u32[]{:S(2)}) %collective-permute-start.14) | collective-permute-done | bytes 131104 | tf_op jit(solution)/shard_map/ppermute | solution.py:509
  155.3 10.9 %collective-permute-done.29.refs_5_ = f32[8,1,32,512]{3,2,1,0:T(8,128)S(1)} collective-permute-done((f32[8,1,32,512]{3,2,1,0:T(8,128)S(1)}, f32[8,1,32,512]{3,2,1,0:T(8,128)S(1)}, u32[]{:S(2)}, u32[]{:S(2)}) %collective-permute-start.29) | collective-permute-done | bytes 524320 | tf_op jit(solution)/shard_map/ppermute | solution.py:509
  167.0 10.3 %collective-permute-done.28.refs_4_ = f32[8,1,32,512]{3,2,1,0:T(8,128)S(1)} collective-permute-done((f32[8,1,32,512]{3,2,1,0:T(8,128)S(1)}, f32[8,1,32,512]{3,2,1,0:T(8,128)S(1)}, u32[]{:S(2)}, u32[]{:S(2)}) %collective-permute-start.28) | collective-permute-done | bytes 524320 | tf_op jit(solution)/shard_map/ppermute | solution.py:509
  178.7 9.8 %collective-permute-done.27.refs_3_ = f32[8,1,32,512]{3,2,1,0:T(8,128)S(1)} collective-permute-done((f32[8,1,32,512]{3,2,1,0:T(8,128)S(1)}, f32[8,1,32,512]{3,2,1,0:T(8,128)S(1)}, u32[]{:S(2)}, u32[]{:S(2)}) %collective-permute-start.27) | collective-permute-done | bytes 524320 | tf_op jit(solution)/shard_map/ppermute | solution.py:509
  197.7 5.5 constant_dynamic-slice_fusion.6
  203.2 23.5 %collective-permute-done.21.refs_4_ = f32[8,3,32,512]{3,2,1,0:T(8,128)} collective-permute-done((f32[8,3,32,512]{3,2,1,0:T(8,128)}, f32[8,3,32,512]{3,2,1,0:T(8,128)}, u32[]{:S(2)}, u32[]{:S(2)}) %collective-permute-start.21) | collective-permute-done | bytes 1572896 | tf_op jit(solution)/shard_map/ppermute | solution.py:509
  229.5 31.5 %collective-permute-done.20.refs_3_ = f32[8,3,32,512]{3,2,1,0:T(8,128)} collective-permute-done((f32[8,3,32,512]{3,2,1,0:T(8,128)}, f32[8,3,32,512]{3,2,1,0:T(8,128)}, u32[]{:S(2)}, u32[]{:S(2)}) %collective-permute-start.20) | collective-permute-done | bytes 1572896 | tf_op jit(solution)/shard_map/ppermute | solution.py:509
  261.0 3.2 collective-permute-start.61
  267.0 13.3 %gram_y.1 = f32[16,16]{1,0:T(8,128)S(1)} custom-call(f32[8,16,2,32,512]{4,3,2,1,0:T(8,128)} %g_ref), custom_call_target="tpu_custom_call" | custom-call | tf_op jit(solution)/shard_map/gram_y/pallas_call | solution.py:99
  286.7 3.7 shard_map.92.refs_7_
  290.5 9.1 %shard_map.93 = (f32[40,256]{1,0:T(8,128)S(1)}, f32[40,256]{1,0:T(8,128)S(1)}, f32[40,256]{1,0:T(8,128)S(1)}, f32[40,256]{1,0:T(8,128)S(1)}, f32[40,256]{1,0:T(8...) custom-call(s32[2]{0:T(128)S(1)} %get-tuple-element.125.s_ref, ...), custom_call_target="tpu_custom_call" | custom-call | tf_op jit(solution)/shard_map/pallas_call | solution.py:160
  303.9 18.5 %collective-permute-start.57 = (f32[8,1,32,512]{3,2,1,0:T(8,128)S(1)}, f32[8,1,32,512]{3,2,1,0:T(8,128)S(1)}, u32[]{:S(2)}, u32[]{:S(2)}) collective-permute-start(f32[8,1,32,512]{3,2,1,0:T(8,128)S(1)} %copy-done.71), channel_id=1, source_target_pairs={{0,1},{1,0},{2,3},{3,2},{4,5},{5,4},{6,7},{7,6},{8,9},{9,8},{10,11... | collective-permute-start | bytes 1572872 | tf_op jit(solution)/shard_map/ppermute | solution.py:509
  322.4 3.4 collective-permute-start.56
  325.9 3.8 collective-permute-done.35
  330.8 3.9 collective-permute-done.36
  334.7 4.3 collective-permute-done.37
  343.7 11.4 %collective-permute-done.57.refs_0_ = f32[8,1,32,512]{3,2,1,0:T(8,128)S(1)} collective-permute-done((f32[8,1,32,512]{3,2,1,0:T(8,128)S(1)}, f32[8,1,32,512]{3,2,1,0:T(8,128)S(1)}, u32[]{:S(2)}, u32[]{:S(2)}) %collective-permute-start.57) | collective-permute-done | bytes 524320 | tf_op jit(solution)/shard_map/ppermute | solution.py:509
  356.7 35.2 %collective-permute-start.54 = (f32[8,1,32,512]{3,2,1,0:T(8,128)}, f32[8,1,32,512]{3,2,1,0:T(8,128)}, u32[]{:S(2)}, u32[]{:S(2)}) collective-permute-start(f32[8,1,32,512]{3,2,1,0:T(8,128)} %get-tuple-element.89), channel_id=1, source_target_pairs={{0,1},{1,0},{2,3},{3,2},{4,5},{5,4},{6,7},{7,6},{8,9},{9,8},{10,11... | collective-permute-start | bytes 1572872 | tf_op jit(solution)/shard_map/ppermute | solution.py:509
  391.9 9.3 %collective-permute-done.55.refs_1_ = f32[8,1,32,512]{3,2,1,0:T(8,128)S(1)} collective-permute-done((f32[8,1,32,512]{3,2,1,0:T(8,128)}, f32[8,1,32,512]{3,2,1,0:T(8,128)S(1)}, u32[]{:S(2)}, u32[]{:S(2)}) %collective-permute-start.55) | collective-permute-done | bytes 524320 | tf_op jit(solution)/shard_map/ppermute | solution.py:509
  402.0 3.9 collective-permute-start.53
  405.9 32.9 %collective-permute-start.52 = (f32[8,1,32,512]{3,2,1,0:T(8,128)}, f32[8,1,32,512]{3,2,1,0:T(8,128)}, u32[]{:S(2)}, u32[]{:S(2)}) collective-permute-start(f32[8,1,32,512]{3,2,1,0:T(8,128)} %get-tuple-element.91), channel_id=1, source_target_pairs={{0,2},{1,3},{2,0},{3,1},{4,6},{5,7},{6,4},{7,5},{8,10},{9,11},{10,... | collective-permute-start | bytes 1572872 | tf_op jit(solution)/shard_map/ppermute | solution.py:509
  439.6 9.6 %collective-permute-done.38 = f32[40,256]{1,0:T(8,128)S(1)} collective-permute-done((f32[40,256]{1,0:T(8,128)S(1)}, f32[40,256]{1,0:T(8,128)S(1)}, u32[]{:S(2)}, u32[]{:S(2)}) %collective-permute-start.38) | collective-permute-done | bytes 40992 | tf_op jit(solution)/shard_map/ppermute | solution.py:509
  451.6 3.7 constant_dynamic-slice_fusion.18
  456.5 5.8 collective-permute-start.64
  462.2 8.4 %collective-permute-done.52.refs_1_ = f32[8,1,32,512]{3,2,1,0:T(8,128)} collective-permute-done((f32[8,1,32,512]{3,2,1,0:T(8,128)}, f32[8,1,32,512]{3,2,1,0:T(8,128)}, u32[]{:S(2)}, u32[]{:S(2)}) %collective-permute-start.52) | collective-permute-done | bytes 524320 | tf_op jit(solution)/shard_map/ppermute | solution.py:509
  471.5 21.0 %collective-permute-done.51.refs_0_ = f32[8,1,32,512]{3,2,1,0:T(8,128)} collective-permute-done((f32[8,1,32,512]{3,2,1,0:T(8,128)}, f32[8,1,32,512]{3,2,1,0:T(8,128)}, u32[]{:S(2)}, u32[]{:S(2)}) %collective-permute-start.51) | collective-permute-done | bytes 524320 | tf_op jit(solution)/shard_map/ppermute | solution.py:509
  501.8 3.4 collective-permute-start.48
  515.1 25.3 %sweeps.4.refs_7_ = f32[512,128]{1,0:T(8,128)S(1)} custom-call(s32[1]{0:T(128)} %constant.44.clone.1.place_ref, f32[64,512]{1,0:T(8,128)S(1)} %pad_maximum_fusion.refs_0_, f32[64,512]{1,0:T(8,128)S(1)} %copy-done.46, f32[64,512]{1,0:T(8,128)S(1)} %copy-done.44, f32[64,512]{1,0:T(8,128)S(1)} %copy-done.42, f32[64,512]{1,0:T(8,128)S(1)} %copy-done.40, ...), custom_call_target="tpu_custom_call" | custom-call | tf_op jit(solution)/shard_map/sweeps/pallas_call | solution.py:493
  540.5 22.5 %sweeps.5 = (f32[256,128]{1,0:T(8,128)S(1)}, f32[128,256]{1,0:T(8,128)S(1)}) custom-call(s32[1]{0:T(128)} %bitcast.4.place_ref.s_ref, f32[32,256]{1,0:T(8,128)S(1)} %copy-done.48, f32[32,256]{1,0:T(8,128)S(1)} %copy-done.62, f32[32,256]{1,0:T(8,128)S(1)} %copy-done.60, f32[32,256]{1,0:T(8,128)S(1)} %copy-done.58, f32[32,256]{1,0:T(8,128)S(1)} %copy-done.56, ...), custom_call_target="tpu_custom_call" | custom-call | tf_op jit(solution)/shard_map/sweeps/pallas_call | solution.py:493
  564.1 6.2 project.2
  570.3 14.5 %project.3 = (f32[8,4,16,128]{3,2,1,0:T(8,128)S(1)}, f32[8,4,16,128]{3,2,1,0:T(8,128)S(1)}, f32[8,4,16,128]{3,2,1,0:T(8,128)}, f32[8,4,16,128]{3,2,1,0:T(8,128)S...) custom-call(s32[1]{0:T(128)} %bitcast.5.s_ref, ...), custom_call_target="tpu_custom_call", output_to_operand_aliasing={{0}: (11, {}), {1}: (12, {}), {2}: (13, {}), {3}: (14, {}),... | custom-call | tf_op jit(solution)/shard_map/project/pallas_call | solution.py:265
  589.6 4.1 shard_map.94.refs_3_
  593.8 3.1 shard_map.95.refs_3_
  602.5 3.1 shard_map.98.refs_3_
  605.6 5.1 shard_map.99
  621.7 10.3 %collective-permute-done.76.refs_4_ = f32[8,4,16,128]{3,2,1,0:T(8,128)S(1)} collective-permute-done((f32[8,4,16,128]{3,2,1,0:T(8,128)S(1)}, f32[8,4,16,128]{3,2,1,0:T(8,128)S(1)}, u32[]{:S(2)}, u32[]{:S(2)}) %collective-permute-start.76) | collective-permute-done | bytes 262176 | tf_op jit(solution)/shard_map/ppermute | solution.py:509
  632.2 4.3 collective-permute-done.77.refs_5_
  636.5 2.8 contract_y.1
  649.0 3.1 collective-permute-done.72
  654.4 11.7 %collective-permute-done.81.refs_2_ = f32[8,64,128]{2,1,0:T(8,128)S(1)} collective-permute-done((f32[8,64,128]{2,1,0:T(8,128)S(1)}, f32[8,64,128]{2,1,0:T(8,128)S(1)}, u32[]{:S(2)}, u32[]{:S(2)}) %collective-permute-start.81) | collective-permute-done | bytes 262176 | tf_op jit(solution)/shard_map/ppermute | solution.py:509
  675.1 5.8 collective-permute-done.84.refs_2_
  (344 shorter events, 146.8 us)
Async XLA Ops:
  51.7 102.4 %collective-permute-start.30 = (f32[8,1,32,512]{3,2,1,0:T(8,128)}, f32[8,1,32,512]{3,2,1,0:T(8,128)S(1)}, u32[]{:S(2)}, u32[]{:S(2)}) collective-permute-start(f32[8,1,32,512]{3,2,1,0:T(8,128)} %get-tuple-element.96), channel_id=1, source_target_pairs={{0,28},{4,24},{8,20},{12,16},{16,12},{20,8},{24,4},{28,0},{1,29},{... | collective-permute-start | bytes 1572872 | tf_op jit(solution)/shard_map/ppermute | solution.py:509
  64.4 129.8 %collective-permute-start.23 = (f32[8,3,32,512]{3,2,1,0:T(8,128)S(1)}, f32[8,3,32,512]{3,2,1,0:T(8,128)S(1)}, u32[]{:S(2)}, u32[]{:S(2)}) collective-permute-start(f32[8,3,32,512]{3,2,1,0:T(8,128)S(1)} %get-tuple-element.103), channel_id=1, source_target_pairs={{0,28},{4,24},{8,20},{12,16},{16,12},{20,8},{24,4},{28,0},{1,29},{... | collective-permute-start | bytes 4718600 | tf_op jit(solution)/shard_map/ppermute | solution.py:509
  64.5 40.4 %collective-permute-start.16 = (f32[64,512]{1,0:T(8,128)S(1)}, f32[64,512]{1,0:T(8,128)S(1)}, u32[]{:S(2)}, u32[]{:S(2)}) collective-permute-start(f32[64,512]{1,0:T(8,128)S(1)} %pad_maximum_fusion.refs_0_), channel_id=1, source_target_pairs={{0,28},{4,24},{8,20},{12,16},{16,12},{20,8},{24,4},{28,0},{1,29},{... | collective-permute-start | bytes 393224 | tf_op jit(solution)/shard_map/ppermute | solution.py:509
  67.2 40.5 %collective-permute-start.15 = (f32[64,512]{1,0:T(8,128)S(1)}, f32[64,512]{1,0:T(8,128)S(1)}, u32[]{:S(2)}, u32[]{:S(2)}) collective-permute-start(f32[64,512]{1,0:T(8,128)S(1)} %pad_maximum_fusion.refs_0_), channel_id=1, source_target_pairs={{0,24},{4,28},{8,16},{12,20},{16,8},{20,12},{24,0},{28,4},{1,25},{... | collective-permute-start | bytes 393224 | tf_op jit(solution)/shard_map/ppermute | solution.py:509
  69.5 125.9 %collective-permute-start.22 = (f32[8,3,32,512]{3,2,1,0:T(8,128)S(1)}, f32[8,3,32,512]{3,2,1,0:T(8,128)S(1)}, u32[]{:S(2)}, u32[]{:S(2)}) collective-permute-start(f32[8,3,32,512]{3,2,1,0:T(8,128)S(1)} %get-tuple-element.104), channel_id=1, source_target_pairs={{0,24},{4,28},{8,16},{12,20},{16,8},{20,12},{24,0},{28,4},{1,25},{... | collective-permute-start | bytes 4718600 | tf_op jit(solution)/shard_map/ppermute | solution.py:509
  104.8 39.3 %collective-permute-start.14 = (f32[64,512]{1,0:T(8,128)S(1)}, f32[64,512]{1,0:T(8,128)S(1)}, u32[]{:S(2)}, u32[]{:S(2)}) collective-permute-start(f32[64,512]{1,0:T(8,128)S(1)} %pad_maximum_fusion.refs_0_), channel_id=1, source_target_pairs={{0,20},{4,16},{8,28},{12,24},{16,4},{20,0},{24,12},{28,8},{1,21},{... | collective-permute-start | bytes 393224 | tf_op jit(solution)/shard_map/ppermute | solution.py:509
  108.3 38.7 %collective-permute-start.13 = (f32[64,512]{1,0:T(8,128)S(1)}, f32[64,512]{1,0:T(8,128)S(1)}, u32[]{:S(2)}, u32[]{:S(2)}) collective-permute-start(f32[64,512]{1,0:T(8,128)S(1)} %pad_maximum_fusion.refs_0_), channel_id=1, source_target_pairs={{0,16},{4,20},{8,24},{12,28},{16,0},{20,4},{24,8},{28,12},{1,17},{... | collective-permute-start | bytes 393224 | tf_op jit(solution)/shard_map/ppermute | solution.py:509
  154.1 23.3 %collective-permute-start.28 = (f32[8,1,32,512]{3,2,1,0:T(8,128)S(1)}, f32[8,1,32,512]{3,2,1,0:T(8,128)S(1)}, u32[]{:S(2)}, u32[]{:S(2)}) collective-permute-start(f32[8,1,32,512]{3,2,1,0:T(8,128)S(1)} %copy-done.69), channel_id=1, source_target_pairs={{0,20},{4,16},{8,28},{12,24},{16,4},{20,0},{24,12},{28,8},{1,21},{... | collective-permute-start | bytes 1572872 | tf_op jit(solution)/shard_map/ppermute | solution.py:509
  154.1 34.4 %collective-permute-start.27 = (f32[8,1,32,512]{3,2,1,0:T(8,128)S(1)}, f32[8,1,32,512]{3,2,1,0:T(8,128)S(1)}, u32[]{:S(2)}, u32[]{:S(2)}) collective-permute-start(f32[8,1,32,512]{3,2,1,0:T(8,128)S(1)} %copy-done.68), channel_id=1, source_target_pairs={{0,16},{4,20},{8,24},{12,28},{16,0},{20,4},{24,8},{28,12},{1,17},{... | collective-permute-start | bytes 1572872 | tf_op jit(solution)/shard_map/ppermute | solution.py:509
  167.0 22.5 %collective-permute-start.26 = (f32[8,1,32,512]{3,2,1,0:T(8,128)S(1)}, f32[8,1,32,512]{3,2,1,0:T(8,128)S(1)}, u32[]{:S(2)}, u32[]{:S(2)}) collective-permute-start(f32[8,1,32,512]{3,2,1,0:T(8,128)S(1)} %copy-done.67), channel_id=1, source_target_pairs={{0,12},{4,8},{8,4},{12,0},{16,28},{20,24},{24,20},{28,16},{1,13},{... | collective-permute-start | bytes 1572872 | tf_op jit(solution)/shard_map/ppermute | solution.py:509
  190.2 36.5 %collective-permute-start.21 = (f32[8,3,32,512]{3,2,1,0:T(8,128)}, f32[8,3,32,512]{3,2,1,0:T(8,128)}, u32[]{:S(2)}, u32[]{:S(2)}) collective-permute-start(f32[8,3,32,512]{3,2,1,0:T(8,128)} %get-tuple-element.105), channel_id=1, source_target_pairs={{0,20},{4,16},{8,28},{12,24},{16,4},{20,0},{24,12},{28,8},{1,21},{... | collective-permute-start | bytes 4718600 | tf_op jit(solution)/shard_map/ppermute | solution.py:509
  192.9 68.1 %collective-permute-start.20 = (f32[8,3,32,512]{3,2,1,0:T(8,128)}, f32[8,3,32,512]{3,2,1,0:T(8,128)}, u32[]{:S(2)}, u32[]{:S(2)}) collective-permute-start(f32[8,3,32,512]{3,2,1,0:T(8,128)} %get-tuple-element.106), channel_id=1, source_target_pairs={{0,16},{4,20},{8,24},{12,28},{16,0},{20,4},{24,8},{28,12},{1,17},{... | collective-permute-start | bytes 4718600 | tf_op jit(solution)/shard_map/ppermute | solution.py:509
  194.2 69.9 %collective-permute-start.19 = (f32[8,3,32,512]{3,2,1,0:T(8,128)}, f32[8,3,32,512]{3,2,1,0:T(8,128)}, u32[]{:S(2)}, u32[]{:S(2)}) collective-permute-start(f32[8,3,32,512]{3,2,1,0:T(8,128)} %get-tuple-element.107), channel_id=1, source_target_pairs={{0,12},{4,8},{8,4},{12,0},{16,28},{20,24},{24,20},{28,16},{1,13},{... | collective-permute-start | bytes 4718600 | tf_op jit(solution)/shard_map/ppermute | solution.py:509
  194.3 70.1 %collective-permute-start.18 = (f32[8,3,32,512]{3,2,1,0:T(8,128)}, f32[8,3,32,512]{3,2,1,0:T(8,128)S(1)}, u32[]{:S(2)}, u32[]{:S(2)}) collective-permute-start(f32[8,3,32,512]{3,2,1,0:T(8,128)} %get-tuple-element.108), channel_id=1, source_target_pairs={{0,8},{4,12},{8,0},{12,4},{16,24},{20,28},{24,16},{28,20},{1,9},{5... | collective-permute-start | bytes 4718600 | tf_op jit(solution)/shard_map/ppermute | solution.py:509
  196.7 83.6 %collective-permute-start.17 = (f32[8,3,32,512]{3,2,1,0:T(8,128)}, f32[8,3,32,512]{3,2,1,0:T(8,128)S(1)}, u32[]{:S(2)}, u32[]{:S(2)}) collective-permute-start(f32[8,3,32,512]{3,2,1,0:T(8,128)} %get-tuple-element.109), channel_id=1, source_target_pairs={{0,4},{4,0},{8,12},{12,8},{16,20},{20,16},{24,28},{28,24},{1,5},{5... | collective-permute-start | bytes 4718600 | tf_op jit(solution)/shard_map/ppermute | solution.py:509
  226.7 73.5 %collective-permute-start.62 = (f32[8,1,32,512]{3,2,1,0:T(8,128)}, f32[8,1,32,512]{3,2,1,0:T(8,128)}, u32[]{:S(2)}, u32[]{:S(2)}) collective-permute-start(f32[8,1,32,512]{3,2,1,0:T(8,128)} %get-tuple-element.81), channel_id=1, source_target_pairs={{0,3},{1,2},{2,1},{3,0},{4,7},{5,6},{6,5},{7,4},{8,11},{9,10},{10,... | collective-permute-start | bytes 1572872 | tf_op jit(solution)/shard_map/ppermute | solution.py:509
  261.0 40.1 %collective-permute-start.61 = (f32[8,1,32,512]{3,2,1,0:T(8,128)}, f32[8,1,32,512]{3,2,1,0:T(8,128)}, u32[]{:S(2)}, u32[]{:S(2)}) collective-permute-start(f32[8,1,32,512]{3,2,1,0:T(8,128)} %get-tuple-element.82), channel_id=1, source_target_pairs={{0,2},{1,3},{2,0},{3,1},{4,6},{5,7},{6,4},{7,5},{8,10},{9,11},{10,... | collective-permute-start | bytes 1572872 | tf_op jit(solution)/shard_map/ppermute | solution.py:509
  264.1 37.5 %collective-permute-start.60 = (f32[8,1,32,512]{3,2,1,0:T(8,128)}, f32[8,1,32,512]{3,2,1,0:T(8,128)}, u32[]{:S(2)}, u32[]{:S(2)}) collective-permute-start(f32[8,1,32,512]{3,2,1,0:T(8,128)} %get-tuple-element.83), channel_id=1, source_target_pairs={{0,1},{1,0},{2,3},{3,2},{4,5},{5,4},{6,7},{7,6},{8,9},{9,8},{10,11... | collective-permute-start | bytes 1572872 | tf_op jit(solution)/shard_map/ppermute | solution.py:509
  264.3 38.3 %collective-permute-start.59 = (f32[8,1,32,512]{3,2,1,0:T(8,128)}, f32[8,1,32,512]{3,2,1,0:T(8,128)}, u32[]{:S(2)}, u32[]{:S(2)}) collective-permute-start(f32[8,1,32,512]{3,2,1,0:T(8,128)} %get-tuple-element.84), channel_id=1, source_target_pairs={{0,3},{1,2},{2,1},{3,0},{4,7},{5,6},{6,5},{7,4},{8,11},{9,10},{10,... | collective-permute-start | bytes 1572872 | tf_op jit(solution)/shard_map/ppermute | solution.py:509
  300.2 22.3 %collective-permute-start.32 = (f32[40,256]{1,0:T(8,128)S(1)}, f32[40,256]{1,0:T(8,128)S(1)}, u32[]{:S(2)}, u32[]{:S(2)}) collective-permute-start(f32[40,256]{1,0:T(8,128)S(1)} %get-tuple-element.44), channel_id=1, source_target_pairs={{0,8},{4,12},{8,0},{12,4},{16,24},{20,28},{24,16},{28,20},{1,9},{5... | collective-permute-start | bytes 122888 | tf_op jit(solution)/shard_map/ppermute | solution.py:509
  301.1 24.8 %collective-permute-start.33 = (f32[40,256]{1,0:T(8,128)S(1)}, f32[40,256]{1,0:T(8,128)S(1)}, u32[]{:S(2)}, u32[]{:S(2)}) collective-permute-start(f32[40,256]{1,0:T(8,128)S(1)} %get-tuple-element.45), channel_id=1, source_target_pairs={{0,12},{4,8},{8,4},{12,0},{16,28},{20,24},{24,20},{28,16},{1,13},{... | collective-permute-start | bytes 122888 | tf_op jit(solution)/shard_map/ppermute | solution.py:509
  301.6 38.9 %collective-permute-start.58 = (f32[8,1,32,512]{3,2,1,0:T(8,128)S(1)}, f32[8,1,32,512]{3,2,1,0:T(8,128)S(1)}, u32[]{:S(2)}, u32[]{:S(2)}) collective-permute-start(f32[8,1,32,512]{3,2,1,0:T(8,128)S(1)} %copy-done.72), channel_id=1, source_target_pairs={{0,2},{1,3},{2,0},{3,1},{4,6},{5,7},{6,4},{7,5},{8,10},{9,11},{10,... | collective-permute-start | bytes 1572872 | tf_op jit(solution)/shard_map/ppermute | solution.py:509
  302.6 23.2 %collective-permute-start.34 = (f32[40,256]{1,0:T(8,128)S(1)}, f32[40,256]{1,0:T(8,128)S(1)}, u32[]{:S(2)}, u32[]{:S(2)}) collective-permute-start(f32[40,256]{1,0:T(8,128)S(1)} %get-tuple-element.46), channel_id=1, source_target_pairs={{0,16},{4,20},{8,24},{12,28},{16,0},{20,4},{24,8},{28,12},{1,17},{... | collective-permute-start | bytes 122888 | tf_op jit(solution)/shard_map/ppermute | solution.py:509
  303.9 51.1 %collective-permute-start.57 = (f32[8,1,32,512]{3,2,1,0:T(8,128)S(1)}, f32[8,1,32,512]{3,2,1,0:T(8,128)S(1)}, u32[]{:S(2)}, u32[]{:S(2)}) collective-permute-start(f32[8,1,32,512]{3,2,1,0:T(8,128)S(1)} %copy-done.71), channel_id=1, source_target_pairs={{0,1},{1,0},{2,3},{3,2},{4,5},{5,4},{6,7},{7,6},{8,9},{9,8},{10,11... | collective-permute-start | bytes 1572872 | tf_op jit(solution)/shard_map/ppermute | solution.py:509
  322.4 33.4 %collective-permute-start.56 = (f32[8,1,32,512]{3,2,1,0:T(8,128)}, f32[8,1,32,512]{3,2,1,0:T(8,128)S(1)}, u32[]{:S(2)}, u32[]{:S(2)}) collective-permute-start(f32[8,1,32,512]{3,2,1,0:T(8,128)} %get-tuple-element.87), channel_id=1, source_target_pairs={{0,3},{1,2},{2,1},{3,0},{4,7},{5,6},{6,5},{7,4},{8,11},{9,10},{10,... | collective-permute-start | bytes 1572872 | tf_op jit(solution)/shard_map/ppermute | solution.py:509
  325.8 75.3 %collective-permute-start.55 = (f32[8,1,32,512]{3,2,1,0:T(8,128)}, f32[8,1,32,512]{3,2,1,0:T(8,128)S(1)}, u32[]{:S(2)}, u32[]{:S(2)}) collective-permute-start(f32[8,1,32,512]{3,2,1,0:T(8,128)} %get-tuple-element.88), channel_id=1, source_target_pairs={{0,2},{1,3},{2,0},{3,1},{4,6},{5,7},{6,4},{7,5},{8,10},{9,11},{10,... | collective-permute-start | bytes 1572872 | tf_op jit(solution)/shard_map/ppermute | solution.py:509
  339.0 154.3 %collective-permute-start.65 = (f32[8,2,32,512]{3,2,1,0:T(8,128)}, f32[8,2,32,512]{3,2,1,0:T(8,128)}, u32[]{:S(2)}, u32[]{:S(2)}) collective-permute-start(f32[8,2,32,512]{3,2,1,0:T(8,128)} %get-tuple-element.78), channel_id=1, source_target_pairs={{0,3},{1,2},{2,1},{3,0},{4,7},{5,6},{6,5},{7,4},{8,11},{9,10},{10,... | collective-permute-start | bytes 3145736 | tf_op jit(solution)/shard_map/ppermute | solution.py:509
  341.3 64.5 %collective-permute-start.40 = (f32[40,256]{1,0:T(8,128)S(1)}, f32[40,256]{1,0:T(8,128)S(1)}, u32[]{:S(2)}, u32[]{:S(2)}) collective-permute-start(f32[40,256]{1,0:T(8,128)S(1)} %add_add_fusion.2), channel_id=1, source_target_pairs={{0,3},{1,2},{2,1},{3,0},{4,7},{5,6},{6,5},{7,4},{8,11},{9,10},{10,... | collective-permute-start | bytes 122888 | tf_op jit(solution)/shard_map/ppermute | solution.py:509
  355.9 82.9 %collective-permute-start.39 = (f32[40,256]{1,0:T(8,128)S(1)}, f32[40,256]{1,0:T(8,128)S(1)}, u32[]{:S(2)}, u32[]{:S(2)}) collective-permute-start(f32[40,256]{1,0:T(8,128)S(1)} %add_add_fusion.2), channel_id=1, source_target_pairs={{0,2},{1,3},{2,0},{3,1},{4,6},{5,7},{6,4},{7,5},{8,10},{9,11},{10,... | collective-permute-start | bytes 122888 | tf_op jit(solution)/shard_map/ppermute | solution.py:509
  356.7 99.6 %collective-permute-start.54 = (f32[8,1,32,512]{3,2,1,0:T(8,128)}, f32[8,1,32,512]{3,2,1,0:T(8,128)}, u32[]{:S(2)}, u32[]{:S(2)}) collective-permute-start(f32[8,1,32,512]{3,2,1,0:T(8,128)} %get-tuple-element.89), channel_id=1, source_target_pairs={{0,1},{1,0},{2,3},{3,2},{4,5},{5,4},{6,7},{7,6},{8,9},{9,8},{10,11... | collective-permute-start | bytes 1572872 | tf_op jit(solution)/shard_map/ppermute | solution.py:509
  402.0 54.5 %collective-permute-start.53 = (f32[8,1,32,512]{3,2,1,0:T(8,128)}, f32[8,1,32,512]{3,2,1,0:T(8,128)}, u32[]{:S(2)}, u32[]{:S(2)}) collective-permute-start(f32[8,1,32,512]{3,2,1,0:T(8,128)} %get-tuple-element.90), channel_id=1, source_target_pairs={{0,3},{1,2},{2,1},{3,0},{4,7},{5,6},{6,5},{7,4},{8,11},{9,10},{10,... | collective-permute-start | bytes 1572872 | tf_op jit(solution)/shard_map/ppermute | solution.py:509
  405.9 64.7 %collective-permute-start.52 = (f32[8,1,32,512]{3,2,1,0:T(8,128)}, f32[8,1,32,512]{3,2,1,0:T(8,128)}, u32[]{:S(2)}, u32[]{:S(2)}) collective-permute-start(f32[8,1,32,512]{3,2,1,0:T(8,128)} %get-tuple-element.91), channel_id=1, source_target_pairs={{0,2},{1,3},{2,0},{3,1},{4,6},{5,7},{6,4},{7,5},{8,10},{9,11},{10,... | collective-permute-start | bytes 1572872 | tf_op jit(solution)/shard_map/ppermute | solution.py:509
  449.1 43.4 %collective-permute-start.51 = (f32[8,1,32,512]{3,2,1,0:T(8,128)}, f32[8,1,32,512]{3,2,1,0:T(8,128)}, u32[]{:S(2)}, u32[]{:S(2)}) collective-permute-start(f32[8,1,32,512]{3,2,1,0:T(8,128)} %get-tuple-element.92), channel_id=1, source_target_pairs={{0,1},{1,0},{2,3},{3,2},{4,5},{5,4},{6,7},{7,6},{8,9},{9,8},{10,11... | collective-permute-start | bytes 1572872 | tf_op jit(solution)/shard_map/ppermute | solution.py:509
  456.3 132.0 %collective-permute-start.63 = (f32[8,2,32,512]{3,2,1,0:T(8,128)}, f32[8,2,32,512]{3,2,1,0:T(8,128)}, u32[]{:S(2)}, u32[]{:S(2)}) collective-permute-start(f32[8,2,32,512]{3,2,1,0:T(8,128)} %get-tuple-element.80), channel_id=1, source_target_pairs={{0,1},{1,0},{2,3},{3,2},{4,5},{5,4},{6,7},{7,6},{8,9},{9,8},{10,11... | collective-permute-start | bytes 3145736 | tf_op jit(solution)/shard_map/ppermute | solution.py:509
  456.5 131.8 %collective-permute-start.64 = (f32[8,2,32,512]{3,2,1,0:T(8,128)}, f32[8,2,32,512]{3,2,1,0:T(8,128)}, u32[]{:S(2)}, u32[]{:S(2)}) collective-permute-start(f32[8,2,32,512]{3,2,1,0:T(8,128)} %get-tuple-element.79), channel_id=1, source_target_pairs={{0,2},{1,3},{2,0},{3,1},{4,6},{5,7},{6,4},{7,5},{8,10},{9,11},{10,... | collective-permute-start | bytes 3145736 | tf_op jit(solution)/shard_map/ppermute | solution.py:509
  470.6 22.7 %collective-permute-start.47 = (f32[32,256]{1,0:T(8,128)S(1)}, f32[32,256]{1,0:T(8,128)S(1)}, u32[]{:S(2)}, u32[]{:S(2)}) collective-permute-start(f32[32,256]{1,0:T(8,128)S(1)} %slice.29.refs_0_), channel_id=1, source_target_pairs={{0,28},{4,24},{8,20},{12,16},{16,12},{20,8},{24,4},{28,0},{1,29},{... | collective-permute-start | bytes 98312 | tf_op jit(solution)/shard_map/ppermute | solution.py:509
  500.8 104.8 %collective-permute-start.50 = (f32[8,2,32,512]{3,2,1,0:T(8,128)}, f32[8,2,32,512]{3,2,1,0:T(8,128)}, u32[]{:S(2)}, u32[]{:S(2)}) collective-permute-start(f32[8,2,32,512]{3,2,1,0:T(8,128)} %get-tuple-element.93), channel_id=1, source_target_pairs={{0,3},{1,2},{2,1},{3,0},{4,7},{5,6},{6,5},{7,4},{8,11},{9,10},{10,... | collective-permute-start | bytes 3145736 | tf_op jit(solution)/shard_map/ppermute | solution.py:509
  501.5 104.1 %collective-permute-start.49 = (f32[8,2,32,512]{3,2,1,0:T(8,128)}, f32[8,2,32,512]{3,2,1,0:T(8,128)}, u32[]{:S(2)}, u32[]{:S(2)}) collective-permute-start(f32[8,2,32,512]{3,2,1,0:T(8,128)} %get-tuple-element.94), channel_id=1, source_target_pairs={{0,2},{1,3},{2,0},{3,1},{4,6},{5,7},{6,4},{7,5},{8,10},{9,11},{10,... | collective-permute-start | bytes 3145736 | tf_op jit(solution)/shard_map/ppermute | solution.py:509
  501.8 103.8 %collective-permute-start.48 = (f32[8,2,32,512]{3,2,1,0:T(8,128)}, f32[8,2,32,512]{3,2,1,0:T(8,128)}, u32[]{:S(2)}, u32[]{:S(2)}) collective-permute-start(f32[8,2,32,512]{3,2,1,0:T(8,128)} %get-tuple-element.95), channel_id=1, source_target_pairs={{0,1},{1,0},{2,3},{3,2},{4,5},{5,4},{6,7},{7,6},{8,9},{9,8},{10,11... | collective-permute-start | bytes 3145736 | tf_op jit(solution)/shard_map/ppermute | solution.py:509
  588.3 25.1 %collective-permute-start.73 = (f32[8,4,16,128]{3,2,1,0:T(8,128)S(1)}, f32[8,4,16,128]{3,2,1,0:T(8,128)S(1)}, u32[]{:S(2)}, u32[]{:S(2)}) collective-permute-start(f32[8,4,16,128]{3,2,1,0:T(8,128)S(1)} %get-tuple-element.62), channel_id=1, source_target_pairs={{0,4},{4,0},{8,12},{12,8},{16,20},{20,16},{24,28},{28,24},{1,5},{5... | collective-permute-start | bytes 786440 | tf_op jit(solution)/shard_map/ppermute | solution.py:509
  588.3 26.0 %collective-permute-start.74 = (f32[8,4,16,128]{3,2,1,0:T(8,128)}, f32[8,4,16,128]{3,2,1,0:T(8,128)S(1)}, u32[]{:S(2)}, u32[]{:S(2)}) collective-permute-start(f32[8,4,16,128]{3,2,1,0:T(8,128)} %get-tuple-element.63), channel_id=1, source_target_pairs={{0,8},{4,12},{8,0},{12,4},{16,24},{20,28},{24,16},{28,20},{1,9},{5... | collective-permute-start | bytes 786440 | tf_op jit(solution)/shard_map/ppermute | solution.py:509
  611.7 20.4 %collective-permute-start.76 = (f32[8,4,16,128]{3,2,1,0:T(8,128)S(1)}, f32[8,4,16,128]{3,2,1,0:T(8,128)S(1)}, u32[]{:S(2)}, u32[]{:S(2)}) collective-permute-start(f32[8,4,16,128]{3,2,1,0:T(8,128)S(1)} %copy-done.27), channel_id=1, source_target_pairs={{0,16},{4,20},{8,24},{12,28},{16,0},{20,4},{24,8},{28,12},{1,17},{... | collective-permute-start | bytes 786440 | tf_op jit(solution)/shard_map/ppermute | solution.py:509
  612.2 24.2 %collective-permute-start.77 = (f32[8,4,16,128]{3,2,1,0:T(8,128)S(1)}, f32[8,4,16,128]{3,2,1,0:T(8,128)S(1)}, u32[]{:S(2)}, u32[]{:S(2)}) collective-permute-start(f32[8,4,16,128]{3,2,1,0:T(8,128)S(1)} %copy-done.29), channel_id=1, source_target_pairs={{0,20},{4,16},{8,28},{12,24},{16,4},{20,0},{24,12},{28,8},{1,21},{... | collective-permute-start | bytes 786440 | tf_op jit(solution)/shard_map/ppermute | solution.py:509
  613.4 23.1 %collective-permute-start.78 = (f32[8,4,16,128]{3,2,1,0:T(8,128)S(1)}, f32[8,4,16,128]{3,2,1,0:T(8,128)S(1)}, u32[]{:S(2)}, u32[]{:S(2)}) collective-permute-start(f32[8,4,16,128]{3,2,1,0:T(8,128)S(1)} %copy-done.31), channel_id=1, source_target_pairs={{0,24},{4,28},{8,16},{12,20},{16,8},{20,12},{24,0},{28,4},{1,25},{... | collective-permute-start | bytes 786440 | tf_op jit(solution)/shard_map/ppermute | solution.py:509
  614.3 22.1 %collective-permute-start.79 = (f32[8,4,16,128]{3,2,1,0:T(8,128)S(1)}, f32[8,4,16,128]{3,2,1,0:T(8,128)S(1)}, u32[]{:S(2)}, u32[]{:S(2)}) collective-permute-start(f32[8,4,16,128]{3,2,1,0:T(8,128)S(1)} %copy-done.33), channel_id=1, source_target_pairs={{0,28},{4,24},{8,20},{12,16},{16,12},{20,8},{24,4},{28,0},{1,29},{... | collective-permute-start | bytes 786440 | tf_op jit(solution)/shard_map/ppermute | solution.py:509
  619.1 23.8 %collective-permute-start.68 = (f32[32,32]{1,0:T(8,128)S(1)}, f32[32,32]{1,0:T(8,128)S(1)}, u32[]{:S(2)}, u32[]{:S(2)}) collective-permute-start(f32[32,32]{1,0:T(8,128)S(1)} %shard_map.99), channel_id=1, source_target_pairs={{0,3},{1,2},{2,1},{3,0},{4,7},{5,6},{6,5},{7,4},{8,11},{9,10},{10,... | collective-permute-start | bytes 12296 | tf_op jit(solution)/shard_map/ppermute | solution.py:509
  641.6 24.6 %collective-permute-start.81 = (f32[8,64,128]{2,1,0:T(8,128)S(1)}, f32[8,64,128]{2,1,0:T(8,128)S(1)}, u32[]{:S(2)}, u32[]{:S(2)}) collective-permute-start(f32[8,64,128]{2,1,0:T(8,128)S(1)} %get-tuple-element.111), channel_id=1, source_target_pairs={{0,2},{1,3},{2,0},{3,1},{4,6},{5,7},{6,4},{7,5},{8,10},{9,11},{10,... | collective-permute-start | bytes 786440 | tf_op jit(solution)/shard_map/ppermute | solution.py:509
  642.9 23.2 %collective-permute-start.80 = (f32[8,64,128]{2,1,0:T(8,128)S(1)}, f32[8,64,128]{2,1,0:T(8,128)S(1)}, u32[]{:S(2)}, u32[]{:S(2)}) collective-permute-start(f32[8,64,128]{2,1,0:T(8,128)S(1)} %get-tuple-element.112), channel_id=1, source_target_pairs={{0,1},{1,0},{2,3},{3,2},{4,5},{5,4},{6,7},{7,6},{8,9},{9,8},{10,11... | collective-permute-start | bytes 786440 | tf_op jit(solution)/shard_map/ppermute | solution.py:509
  (117 other events, 1928.2 us)

commit v3 on v2

--- a/solution.py
+++ b/solution.py
@@ -575,7 +575,10 @@
         ]
 
     def exchange(axis, parts):
-        return [swap(part, axis, s + 1) for s, part in enumerate(parts)]
+        arrived = []
+        for s, part in enumerate(parts):
+            arrived.append(swap(part, axis, s + 1))
+        return arrived
 
     mode_runs = pieces(per_mode, (2, 1, 1, 1, 1, 2))
     fsdp_runs = pieces(per_fsdp, (1, 3))
@@ -657,7 +660,7 @@
     by_x = by_x[:1] + [swap(by_x[s], "mode", s) for s in range(1, nm)]
     (factor_x,) = sweeps([gram_x], start_x)
     by_p = contract_x(by_x, m, factor_x)
-    by_p = [by_p[0]] + [swap(by_p[s], "mode", s) for s in range(1, nm)]
+    by_p = [by_p[0]] + exchange("mode", by_p[1:])
     core = assemble(by_p, m)
     core = core.reshape(core.shape[0], nb, -1, nc, na)
 

time: 683 us -> 683 us (level)
  no operation moved by 1% of the time
where the time goes in v3:
time: 683 us; the launch traced here: 682 us
  waiting for transfers between devices  295 us (43%)
  starting transfers between devices  176 us (26%)
  Pallas kernels  125 us (18%)
  local copies, waits for them, and re-layouts  63.5 us (9%)
  matrix products  19.5 us (3%)
    ppermute x86, waiting for transfers between devices, swap(): return lax.ppermute(value, axis, [(i, i ^ s) for i in range(n)])  295 us
    ppermute x86, starting transfers between devices, swap(): return lax.ppermute(value, axis, [(i, i ^ s) for i in range(n)])  176 us
    pallas_call x4, Pallas kernels, sweeps(): pl.pallas_call(kernel, in_specs=[pl.BlockSpec(memory_space=pltpu.SMEM)] +...  51.6 us
    unnamed x169, local copies, waits for them, and re-layouts  35.5 us
    pallas_call x8, Pallas kernels, gram_parts(): pl.pallas_call(kernel, grid_spec=grid_spec, out_shape=[jax.ShapeDtypeStru...  33.8 us
    dynamic_slice x5, local copies, waits for them, and re-layouts, cut(): lax.dynamic_slice(source, (0, (place ^ s) * per + run[0], 0, 0), (nx, run...  25 us
    pallas_call x2, Pallas kernels, project(): pl.pallas_call(kernel, grid_spec=grid_spec, out_shape=[jax.ShapeDtypeStru...  20.7 us
    dot_general x1, matrix products, shards(): lax.dot_general(rows, rows, (((0,), (0,)), ((), ())), precision=lax.Preci...  19.5 us
  transfers between devices with their start and end apart: 86, of which 39 were waited for; matrix products, arithmetic and copies ran while one was open for 4% of the time, Pallas kernels for 18%

profile of v3, /device:TPU:0, one launch (start us, length us, event | category | flops | bytes accessed | tf_op | source)
XLA Modules:
  0.0 681.8 jit_solution(17410808024478579459)
XLA Ops:
  0.8 3.6 constant_dynamic-slice_fusion.4
  4.3 3.8 constant_dynamic-slice_fusion.21
  8.1 19.5 %convolution_bitcast_fusion = f32[512,512]{1,0:T(8,128)S(1)} fusion(f32[8,16,2,32,512]{4,3,2,1,0:T(8,128)} %g_ref), kind=kOutput, calls=%fused_computation | convolution fusion | flops 12884901888 | bytes 17825792 | tf_op jit(solution)/shard_map/dot_general | solution.py:611
  28.3 3.6 collective-permute-start.6
  41.5 2.9 collective-permute-done.3
  56.0 8.4 %constant_dynamic-slice_fusion.27 = (f32[8,3,32,512]{3,2,1,0:T(8,128)S(1)}, f32[8,3,32,512]{3,2,1,0:T(8,128)S(1)}, f32[8,3,32,512]{3,2,1,0:T(8,128)}, f32[8,3,32...) fusion(f32[8,32,32,512]{3,2,1,0:T(8,128)} %bitcast.22, ...), kind=kLoop, calls=%fused_computation.43 | loop fusion | bytes 22020124 | tf_op jit(solution)/shard_map/dynamic_slice | solution.py:573
  70.1 34.7 %collective-permute-done.16.refs_7_ = f32[64,512]{1,0:T(8,128)S(1)} collective-permute-done((f32[64,512]{1,0:T(8,128)S(1)}, f32[64,512]{1,0:T(8,128)S(1)}, u32[]{:S(2)}, u32[]{:S(2)}) %collective-permute-start.16) | collective-permute-done | bytes 131104 | tf_op jit(solution)/shard_map/ppermute | solution.py:509
  108.3 35.8 %collective-permute-done.14.refs_5_ = f32[64,512]{1,0:T(8,128)S(1)} collective-permute-done((f32[64,512]{1,0:T(8,128)S(1)}, f32[64,512]{1,0:T(8,128)S(1)}, u32[]{:S(2)}, u32[]{:S(2)}) %collective-permute-start.14) | collective-permute-done | bytes 131104 | tf_op jit(solution)/shard_map/ppermute | solution.py:509
  155.3 10.9 %collective-permute-done.29.refs_5_ = f32[8,1,32,512]{3,2,1,0:T(8,128)S(1)} collective-permute-done((f32[8,1,32,512]{3,2,1,0:T(8,128)S(1)}, f32[8,1,32,512]{3,2,1,0:T(8,128)S(1)}, u32[]{:S(2)}, u32[]{:S(2)}) %collective-permute-start.29) | collective-permute-done | bytes 524320 | tf_op jit(solution)/shard_map/ppermute | solution.py:509
  167.0 10.3 %collective-permute-done.28.refs_4_ = f32[8,1,32,512]{3,2,1,0:T(8,128)S(1)} collective-permute-done((f32[8,1,32,512]{3,2,1,0:T(8,128)S(1)}, f32[8,1,32,512]{3,2,1,0:T(8,128)S(1)}, u32[]{:S(2)}, u32[]{:S(2)}) %collective-permute-start.28) | collective-permute-done | bytes 524320 | tf_op jit(solution)/shard_map/ppermute | solution.py:509
  178.7 9.8 %collective-permute-done.27.refs_3_ = f32[8,1,32,512]{3,2,1,0:T(8,128)S(1)} collective-permute-done((f32[8,1,32,512]{3,2,1,0:T(8,128)S(1)}, f32[8,1,32,512]{3,2,1,0:T(8,128)S(1)}, u32[]{:S(2)}, u32[]{:S(2)}) %collective-permute-start.27) | collective-permute-done | bytes 524320 | tf_op jit(solution)/shard_map/ppermute | solution.py:509
  197.7 5.5 constant_dynamic-slice_fusion.6
  203.2 23.5 %collective-permute-done.21.refs_4_ = f32[8,3,32,512]{3,2,1,0:T(8,128)} collective-permute-done((f32[8,3,32,512]{3,2,1,0:T(8,128)}, f32[8,3,32,512]{3,2,1,0:T(8,128)}, u32[]{:S(2)}, u32[]{:S(2)}) %collective-permute-start.21) | collective-permute-done | bytes 1572896 | tf_op jit(solution)/shard_map/ppermute | solution.py:509
  229.5 31.5 %collective-permute-done.20.refs_3_ = f32[8,3,32,512]{3,2,1,0:T(8,128)} collective-permute-done((f32[8,3,32,512]{3,2,1,0:T(8,128)}, f32[8,3,32,512]{3,2,1,0:T(8,128)}, u32[]{:S(2)}, u32[]{:S(2)}) %collective-permute-start.20) | collective-permute-done | bytes 1572896 | tf_op jit(solution)/shard_map/ppermute | solution.py:509
  261.0 3.2 collective-permute-start.61
  267.0 13.3 %gram_y.1 = f32[16,16]{1,0:T(8,128)S(1)} custom-call(f32[8,16,2,32,512]{4,3,2,1,0:T(8,128)} %g_ref), custom_call_target="tpu_custom_call" | custom-call | tf_op jit(solution)/shard_map/gram_y/pallas_call | solution.py:99
  286.7 3.7 shard_map.92.refs_7_
  290.5 9.1 %shard_map.93 = (f32[40,256]{1,0:T(8,128)S(1)}, f32[40,256]{1,0:T(8,128)S(1)}, f32[40,256]{1,0:T(8,128)S(1)}, f32[40,256]{1,0:T(8,128)S(1)}, f32[40,256]{1,0:T(8...) custom-call(s32[2]{0:T(128)S(1)} %get-tuple-element.125.s_ref, ...), custom_call_target="tpu_custom_call" | custom-call | tf_op jit(solution)/shard_map/pallas_call | solution.py:160
  303.9 18.5 %collective-permute-start.57 = (f32[8,1,32,512]{3,2,1,0:T(8,128)S(1)}, f32[8,1,32,512]{3,2,1,0:T(8,128)S(1)}, u32[]{:S(2)}, u32[]{:S(2)}) collective-permute-start(f32[8,1,32,512]{3,2,1,0:T(8,128)S(1)} %copy-done.71), channel_id=1, source_target_pairs={{0,1},{1,0},{2,3},{3,2},{4,5},{5,4},{6,7},{7,6},{8,9},{9,8},{10,11... | collective-permute-start | bytes 1572872 | tf_op jit(solution)/shard_map/ppermute | solution.py:509
  322.4 3.4 collective-permute-start.56
  325.9 3.8 collective-permute-done.35
  330.8 3.9 collective-permute-done.36
  334.7 4.3 collective-permute-done.37
  343.7 11.4 %collective-permute-done.57.refs_0_ = f32[8,1,32,512]{3,2,1,0:T(8,128)S(1)} collective-permute-done((f32[8,1,32,512]{3,2,1,0:T(8,128)S(1)}, f32[8,1,32,512]{3,2,1,0:T(8,128)S(1)}, u32[]{:S(2)}, u32[]{:S(2)}) %collective-permute-start.57) | collective-permute-done | bytes 524320 | tf_op jit(solution)/shard_map/ppermute | solution.py:509
  356.7 35.2 %collective-permute-start.54 = (f32[8,1,32,512]{3,2,1,0:T(8,128)}, f32[8,1,32,512]{3,2,1,0:T(8,128)}, u32[]{:S(2)}, u32[]{:S(2)}) collective-permute-start(f32[8,1,32,512]{3,2,1,0:T(8,128)} %get-tuple-element.89), channel_id=1, source_target_pairs={{0,1},{1,0},{2,3},{3,2},{4,5},{5,4},{6,7},{7,6},{8,9},{9,8},{10,11... | collective-permute-start | bytes 1572872 | tf_op jit(solution)/shard_map/ppermute | solution.py:509
  391.9 9.3 %collective-permute-done.55.refs_1_ = f32[8,1,32,512]{3,2,1,0:T(8,128)S(1)} collective-permute-done((f32[8,1,32,512]{3,2,1,0:T(8,128)}, f32[8,1,32,512]{3,2,1,0:T(8,128)S(1)}, u32[]{:S(2)}, u32[]{:S(2)}) %collective-permute-start.55) | collective-permute-done | bytes 524320 | tf_op jit(solution)/shard_map/ppermute | solution.py:509
  402.0 3.9 collective-permute-start.53
  405.9 32.9 %collective-permute-start.52 = (f32[8,1,32,512]{3,2,1,0:T(8,128)}, f32[8,1,32,512]{3,2,1,0:T(8,128)}, u32[]{:S(2)}, u32[]{:S(2)}) collective-permute-start(f32[8,1,32,512]{3,2,1,0:T(8,128)} %get-tuple-element.91), channel_id=1, source_target_pairs={{0,2},{1,3},{2,0},{3,1},{4,6},{5,7},{6,4},{7,5},{8,10},{9,11},{10,... | collective-permute-start | bytes 1572872 | tf_op jit(solution)/shard_map/ppermute | solution.py:509
  439.6 9.6 %collective-permute-done.38 = f32[40,256]{1,0:T(8,128)S(1)} collective-permute-done((f32[40,256]{1,0:T(8,128)S(1)}, f32[40,256]{1,0:T(8,128)S(1)}, u32[]{:S(2)}, u32[]{:S(2)}) %collective-permute-start.38) | collective-permute-done | bytes 40992 | tf_op jit(solution)/shard_map/ppermute | solution.py:509
  451.6 3.7 constant_dynamic-slice_fusion.18
  456.5 5.8 collective-permute-start.64
  462.2 8.4 %collective-permute-done.52.refs_1_ = f32[8,1,32,512]{3,2,1,0:T(8,128)} collective-permute-done((f32[8,1,32,512]{3,2,1,0:T(8,128)}, f32[8,1,32,512]{3,2,1,0:T(8,128)}, u32[]{:S(2)}, u32[]{:S(2)}) %collective-permute-start.52) | collective-permute-done | bytes 524320 | tf_op jit(solution)/shard_map/ppermute | solution.py:509
  471.5 21.0 %collective-permute-done.51.refs_0_ = f32[8,1,32,512]{3,2,1,0:T(8,128)} collective-permute-done((f32[8,1,32,512]{3,2,1,0:T(8,128)}, f32[8,1,32,512]{3,2,1,0:T(8,128)}, u32[]{:S(2)}, u32[]{:S(2)}) %collective-permute-start.51) | collective-permute-done | bytes 524320 | tf_op jit(solution)/shard_map/ppermute | solution.py:509
  501.8 3.4 collective-permute-start.48
  515.1 25.3 %sweeps.4.refs_7_ = f32[512,128]{1,0:T(8,128)S(1)} custom-call(s32[1]{0:T(128)} %constant.44.clone.1.place_ref, f32[64,512]{1,0:T(8,128)S(1)} %pad_maximum_fusion.refs_0_, f32[64,512]{1,0:T(8,128)S(1)} %copy-done.46, f32[64,512]{1,0:T(8,128)S(1)} %copy-done.44, f32[64,512]{1,0:T(8,128)S(1)} %copy-done.42, f32[64,512]{1,0:T(8,128)S(1)} %copy-done.40, ...), custom_call_target="tpu_custom_call" | custom-call | tf_op jit(solution)/shard_map/sweeps/pallas_call | solution.py:493
  540.5 22.5 %sweeps.5 = (f32[256,128]{1,0:T(8,128)S(1)}, f32[128,256]{1,0:T(8,128)S(1)}) custom-call(s32[1]{0:T(128)} %bitcast.4.place_ref.s_ref, f32[32,256]{1,0:T(8,128)S(1)} %copy-done.48, f32[32,256]{1,0:T(8,128)S(1)} %copy-done.62, f32[32,256]{1,0:T(8,128)S(1)} %copy-done.60, f32[32,256]{1,0:T(8,128)S(1)} %copy-done.58, f32[32,256]{1,0:T(8,128)S(1)} %copy-done.56, ...), custom_call_target="tpu_custom_call" | custom-call | tf_op jit(solution)/shard_map/sweeps/pallas_call | solution.py:493
  564.1 6.2 project.2
  570.3 14.5 %project.3 = (f32[8,4,16,128]{3,2,1,0:T(8,128)S(1)}, f32[8,4,16,128]{3,2,1,0:T(8,128)S(1)}, f32[8,4,16,128]{3,2,1,0:T(8,128)}, f32[8,4,16,128]{3,2,1,0:T(8,128)S...) custom-call(s32[1]{0:T(128)} %bitcast.5.s_ref, ...), custom_call_target="tpu_custom_call", output_to_operand_aliasing={{0}: (11, {}), {1}: (12, {}), {2}: (13, {}), {3}: (14, {}),... | custom-call | tf_op jit(solution)/shard_map/project/pallas_call | solution.py:265
  589.6 4.1 shard_map.94.refs_3_
  593.8 3.1 shard_map.95.refs_3_
  602.5 3.1 shard_map.98.refs_3_
  605.6 5.1 shard_map.99
  621.7 10.3 %collective-permute-done.76.refs_4_ = f32[8,4,16,128]{3,2,1,0:T(8,128)S(1)} collective-permute-done((f32[8,4,16,128]{3,2,1,0:T(8,128)S(1)}, f32[8,4,16,128]{3,2,1,0:T(8,128)S(1)}, u32[]{:S(2)}, u32[]{:S(2)}) %collective-permute-start.76) | collective-permute-done | bytes 262176 | tf_op jit(solution)/shard_map/ppermute | solution.py:509
  632.2 4.3 collective-permute-done.77.refs_5_
  636.5 2.8 contract_y.1
  649.0 3.1 collective-permute-done.72
  654.4 11.7 %collective-permute-done.81.refs_2_ = f32[8,64,128]{2,1,0:T(8,128)S(1)} collective-permute-done((f32[8,64,128]{2,1,0:T(8,128)S(1)}, f32[8,64,128]{2,1,0:T(8,128)S(1)}, u32[]{:S(2)}, u32[]{:S(2)}) %collective-permute-start.81) | collective-permute-done | bytes 262176 | tf_op jit(solution)/shard_map/ppermute | solution.py:509
  675.1 5.8 collective-permute-done.84.refs_2_
  (344 shorter events, 146.8 us)
Async XLA Ops:
  51.7 102.4 %collective-permute-start.30 = (f32[8,1,32,512]{3,2,1,0:T(8,128)}, f32[8,1,32,512]{3,2,1,0:T(8,128)S(1)}, u32[]{:S(2)}, u32[]{:S(2)}) collective-permute-start(f32[8,1,32,512]{3,2,1,0:T(8,128)} %get-tuple-element.96), channel_id=1, source_target_pairs={{0,28},{4,24},{8,20},{12,16},{16,12},{20,8},{24,4},{28,0},{1,29},{... | collective-permute-start | bytes 1572872 | tf_op jit(solution)/shard_map/ppermute | solution.py:509
  64.4 129.8 %collective-permute-start.23 = (f32[8,3,32,512]{3,2,1,0:T(8,128)S(1)}, f32[8,3,32,512]{3,2,1,0:T(8,128)S(1)}, u32[]{:S(2)}, u32[]{:S(2)}) collective-permute-start(f32[8,3,32,512]{3,2,1,0:T(8,128)S(1)} %get-tuple-element.103), channel_id=1, source_target_pairs={{0,28},{4,24},{8,20},{12,16},{16,12},{20,8},{24,4},{28,0},{1,29},{... | collective-permute-start | bytes 4718600 | tf_op jit(solution)/shard_map/ppermute | solution.py:509
  64.5 40.4 %collective-permute-start.16 = (f32[64,512]{1,0:T(8,128)S(1)}, f32[64,512]{1,0:T(8,128)S(1)}, u32[]{:S(2)}, u32[]{:S(2)}) collective-permute-start(f32[64,512]{1,0:T(8,128)S(1)} %pad_maximum_fusion.refs_0_), channel_id=1, source_target_pairs={{0,28},{4,24},{8,20},{12,16},{16,12},{20,8},{24,4},{28,0},{1,29},{... | collective-permute-start | bytes 393224 | tf_op jit(solution)/shard_map/ppermute | solution.py:509
  67.2 40.5 %collective-permute-start.15 = (f32[64,512]{1,0:T(8,128)S(1)}, f32[64,512]{1,0:T(8,128)S(1)}, u32[]{:S(2)}, u32[]{:S(2)}) collective-permute-start(f32[64,512]{1,0:T(8,128)S(1)} %pad_maximum_fusion.refs_0_), channel_id=1, source_target_pairs={{0,24},{4,28},{8,16},{12,20},{16,8},{20,12},{24,0},{28,4},{1,25},{... | collective-permute-start | bytes 393224 | tf_op jit(solution)/shard_map/ppermute | solution.py:509
  69.5 125.9 %collective-permute-start.22 = (f32[8,3,32,512]{3,2,1,0:T(8,128)S(1)}, f32[8,3,32,512]{3,2,1,0:T(8,128)S(1)}, u32[]{:S(2)}, u32[]{:S(2)}) collective-permute-start(f32[8,3,32,512]{3,2,1,0:T(8,128)S(1)} %get-tuple-element.104), channel_id=1, source_target_pairs={{0,24},{4,28},{8,16},{12,20},{16,8},{20,12},{24,0},{28,4},{1,25},{... | collective-permute-start | bytes 4718600 | tf_op jit(solution)/shard_map/ppermute | solution.py:509
  104.8 39.3 %collective-permute-start.14 = (f32[64,512]{1,0:T(8,128)S(1)}, f32[64,512]{1,0:T(8,128)S(1)}, u32[]{:S(2)}, u32[]{:S(2)}) collective-permute-start(f32[64,512]{1,0:T(8,128)S(1)} %pad_maximum_fusion.refs_0_), channel_id=1, source_target_pairs={{0,20},{4,16},{8,28},{12,24},{16,4},{20,0},{24,12},{28,8},{1,21},{... | collective-permute-start | bytes 393224 | tf_op jit(solution)/shard_map/ppermute | solution.py:509
  108.3 38.7 %collective-permute-start.13 = (f32[64,512]{1,0:T(8,128)S(1)}, f32[64,512]{1,0:T(8,128)S(1)}, u32[]{:S(2)}, u32[]{:S(2)}) collective-permute-start(f32[64,512]{1,0:T(8,128)S(1)} %pad_maximum_fusion.refs_0_), channel_id=1, source_target_pairs={{0,16},{4,20},{8,24},{12,28},{16,0},{20,4},{24,8},{28,12},{1,17},{... | collective-permute-start | bytes 393224 | tf_op jit(solution)/shard_map/ppermute | solution.py:509
  154.1 23.3 %collective-permute-start.28 = (f32[8,1,32,512]{3,2,1,0:T(8,128)S(1)}, f32[8,1,32,512]{3,2,1,0:T(8,128)S(1)}, u32[]{:S(2)}, u32[]{:S(2)}) collective-permute-start(f32[8,1,32,512]{3,2,1,0:T(8,128)S(1)} %copy-done.69), channel_id=1, source_target_pairs={{0,20},{4,16},{8,28},{12,24},{16,4},{20,0},{24,12},{28,8},{1,21},{... | collective-permute-start | bytes 1572872 | tf_op jit(solution)/shard_map/ppermute | solution.py:509
  154.1 34.4 %collective-permute-start.27 = (f32[8,1,32,512]{3,2,1,0:T(8,128)S(1)}, f32[8,1,32,512]{3,2,1,0:T(8,128)S(1)}, u32[]{:S(2)}, u32[]{:S(2)}) collective-permute-start(f32[8,1,32,512]{3,2,1,0:T(8,128)S(1)} %copy-done.68), channel_id=1, source_target_pairs={{0,16},{4,20},{8,24},{12,28},{16,0},{20,4},{24,8},{28,12},{1,17},{... | collective-permute-start | bytes 1572872 | tf_op jit(solution)/shard_map/ppermute | solution.py:509
  167.0 22.5 %collective-permute-start.26 = (f32[8,1,32,512]{3,2,1,0:T(8,128)S(1)}, f32[8,1,32,512]{3,2,1,0:T(8,128)S(1)}, u32[]{:S(2)}, u32[]{:S(2)}) collective-permute-start(f32[8,1,32,512]{3,2,1,0:T(8,128)S(1)} %copy-done.67), channel_id=1, source_target_pairs={{0,12},{4,8},{8,4},{12,0},{16,28},{20,24},{24,20},{28,16},{1,13},{... | collective-permute-start | bytes 1572872 | tf_op jit(solution)/shard_map/ppermute | solution.py:509
  190.2 36.5 %collective-permute-start.21 = (f32[8,3,32,512]{3,2,1,0:T(8,128)}, f32[8,3,32,512]{3,2,1,0:T(8,128)}, u32[]{:S(2)}, u32[]{:S(2)}) collective-permute-start(f32[8,3,32,512]{3,2,1,0:T(8,128)} %get-tuple-element.105), channel_id=1, source_target_pairs={{0,20},{4,16},{8,28},{12,24},{16,4},{20,0},{24,12},{28,8},{1,21},{... | collective-permute-start | bytes 4718600 | tf_op jit(solution)/shard_map/ppermute | solution.py:509
  192.9 68.1 %collective-permute-start.20 = (f32[8,3,32,512]{3,2,1,0:T(8,128)}, f32[8,3,32,512]{3,2,1,0:T(8,128)}, u32[]{:S(2)}, u32[]{:S(2)}) collective-permute-start(f32[8,3,32,512]{3,2,1,0:T(8,128)} %get-tuple-element.106), channel_id=1, source_target_pairs={{0,16},{4,20},{8,24},{12,28},{16,0},{20,4},{24,8},{28,12},{1,17},{... | collective-permute-start | bytes 4718600 | tf_op jit(solution)/shard_map/ppermute | solution.py:509
  194.2 69.9 %collective-permute-start.19 = (f32[8,3,32,512]{3,2,1,0:T(8,128)}, f32[8,3,32,512]{3,2,1,0:T(8,128)}, u32[]{:S(2)}, u32[]{:S(2)}) collective-permute-start(f32[8,3,32,512]{3,2,1,0:T(8,128)} %get-tuple-element.107), channel_id=1, source_target_pairs={{0,12},{4,8},{8,4},{12,0},{16,28},{20,24},{24,20},{28,16},{1,13},{... | collective-permute-start | bytes 4718600 | tf_op jit(solution)/shard_map/ppermute | solution.py:509
  194.3 70.1 %collective-permute-start.18 = (f32[8,3,32,512]{3,2,1,0:T(8,128)}, f32[8,3,32,512]{3,2,1,0:T(8,128)S(1)}, u32[]{:S(2)}, u32[]{:S(2)}) collective-permute-start(f32[8,3,32,512]{3,2,1,0:T(8,128)} %get-tuple-element.108), channel_id=1, source_target_pairs={{0,8},{4,12},{8,0},{12,4},{16,24},{20,28},{24,16},{28,20},{1,9},{5... | collective-permute-start | bytes 4718600 | tf_op jit(solution)/shard_map/ppermute | solution.py:509
  196.7 83.6 %collective-permute-start.17 = (f32[8,3,32,512]{3,2,1,0:T(8,128)}, f32[8,3,32,512]{3,2,1,0:T(8,128)S(1)}, u32[]{:S(2)}, u32[]{:S(2)}) collective-permute-start(f32[8,3,32,512]{3,2,1,0:T(8,128)} %get-tuple-element.109), channel_id=1, source_target_pairs={{0,4},{4,0},{8,12},{12,8},{16,20},{20,16},{24,28},{28,24},{1,5},{5... | collective-permute-start | bytes 4718600 | tf_op jit(solution)/shard_map/ppermute | solution.py:509
  226.7 73.5 %collective-permute-start.62 = (f32[8,1,32,512]{3,2,1,0:T(8,128)}, f32[8,1,32,512]{3,2,1,0:T(8,128)}, u32[]{:S(2)}, u32[]{:S(2)}) collective-permute-start(f32[8,1,32,512]{3,2,1,0:T(8,128)} %get-tuple-element.81), channel_id=1, source_target_pairs={{0,3},{1,2},{2,1},{3,0},{4,7},{5,6},{6,5},{7,4},{8,11},{9,10},{10,... | collective-permute-start | bytes 1572872 | tf_op jit(solution)/shard_map/ppermute | solution.py:509
  261.0 40.1 %collective-permute-start.61 = (f32[8,1,32,512]{3,2,1,0:T(8,128)}, f32[8,1,32,512]{3,2,1,0:T(8,128)}, u32[]{:S(2)}, u32[]{:S(2)}) collective-permute-start(f32[8,1,32,512]{3,2,1,0:T(8,128)} %get-tuple-element.82), channel_id=1, source_target_pairs={{0,2},{1,3},{2,0},{3,1},{4,6},{5,7},{6,4},{7,5},{8,10},{9,11},{10,... | collective-permute-start | bytes 1572872 | tf_op jit(solution)/shard_map/ppermute | solution.py:509
  264.1 37.5 %collective-permute-start.60 = (f32[8,1,32,512]{3,2,1,0:T(8,128)}, f32[8,1,32,512]{3,2,1,0:T(8,128)}, u32[]{:S(2)}, u32[]{:S(2)}) collective-permute-start(f32[8,1,32,512]{3,2,1,0:T(8,128)} %get-tuple-element.83), channel_id=1, source_target_pairs={{0,1},{1,0},{2,3},{3,2},{4,5},{5,4},{6,7},{7,6},{8,9},{9,8},{10,11... | collective-permute-start | bytes 1572872 | tf_op jit(solution)/shard_map/ppermute | solution.py:509
  264.3 38.3 %collective-permute-start.59 = (f32[8,1,32,512]{3,2,1,0:T(8,128)}, f32[8,1,32,512]{3,2,1,0:T(8,128)}, u32[]{:S(2)}, u32[]{:S(2)}) collective-permute-start(f32[8,1,32,512]{3,2,1,0:T(8,128)} %get-tuple-element.84), channel_id=1, source_target_pairs={{0,3},{1,2},{2,1},{3,0},{4,7},{5,6},{6,5},{7,4},{8,11},{9,10},{10,... | collective-permute-start | bytes 1572872 | tf_op jit(solution)/shard_map/ppermute | solution.py:509
  300.2 22.3 %collective-permute-start.32 = (f32[40,256]{1,0:T(8,128)S(1)}, f32[40,256]{1,0:T(8,128)S(1)}, u32[]{:S(2)}, u32[]{:S(2)}) collective-permute-start(f32[40,256]{1,0:T(8,128)S(1)} %get-tuple-element.44), channel_id=1, source_target_pairs={{0,8},{4,12},{8,0},{12,4},{16,24},{20,28},{24,16},{28,20},{1,9},{5... | collective-permute-start | bytes 122888 | tf_op jit(solution)/shard_map/ppermute | solution.py:509
  301.1 24.8 %collective-permute-start.33 = (f32[40,256]{1,0:T(8,128)S(1)}, f32[40,256]{1,0:T(8,128)S(1)}, u32[]{:S(2)}, u32[]{:S(2)}) collective-permute-start(f32[40,256]{1,0:T(8,128)S(1)} %get-tuple-element.45), channel_id=1, source_target_pairs={{0,12},{4,8},{8,4},{12,0},{16,28},{20,24},{24,20},{28,16},{1,13},{... | collective-permute-start | bytes 122888 | tf_op jit(solution)/shard_map/ppermute | solution.py:509
  301.6 38.9 %collective-permute-start.58 = (f32[8,1,32,512]{3,2,1,0:T(8,128)S(1)}, f32[8,1,32,512]{3,2,1,0:T(8,128)S(1)}, u32[]{:S(2)}, u32[]{:S(2)}) collective-permute-start(f32[8,1,32,512]{3,2,1,0:T(8,128)S(1)} %copy-done.72), channel_id=1, source_target_pairs={{0,2},{1,3},{2,0},{3,1},{4,6},{5,7},{6,4},{7,5},{8,10},{9,11},{10,... | collective-permute-start | bytes 1572872 | tf_op jit(solution)/shard_map/ppermute | solution.py:509
  302.6 23.2 %collective-permute-start.34 = (f32[40,256]{1,0:T(8,128)S(1)}, f32[40,256]{1,0:T(8,128)S(1)}, u32[]{:S(2)}, u32[]{:S(2)}) collective-permute-start(f32[40,256]{1,0:T(8,128)S(1)} %get-tuple-element.46), channel_id=1, source_target_pairs={{0,16},{4,20},{8,24},{12,28},{16,0},{20,4},{24,8},{28,12},{1,17},{... | collective-permute-start | bytes 122888 | tf_op jit(solution)/shard_map/ppermute | solution.py:509
  303.9 51.1 %collective-permute-start.57 = (f32[8,1,32,512]{3,2,1,0:T(8,128)S(1)}, f32[8,1,32,512]{3,2,1,0:T(8,128)S(1)}, u32[]{:S(2)}, u32[]{:S(2)}) collective-permute-start(f32[8,1,32,512]{3,2,1,0:T(8,128)S(1)} %copy-done.71), channel_id=1, source_target_pairs={{0,1},{1,0},{2,3},{3,2},{4,5},{5,4},{6,7},{7,6},{8,9},{9,8},{10,11... | collective-permute-start | bytes 1572872 | tf_op jit(solution)/shard_map/ppermute | solution.py:509
  322.4 33.4 %collective-permute-start.56 = (f32[8,1,32,512]{3,2,1,0:T(8,128)}, f32[8,1,32,512]{3,2,1,0:T(8,128)S(1)}, u32[]{:S(2)}, u32[]{:S(2)}) collective-permute-start(f32[8,1,32,512]{3,2,1,0:T(8,128)} %get-tuple-element.87), channel_id=1, source_target_pairs={{0,3},{1,2},{2,1},{3,0},{4,7},{5,6},{6,5},{7,4},{8,11},{9,10},{10,... | collective-permute-start | bytes 1572872 | tf_op jit(solution)/shard_map/ppermute | solution.py:509
  325.8 75.3 %collective-permute-start.55 = (f32[8,1,32,512]{3,2,1,0:T(8,128)}, f32[8,1,32,512]{3,2,1,0:T(8,128)S(1)}, u32[]{:S(2)}, u32[]{:S(2)}) collective-permute-start(f32[8,1,32,512]{3,2,1,0:T(8,128)} %get-tuple-element.88), channel_id=1, source_target_pairs={{0,2},{1,3},{2,0},{3,1},{4,6},{5,7},{6,4},{7,5},{8,10},{9,11},{10,... | collective-permute-start | bytes 1572872 | tf_op jit(solution)/shard_map/ppermute | solution.py:509
  339.0 154.3 %collective-permute-start.65 = (f32[8,2,32,512]{3,2,1,0:T(8,128)}, f32[8,2,32,512]{3,2,1,0:T(8,128)}, u32[]{:S(2)}, u32[]{:S(2)}) collective-permute-start(f32[8,2,32,512]{3,2,1,0:T(8,128)} %get-tuple-element.78), channel_id=1, source_target_pairs={{0,3},{1,2},{2,1},{3,0},{4,7},{5,6},{6,5},{7,4},{8,11},{9,10},{10,... | collective-permute-start | bytes 3145736 | tf_op jit(solution)/shard_map/ppermute | solution.py:509
  341.3 64.5 %collective-permute-start.40 = (f32[40,256]{1,0:T(8,128)S(1)}, f32[40,256]{1,0:T(8,128)S(1)}, u32[]{:S(2)}, u32[]{:S(2)}) collective-permute-start(f32[40,256]{1,0:T(8,128)S(1)} %add_add_fusion.2), channel_id=1, source_target_pairs={{0,3},{1,2},{2,1},{3,0},{4,7},{5,6},{6,5},{7,4},{8,11},{9,10},{10,... | collective-permute-start | bytes 122888 | tf_op jit(solution)/shard_map/ppermute | solution.py:509
  355.9 82.9 %collective-permute-start.39 = (f32[40,256]{1,0:T(8,128)S(1)}, f32[40,256]{1,0:T(8,128)S(1)}, u32[]{:S(2)}, u32[]{:S(2)}) collective-permute-start(f32[40,256]{1,0:T(8,128)S(1)} %add_add_fusion.2), channel_id=1, source_target_pairs={{0,2},{1,3},{2,0},{3,1},{4,6},{5,7},{6,4},{7,5},{8,10},{9,11},{10,... | collective-permute-start | bytes 122888 | tf_op jit(solution)/shard_map/ppermute | solution.py:509
  356.7 99.6 %collective-permute-start.54 = (f32[8,1,32,512]{3,2,1,0:T(8,128)}, f32[8,1,32,512]{3,2,1,0:T(8,128)}, u32[]{:S(2)}, u32[]{:S(2)}) collective-permute-start(f32[8,1,32,512]{3,2,1,0:T(8,128)} %get-tuple-element.89), channel_id=1, source_target_pairs={{0,1},{1,0},{2,3},{3,2},{4,5},{5,4},{6,7},{7,6},{8,9},{9,8},{10,11... | collective-permute-start | bytes 1572872 | tf_op jit(solution)/shard_map/ppermute | solution.py:509
  402.0 54.5 %collective-permute-start.53 = (f32[8,1,32,512]{3,2,1,0:T(8,128)}, f32[8,1,32,512]{3,2,1,0:T(8,128)}, u32[]{:S(2)}, u32[]{:S(2)}) collective-permute-start(f32[8,1,32,512]{3,2,1,0:T(8,128)} %get-tuple-element.90), channel_id=1, source_target_pairs={{0,3},{1,2},{2,1},{3,0},{4,7},{5,6},{6,5},{7,4},{8,11},{9,10},{10,... | collective-permute-start | bytes 1572872 | tf_op jit(solution)/shard_map/ppermute | solution.py:509
  405.9 64.7 %collective-permute-start.52 = (f32[8,1,32,512]{3,2,1,0:T(8,128)}, f32[8,1,32,512]{3,2,1,0:T(8,128)}, u32[]{:S(2)}, u32[]{:S(2)}) collective-permute-start(f32[8,1,32,512]{3,2,1,0:T(8,128)} %get-tuple-element.91), channel_id=1, source_target_pairs={{0,2},{1,3},{2,0},{3,1},{4,6},{5,7},{6,4},{7,5},{8,10},{9,11},{10,... | collective-permute-start | bytes 1572872 | tf_op jit(solution)/shard_map/ppermute | solution.py:509
  449.1 43.4 %collective-permute-start.51 = (f32[8,1,32,512]{3,2,1,0:T(8,128)}, f32[8,1,32,512]{3,2,1,0:T(8,128)}, u32[]{:S(2)}, u32[]{:S(2)}) collective-permute-start(f32[8,1,32,512]{3,2,1,0:T(8,128)} %get-tuple-element.92), channel_id=1, source_target_pairs={{0,1},{1,0},{2,3},{3,2},{4,5},{5,4},{6,7},{7,6},{8,9},{9,8},{10,11... | collective-permute-start | bytes 1572872 | tf_op jit(solution)/shard_map/ppermute | solution.py:509
  456.3 132.0 %collective-permute-start.63 = (f32[8,2,32,512]{3,2,1,0:T(8,128)}, f32[8,2,32,512]{3,2,1,0:T(8,128)}, u32[]{:S(2)}, u32[]{:S(2)}) collective-permute-start(f32[8,2,32,512]{3,2,1,0:T(8,128)} %get-tuple-element.80), channel_id=1, source_target_pairs={{0,1},{1,0},{2,3},{3,2},{4,5},{5,4},{6,7},{7,6},{8,9},{9,8},{10,11... | collective-permute-start | bytes 3145736 | tf_op jit(solution)/shard_map/ppermute | solution.py:509
  456.5 131.8 %collective-permute-start.64 = (f32[8,2,32,512]{3,2,1,0:T(8,128)}, f32[8,2,32,512]{3,2,1,0:T(8,128)}, u32[]{:S(2)}, u32[]{:S(2)}) collective-permute-start(f32[8,2,32,512]{3,2,1,0:T(8,128)} %get-tuple-element.79), channel_id=1, source_target_pairs={{0,2},{1,3},{2,0},{3,1},{4,6},{5,7},{6,4},{7,5},{8,10},{9,11},{10,... | collective-permute-start | bytes 3145736 | tf_op jit(solution)/shard_map/ppermute | solution.py:509
  470.6 22.7 %collective-permute-start.47 = (f32[32,256]{1,0:T(8,128)S(1)}, f32[32,256]{1,0:T(8,128)S(1)}, u32[]{:S(2)}, u32[]{:S(2)}) collective-permute-start(f32[32,256]{1,0:T(8,128)S(1)} %slice.29.refs_0_), channel_id=1, source_target_pairs={{0,28},{4,24},{8,20},{12,16},{16,12},{20,8},{24,4},{28,0},{1,29},{... | collective-permute-start | bytes 98312 | tf_op jit(solution)/shard_map/ppermute | solution.py:509
  500.8 104.8 %collective-permute-start.50 = (f32[8,2,32,512]{3,2,1,0:T(8,128)}, f32[8,2,32,512]{3,2,1,0:T(8,128)}, u32[]{:S(2)}, u32[]{:S(2)}) collective-permute-start(f32[8,2,32,512]{3,2,1,0:T(8,128)} %get-tuple-element.93), channel_id=1, source_target_pairs={{0,3},{1,2},{2,1},{3,0},{4,7},{5,6},{6,5},{7,4},{8,11},{9,10},{10,... | collective-permute-start | bytes 3145736 | tf_op jit(solution)/shard_map/ppermute | solution.py:509
  501.5 104.1 %collective-permute-start.49 = (f32[8,2,32,512]{3,2,1,0:T(8,128)}, f32[8,2,32,512]{3,2,1,0:T(8,128)}, u32[]{:S(2)}, u32[]{:S(2)}) collective-permute-start(f32[8,2,32,512]{3,2,1,0:T(8,128)} %get-tuple-element.94), channel_id=1, source_target_pairs={{0,2},{1,3},{2,0},{3,1},{4,6},{5,7},{6,4},{7,5},{8,10},{9,11},{10,... | collective-permute-start | bytes 3145736 | tf_op jit(solution)/shard_map/ppermute | solution.py:509
  501.8 103.8 %collective-permute-start.48 = (f32[8,2,32,512]{3,2,1,0:T(8,128)}, f32[8,2,32,512]{3,2,1,0:T(8,128)}, u32[]{:S(2)}, u32[]{:S(2)}) collective-permute-start(f32[8,2,32,512]{3,2,1,0:T(8,128)} %get-tuple-element.95), channel_id=1, source_target_pairs={{0,1},{1,0},{2,3},{3,2},{4,5},{5,4},{6,7},{7,6},{8,9},{9,8},{10,11... | collective-permute-start | bytes 3145736 | tf_op jit(solution)/shard_map/ppermute | solution.py:509
  588.3 25.1 %collective-permute-start.73 = (f32[8,4,16,128]{3,2,1,0:T(8,128)S(1)}, f32[8,4,16,128]{3,2,1,0:T(8,128)S(1)}, u32[]{:S(2)}, u32[]{:S(2)}) collective-permute-start(f32[8,4,16,128]{3,2,1,0:T(8,128)S(1)} %get-tuple-element.62), channel_id=1, source_target_pairs={{0,4},{4,0},{8,12},{12,8},{16,20},{20,16},{24,28},{28,24},{1,5},{5... | collective-permute-start | bytes 786440 | tf_op jit(solution)/shard_map/ppermute | solution.py:509
  588.3 26.0 %collective-permute-start.74 = (f32[8,4,16,128]{3,2,1,0:T(8,128)}, f32[8,4,16,128]{3,2,1,0:T(8,128)S(1)}, u32[]{:S(2)}, u32[]{:S(2)}) collective-permute-start(f32[8,4,16,128]{3,2,1,0:T(8,128)} %get-tuple-element.63), channel_id=1, source_target_pairs={{0,8},{4,12},{8,0},{12,4},{16,24},{20,28},{24,16},{28,20},{1,9},{5... | collective-permute-start | bytes 786440 | tf_op jit(solution)/shard_map/ppermute | solution.py:509
  611.7 20.4 %collective-permute-start.76 = (f32[8,4,16,128]{3,2,1,0:T(8,128)S(1)}, f32[8,4,16,128]{3,2,1,0:T(8,128)S(1)}, u32[]{:S(2)}, u32[]{:S(2)}) collective-permute-start(f32[8,4,16,128]{3,2,1,0:T(8,128)S(1)} %copy-done.27), channel_id=1, source_target_pairs={{0,16},{4,20},{8,24},{12,28},{16,0},{20,4},{24,8},{28,12},{1,17},{... | collective-permute-start | bytes 786440 | tf_op jit(solution)/shard_map/ppermute | solution.py:509
  612.2 24.2 %collective-permute-start.77 = (f32[8,4,16,128]{3,2,1,0:T(8,128)S(1)}, f32[8,4,16,128]{3,2,1,0:T(8,128)S(1)}, u32[]{:S(2)}, u32[]{:S(2)}) collective-permute-start(f32[8,4,16,128]{3,2,1,0:T(8,128)S(1)} %copy-done.29), channel_id=1, source_target_pairs={{0,20},{4,16},{8,28},{12,24},{16,4},{20,0},{24,12},{28,8},{1,21},{... | collective-permute-start | bytes 786440 | tf_op jit(solution)/shard_map/ppermute | solution.py:509
  613.4 23.1 %collective-permute-start.78 = (f32[8,4,16,128]{3,2,1,0:T(8,128)S(1)}, f32[8,4,16,128]{3,2,1,0:T(8,128)S(1)}, u32[]{:S(2)}, u32[]{:S(2)}) collective-permute-start(f32[8,4,16,128]{3,2,1,0:T(8,128)S(1)} %copy-done.31), channel_id=1, source_target_pairs={{0,24},{4,28},{8,16},{12,20},{16,8},{20,12},{24,0},{28,4},{1,25},{... | collective-permute-start | bytes 786440 | tf_op jit(solution)/shard_map/ppermute | solution.py:509
  614.3 22.1 %collective-permute-start.79 = (f32[8,4,16,128]{3,2,1,0:T(8,128)S(1)}, f32[8,4,16,128]{3,2,1,0:T(8,128)S(1)}, u32[]{:S(2)}, u32[]{:S(2)}) collective-permute-start(f32[8,4,16,128]{3,2,1,0:T(8,128)S(1)} %copy-done.33), channel_id=1, source_target_pairs={{0,28},{4,24},{8,20},{12,16},{16,12},{20,8},{24,4},{28,0},{1,29},{... | collective-permute-start | bytes 786440 | tf_op jit(solution)/shard_map/ppermute | solution.py:509
  619.1 23.8 %collective-permute-start.68 = (f32[32,32]{1,0:T(8,128)S(1)}, f32[32,32]{1,0:T(8,128)S(1)}, u32[]{:S(2)}, u32[]{:S(2)}) collective-permute-start(f32[32,32]{1,0:T(8,128)S(1)} %shard_map.99), channel_id=1, source_target_pairs={{0,3},{1,2},{2,1},{3,0},{4,7},{5,6},{6,5},{7,4},{8,11},{9,10},{10,... | collective-permute-start | bytes 12296 | tf_op jit(solution)/shard_map/ppermute | solution.py:509
  641.6 24.6 %collective-permute-start.81 = (f32[8,64,128]{2,1,0:T(8,128)S(1)}, f32[8,64,128]{2,1,0:T(8,128)S(1)}, u32[]{:S(2)}, u32[]{:S(2)}) collective-permute-start(f32[8,64,128]{2,1,0:T(8,128)S(1)} %get-tuple-element.111), channel_id=1, source_target_pairs={{0,2},{1,3},{2,0},{3,1},{4,6},{5,7},{6,4},{7,5},{8,10},{9,11},{10,... | collective-permute-start | bytes 786440 | tf_op jit(solution)/shard_map/ppermute | solution.py:509
  642.9 23.2 %collective-permute-start.80 = (f32[8,64,128]{2,1,0:T(8,128)S(1)}, f32[8,64,128]{2,1,0:T(8,128)S(1)}, u32[]{:S(2)}, u32[]{:S(2)}) collective-permute-start(f32[8,64,128]{2,1,0:T(8,128)S(1)} %get-tuple-element.112), channel_id=1, source_target_pairs={{0,1},{1,0},{2,3},{3,2},{4,5},{5,4},{6,7},{7,6},{8,9},{9,8},{10,11... | collective-permute-start | bytes 786440 | tf_op jit(solution)/shard_map/ppermute | solution.py:509
  (117 other events, 1928.2 us)
